TPU v7x, 32 devices: a whole 2x2x4 slice. The times are simulated.
32 devices in a mesh: rep: 4 (over x, core), fsdp: 8 (over z, y).
Axes of the slice: x: 2, y: 2, z: 4, core: 2. Of those that a mesh axis runs over, the one named last changes fastest.
Arguments:
- tokens: bfloat16 [8192, 2048], P(('rep', 'fsdp')), may hold values from -6 to 6
- query_weight: bfloat16 [2048, 2048], P('fsdp'), may hold values from -0.125 to 0.125
- key_weight: bfloat16 [2048, 2048], P('fsdp'), may hold values from -0.125 to 0.125
- value_weight: bfloat16 [2048, 2048], P('fsdp'), may hold values from -0.125 to 0.125
- query_norm: bfloat16 [2048], P('fsdp'), may hold values from 0.25 to 1.75
- key_norm: bfloat16 [2048], P('fsdp'), may hold values from 0.25 to 1.75
- output_weight: bfloat16 [2048, 2048], P('fsdp'), may hold values from -0.125 to 0.125
- mixer_norm: bfloat16 [2048], P('fsdp'), may hold values from 0.25 to 1.75
- gate_weight: bfloat16 [2048, 8192], P(None, 'fsdp'), may hold values from -0.125 to 0.125
- up_weight: bfloat16 [2048, 8192], P(None, 'fsdp'), may hold values from -0.125 to 0.125
- down_weight: bfloat16 [2048, 8192], P(None, 'fsdp'), may hold values from -0.0625 to 0.0625
- feeder_norm: bfloat16 [2048], P('fsdp'), may hold values from 0.25 to 1.75
- piece_starts: int32 [4, 2], replicated, may hold values from 0 to 1792, as said below
- cotangent: bfloat16 [8192, 2048], P(('rep', 'fsdp')), may hold values from -6 to 6
Outputs:
- result: bfloat16 [8192, 2048], P(('rep', 'fsdp'))
- gradient_tokens: bfloat16 [8192, 2048], P(('rep', 'fsdp'))
- gradient_query: float32 [2048, 2048], P('fsdp')
- gradient_key: float32 [2048, 2048], P('fsdp')
- gradient_value: float32 [2048, 2048], P('fsdp')
- gradient_querynorm: float32 [2048], P('fsdp')
- gradient_keynorm: float32 [2048], P('fsdp')
- gradient_output: float32 [2048, 2048], P('fsdp')
- gradient_mixernorm: float32 [2048], P('fsdp')
- gradient_gate: float32 [2048, 8192], P(None, 'fsdp')
- gradient_up: float32 [2048, 8192], P(None, 'fsdp')
- gradient_down: float32 [2048, 8192], P(None, 'fsdp')
- gradient_feedernorm: float32 [2048], P('fsdp')
Inputs may be any that keep to these rules, and one draw needn't show every extreme that they name: `piece_starts`: each of the 4 sequences holds 2 pieces of 256 tokens; piece j of a sequence starts between j * 1024 and (j + 1) * 1024 - 256, so the pieces of a sequence never intersect. Positions count from the sequence's first token.
All inputs are finite; a program needn't handle non-finite values.
Results may differ from a plain program's by a relative error of at most 0.022.
Values may be sent and summed in bfloat16 or wider, within the bound.
No kernel may reach another device: no remote copies, remote signals or barrier semaphores. Data moves between devices by JAX's collectives and lax.ppermute only.
A program may use at most 832 MiB of HBM per device.

v0:
```python
import jax
import jax.numpy as jnp
from jax import lax
from jax.sharding import PartitionSpec as P

HEADS = 16
HEAD_DIM = 128
FF = 8192
SEQ = 2048
PIECE = 256
HOPS = 7


norm_epsilon = 1e-06
rope_base = 500000.0
masked_score = -1e30


def passed_along(block, axis, distance):
    devices = range(lax.axis_size(axis))
    route = [(i - distance, i) for i in devices if i - distance in devices]
    return lax.ppermute(block, axis, route)


def matmul(first_op, second_op):
    return jnp.dot(first_op, second_op, preferred_element_type=jnp.float32)


def against(first_op, second_op):
    return lax.dot_general(
        first_op, second_op, (((1,), (1,)), ((), ())), preferred_element_type=jnp.float32
    )


def across(first_op, second_op):
    return lax.dot_general(
        first_op, second_op, (((0,), (0,)), ((), ())), preferred_element_type=jnp.float32
    )


def inverse_rms(values):
    return lax.rsqrt(jnp.mean(values * values, axis=-1, keepdims=True) + norm_epsilon)


def norm_backward(values, factor, gain_row, upstream):
    weighted = upstream * gain_row
    inner_mean = jnp.mean(weighted * values, axis=-1, keepdims=True)
    return factor * weighted - values * (factor * factor * factor) * inner_mean


def rope_tables(positions, head_dim):
    half_dim = head_dim // 2
    frequency = rope_base ** (-(jnp.arange(half_dim, dtype=jnp.float32) * (2.0 / head_dim)))
    angles = positions.astype(jnp.float32)[:, None] * frequency[None, :]
    return (jnp.cos(angles), jnp.sin(angles))


def rotate(values, cosine_table, sine_table, head_count):
    row_count = values.shape[0]
    shaped = values.reshape(row_count, head_count, 2, -1)
    first_half = shaped[:, :, 0]
    second_half = shaped[:, :, 1]
    cosine_part = cosine_table[:, None, :]
    sine_part = sine_table[:, None, :]
    turned = jnp.stack(
        [
            first_half * cosine_part - second_half * sine_part,
            second_half * cosine_part + first_half * sine_part,
        ],
        axis=2,
    )
    return turned.reshape(row_count, -1)


def piece_labels(places, piece_starts, piece_len, sequence_len):
    sequence_count, pieces_each = piece_starts.shape
    begins = (
        jnp.arange(sequence_count, dtype=jnp.int32)[:, None] * sequence_len + piece_starts
    ).reshape(-1)
    inside = (places[:, None] >= begins[None, :]) & (places[:, None] < begins[None, :] + piece_len)
    labels = jnp.arange(1, sequence_count * pieces_each + 1, dtype=jnp.int32)
    return jnp.sum(jnp.where(inside, labels[None, :], 0), axis=1) - 1


def allowed_pairs(query_places, key_places, query_labels, key_labels, sequence_len):
    same = query_places[:, None] // sequence_len == key_places[None, :] // sequence_len
    causal = key_places[None, :] <= query_places[:, None]
    joint = (query_labels[:, None] == key_labels[None, :]) & (query_labels[:, None] >= 0)
    return same & (causal | joint)


def body(
    tokens,
    query_weight,
    key_weight,
    value_weight,
    query_norm,
    key_norm,
    output_weight,
    mixer_norm,
    gate_weight,
    up_weight,
    down_weight,
    feeder_norm,
    piece_starts,
    cotangent,
):
    own_rows, model_width = tokens.shape
    head_count = HEADS
    head_dim = HEAD_DIM
    width_ratio = FF // model_width
    group_size = lax.axis_size("fsdp")
    first_place = (lax.axis_index("rep") * group_size + lax.axis_index("fsdp")) * own_rows
    places = first_place + jnp.arange(own_rows, dtype=jnp.int32)
    cosine_table, sine_table = rope_tables(places % SEQ, head_dim)
    float_tokens = tokens.astype(jnp.float32)
    pieces = (
        lax.all_gather(query_weight, "fsdp", axis=0, tiled=True),
        lax.all_gather(key_weight, "fsdp", axis=0, tiled=True),
        lax.all_gather(value_weight, "fsdp", axis=0, tiled=True),
        lax.all_gather(query_norm, "fsdp", axis=0, tiled=True),
        lax.all_gather(key_norm, "fsdp", axis=0, tiled=True),
    )
    columns = tokens
    query_pre = matmul(columns, pieces[0])
    key_pre = matmul(columns, pieces[1])
    value_pre = matmul(columns, pieces[2])
    query_gain = pieces[3].astype(jnp.float32)
    key_gain = pieces[4].astype(jnp.float32)
    value_low = value_pre.astype(jnp.bfloat16)
    query_factor = inverse_rms(query_pre)
    key_factor = inverse_rms(key_pre)
    query_low = rotate(
        query_pre * query_factor * query_gain, cosine_table, sine_table, head_count
    ).astype(jnp.bfloat16)
    key_low = rotate(key_pre * key_factor * key_gain, cosine_table, sine_table, head_count).astype(
        jnp.bfloat16
    )
    hop_count = HOPS
    offsets = list(range(hop_count, 0, -1)) + [-1] * min(hop_count, 1)
    sent_pair = jnp.stack([key_low, value_low])
    received = []
    for offset in offsets:
        received.append(passed_along(sent_pair, "fsdp", offset))
    window_parts = received[:hop_count] + [sent_pair] + received[hop_count:]
    slot_offsets = offsets[:hop_count] + [0] + offsets[hop_count:]
    window_pair = jnp.concatenate(window_parts, axis=1)
    key_places = jnp.concatenate([places - offset * own_rows for offset in slot_offsets])
    window_rows = key_places.shape[0]
    query_labels = piece_labels(places, piece_starts, PIECE, SEQ)
    key_labels = piece_labels(key_places, piece_starts, PIECE, SEQ)
    allowed = allowed_pairs(places, key_places, query_labels, key_labels, SEQ)
    score_factor = head_dim ** (-0.5)

    def by_heads(matrix, row_count):
        return matrix.reshape(row_count, head_count, head_dim).transpose(1, 0, 2)

    def by_rows(matrix, row_count):
        return matrix.transpose(1, 0, 2).reshape(row_count, model_width)

    head_queries = by_heads(query_low, own_rows)
    head_keys = by_heads(window_pair[0], window_rows)
    head_values = by_heads(window_pair[1], window_rows)

    def attend(operands):
        head_query, head_key, head_value = operands
        scores = jnp.where(allowed, against(head_query, head_key) * score_factor, masked_score)
        row_max = jnp.max(scores, axis=1, keepdims=True)
        exponent = jnp.exp(scores - row_max)
        row_total = jnp.sum(exponent, axis=1, keepdims=True)
        shares = (exponent / row_total).astype(jnp.bfloat16)
        return (matmul(shares, head_value), (row_max + jnp.log(row_total))[:, 0])

    head_mixed, log_totals = lax.map(attend, (head_queries, head_keys, head_values))
    mixed_low = by_rows(head_mixed, own_rows).astype(jnp.bfloat16)
    pieces = (
        lax.all_gather(output_weight, "fsdp", axis=0, tiled=True),
        lax.all_gather(mixer_norm, "fsdp", axis=0, tiled=True),
        lax.all_gather(feeder_norm, "fsdp", axis=0, tiled=True),
    )
    columns = mixed_low
    branch_pre = matmul(columns, pieces[0])
    mixer_gain = pieces[1].astype(jnp.float32)
    feeder_gain = pieces[2].astype(jnp.float32)
    branch_factor = inverse_rms(branch_pre)
    hidden = float_tokens + branch_pre * branch_factor * mixer_gain
    hidden_low = hidden.astype(jnp.bfloat16)
    pieces = (
        lax.all_gather(gate_weight, "fsdp", axis=1, tiled=True),
        lax.all_gather(up_weight, "fsdp", axis=1, tiled=True),
        lax.all_gather(down_weight, "fsdp", axis=1, tiled=True),
    )
    gate_part = matmul(hidden_low, pieces[0])
    up_part = matmul(hidden_low, pieces[1])
    inner_part = (gate_part * jax.nn.sigmoid(gate_part) * up_part).astype(jnp.bfloat16)
    down_pre = against(inner_part, pieces[2])
    down_factor = inverse_rms(down_pre)
    result = (hidden + down_pre * down_factor * feeder_gain).astype(jnp.bfloat16)
    tangent = cotangent.astype(jnp.float32)
    feeder_part = jnp.sum(tangent * down_pre * down_factor, axis=0)
    down_grad = norm_backward(down_pre, down_factor, feeder_gain, tangent).astype(jnp.bfloat16)
    pieces = (
        lax.all_gather(gate_weight, "fsdp", axis=1, tiled=True),
        lax.all_gather(up_weight, "fsdp", axis=1, tiled=True),
        lax.all_gather(down_weight, "fsdp", axis=1, tiled=True),
    )
    gate_part = matmul(hidden_low, pieces[0])
    up_part = matmul(hidden_low, pieces[1])
    sigmoid_part = jax.nn.sigmoid(gate_part)
    inner_part = (gate_part * sigmoid_part * up_part).astype(jnp.bfloat16)
    inner_grad = matmul(down_grad, pieces[2])
    gate_grad = (
        inner_grad * up_part * sigmoid_part * (1.0 + gate_part * (1.0 - sigmoid_part))
    ).astype(jnp.bfloat16)
    up_grad = (inner_grad * gate_part * sigmoid_part).astype(jnp.bfloat16)
    feed_back = against(gate_grad, pieces[0]) + against(up_grad, pieces[1])
    hidden_grad = tangent + feed_back
    mixer_part = jnp.sum(hidden_grad * branch_pre * branch_factor, axis=0)
    branch_grad = norm_backward(branch_pre, branch_factor, mixer_gain, hidden_grad).astype(
        jnp.bfloat16
    )
    mixed_grad = against(
        branch_grad, lax.all_gather(output_weight, "fsdp", axis=0, tiled=True)
    ).astype(jnp.bfloat16)
    head_mixed_grad = by_heads(mixed_grad, own_rows)

    def attend_back(operands):
        head_query, head_key, head_value, head_grad, log_total = operands
        scores = jnp.where(allowed, against(head_query, head_key) * score_factor, masked_score)
        shares = jnp.exp(scores - log_total[:, None])
        share_grad = against(head_grad, head_value)
        inner_sum = jnp.sum(shares * share_grad, axis=1, keepdims=True)
        score_grad = (shares * (share_grad - inner_sum)).astype(jnp.bfloat16)
        return (
            matmul(score_grad, head_key) * score_factor,
            across(score_grad, head_query) * score_factor,
            across(shares.astype(jnp.bfloat16), head_grad),
        )

    head_query_grad, head_key_grad, head_value_grad = lax.map(
        attend_back, (head_queries, head_keys, head_values, head_mixed_grad, log_totals)
    )
    query_rot_grad = by_rows(head_query_grad, own_rows)
    window_grads = jnp.stack(
        [by_rows(head_key_grad, window_rows), by_rows(head_value_grad, window_rows)]
    )
    pair_grad = window_grads[:, hop_count * own_rows : (hop_count + 1) * own_rows]
    for slot_index, offset in enumerate(slot_offsets):
        if offset != 0:
            returned = passed_along(
                window_grads[:, slot_index * own_rows : (slot_index + 1) * own_rows].astype(
                    jnp.bfloat16
                ),
                "fsdp",
                -offset,
            ).astype(jnp.float32)
            pair_grad = pair_grad + returned
    key_normed_grad = rotate(pair_grad[0], cosine_table, -sine_table, head_count)
    key_part = jnp.sum(key_normed_grad * key_pre * key_factor, axis=0)
    key_grad = norm_backward(key_pre, key_factor, key_gain, key_normed_grad).astype(jnp.bfloat16)
    value_grad = pair_grad[1].astype(jnp.bfloat16)
    query_normed_grad = rotate(query_rot_grad, cosine_table, -sine_table, head_count)
    query_part = jnp.sum(query_normed_grad * query_pre * query_factor, axis=0)
    query_grad = norm_backward(query_pre, query_factor, query_gain, query_normed_grad).astype(
        jnp.bfloat16
    )
    pieces = (
        lax.all_gather(query_weight, "fsdp", axis=0, tiled=True),
        lax.all_gather(key_weight, "fsdp", axis=0, tiled=True),
        lax.all_gather(value_weight, "fsdp", axis=0, tiled=True),
    )
    columns = (
        against(query_grad, pieces[0])
        + against(key_grad, pieces[1])
        + against(value_grad, pieces[2])
    )
    gradient_tokens = (hidden_grad + columns).astype(jnp.bfloat16)
    gain_parts = (
        lax.psum_scatter(
            query_part.astype(jnp.bfloat16), "fsdp", scatter_dimension=0, tiled=True
        ).astype(jnp.float32),
        lax.psum_scatter(
            key_part.astype(jnp.bfloat16), "fsdp", scatter_dimension=0, tiled=True
        ).astype(jnp.float32),
        lax.psum_scatter(
            mixer_part.astype(jnp.bfloat16), "fsdp", scatter_dimension=0, tiled=True
        ).astype(jnp.float32),
        lax.psum_scatter(
            feeder_part.astype(jnp.bfloat16), "fsdp", scatter_dimension=0, tiled=True
        ).astype(jnp.float32),
    )
    shard_rows = model_width // group_size
    model_count = tokens.shape[1]
    stacked = lax.psum_scatter(
        jnp.concatenate(
            [
                across(tokens, query_grad),
                across(tokens, key_grad),
                across(tokens, value_grad),
                across(mixed_low, branch_grad),
                across(gate_grad, hidden_low).reshape(model_count, -1),
                across(up_grad, hidden_low).reshape(model_count, -1),
                across(inner_part, down_grad).reshape(model_count, -1),
            ],
            axis=1,
        ).astype(jnp.bfloat16),
        "fsdp",
        scatter_dimension=0,
        tiled=True,
    ).astype(jnp.float32)
    stacked, gain_query, gain_key, gain_mixer, gain_feeder = (
        lax.psum(stacked.astype(jnp.bfloat16), "rep").astype(jnp.float32),
        lax.psum(gain_parts[0].astype(jnp.bfloat16), "rep").astype(jnp.float32),
        lax.psum(gain_parts[1].astype(jnp.bfloat16), "rep").astype(jnp.float32),
        lax.psum(gain_parts[2].astype(jnp.bfloat16), "rep").astype(jnp.float32),
        lax.psum(gain_parts[3].astype(jnp.bfloat16), "rep").astype(jnp.float32),
    )
    gradient_query = stacked[:, :model_width]
    gradient_key = stacked[:, model_width : 2 * model_width]
    gradient_value = stacked[:, 2 * model_width : 3 * model_width]
    gradient_output = stacked[:, 3 * model_width : 4 * model_width]
    hidden_span = width_ratio * model_width
    gate_start = 4 * model_width
    gradient_gate = (
        stacked[:, gate_start : gate_start + hidden_span]
        .reshape(shard_rows * width_ratio, model_width)
        .T
    )
    gradient_up = (
        stacked[:, gate_start + hidden_span : gate_start + 2 * hidden_span]
        .reshape(shard_rows * width_ratio, model_width)
        .T
    )
    gradient_down = (
        stacked[:, gate_start + 2 * hidden_span :].reshape(shard_rows * width_ratio, model_width).T
    )
    return (
        result,
        gradient_tokens,
        gradient_query,
        gradient_key,
        gradient_value,
        gain_query,
        gain_key,
        gradient_output,
        gain_mixer,
        gradient_gate,
        gradient_up,
        gradient_down,
        gain_feeder,
    )


def solution(mesh):
    return jax.shard_map(
        body,
        mesh=mesh,
        in_specs=(
            P(("rep", "fsdp"), None),
            P("fsdp", None),
            P("fsdp", None),
            P("fsdp", None),
            P("fsdp"),
            P("fsdp"),
            P("fsdp", None),
            P("fsdp"),
            P(None, "fsdp"),
            P(None, "fsdp"),
            P(None, "fsdp"),
            P("fsdp"),
            P(),
            P(("rep", "fsdp"), None),
        ),
        out_specs=(
            P(("rep", "fsdp"), None),
            P(("rep", "fsdp"), None),
            P("fsdp", None),
            P("fsdp", None),
            P("fsdp", None),
            P("fsdp"),
            P("fsdp"),
            P("fsdp", None),
            P("fsdp"),
            P(None, "fsdp"),
            P(None, "fsdp"),
            P(None, "fsdp"),
            P("fsdp"),
        ),
        check_vma=False,
    )
```

profile of v0, /device:TPU:0, one launch (start us, length us, event | category | flops | bytes accessed | tf_op | source)
XLA Modules:
  0.0 6360.3 jit_solution(8324933085046162822)
XLA Ops:
  12.0 22.8 all-gather.1
  34.8 17.4 all-gather
  53.2 84.3 %all-gather.14.cloned.1.call-done = bf16[2048,2048]{1,0:T(8,128)(2,1)} async-done(((bf16[256,2048]{1,0:T(8,128)(2,1)}), bf16[2048,2048]{1,0:T(8,128)(2,1)}) %all-gather.14.cloned.1.call-update) | async-done | bytes 8388624 | tf_op jit(solution)/shard_map/all_gather | solution.py:119
  148.2 114.1 %all-gather.12.cloned.1.call-done = bf16[2048,2048]{1,0:T(8,128)(2,1)} async-done(((bf16[256,2048]{1,0:T(8,128)(2,1)}), bf16[2048,2048]{1,0:T(8,128)(2,1)}) %all-gather.12.cloned.1.call-update) | async-done | bytes 8388624 | tf_op jit(solution)/shard_map/all_gather | solution.py:118
  277.8 109.3 %all-gather.16.cloned.1.call-done = bf16[2048,2048]{1,0:T(8,128)(2,1)} async-done(((bf16[256,2048]{1,0:T(8,128)(2,1)}), bf16[2048,2048]{1,0:T(8,128)(2,1)}) %all-gather.16.cloned.1.call-update) | async-done | bytes 8388624 | tf_op jit(solution)/shard_map/all_gather | solution.py:120
  410.1 65.8 %collective-permute-done = bf16[2,256,2048]{2,1,0:T(8,128)(2,1)} collective-permute-done((bf16[2,256,2048]{2,1,0:T(8,128)(2,1)}, bf16[2,256,2048]{2,1,0:T(8,128)(2,1)}, u32[]{:S(2)}, u32[]{:S(2)}) %collective-permute-start) | collective-permute-done | bytes 2097184 | tf_op jit(solution)/shard_map/ppermute | solution.py:22
  478.4 303.4 %all-gather.2 = bf16[8,1,256]{2,1,0:T(2,128)(2,1)S(1)} all-gather(bf16[1,1,256]{2,1,0:T(2,128)(2,1)S(1)} %reshape.551), channel_id=1, replica_groups=mesh['rep'=4,'fsdp'=8] {'fsdp'}, dimensions={0}, use_global_device_ids=true | all-gather | bytes 4608 | tf_op jit(solution)/shard_map/all_gather | solution.py:178
  781.9 161.4 %all-gather.3 = bf16[8,1,256]{2,1,0:T(2,128)(2,1)S(1)} all-gather(bf16[1,1,256]{2,1,0:T(2,128)(2,1)S(1)} %reshape.553), channel_id=1, replica_groups=mesh['rep'=4,'fsdp'=8] {'fsdp'}, dimensions={0}, use_global_device_ids=true | all-gather | bytes 4608 | tf_op jit(solution)/shard_map/all_gather | solution.py:179
  963.3 161.8 %collective-permute-done.6 = bf16[2,256,2048]{2,1,0:T(8,128)(2,1)} collective-permute-done((bf16[2,256,2048]{2,1,0:T(8,128)(2,1)}, bf16[2,256,2048]{2,1,0:T(8,128)(2,1)}, u32[]{:S(2)}, u32[]{:S(2)}) %collective-permute-start.6) | collective-permute-done | bytes 2097184 | tf_op jit(solution)/shard_map/ppermute | solution.py:22
  1180.6 95.2 %while.30 = (s32[]{:T(128)}, bf16[16,256,128]{1,2,0:T(8,128)(2,1)S(1)}, f32[16,256]{1,0:T(8,128)}, bf16[16,256,128]{2,1,0:T(8,128)(2,1)}, bf16[16,2304,128]{2,1,...) while((s32[]{:T(128)}, ...), condition=%wide.region_7.8_spmd.clone.clone, body=%wide.region_4.7_spmd.clone.sunk.clone | while | flops 310247168 | bytes 8497545 | solution.py:174
  1284.0 211.8 %all-gather.20.cloned.1.call-done = bf16[2048,8192]{1,0:T(8,128)(2,1)} async-done(((bf16[2048,1024]{1,0:T(8,128)(2,1)}), bf16[2048,8192]{1,0:T(8,128)(2,1)}) %all-gather.20.cloned.1.call-update) | async-done | bytes 33554448 | tf_op jit(solution)/shard_map/all_gather | solution.py:189
  1495.8 17.1 fusion.81
  1512.8 659.8 %all-gather.22.cloned.1.call-done = bf16[2048,8192]{1,0:T(8,128)(2,1)} async-done(((bf16[2048,1024]{1,0:T(8,128)(2,1)}), bf16[2048,8192]{1,0:T(8,128)(2,1)}) %all-gather.22.cloned.1.call-update) | async-done | bytes 33554448 | tf_op jit(solution)/shard_map/all_gather | solution.py:190
  2172.7 24.3 multiply_convert_fusion.3
  2196.9 615.0 %all-gather.24.cloned.1.call-done = bf16[2048,8192]{1,0:T(8,128)(2,1)} async-done(((bf16[2048,1024]{1,0:T(8,128)(2,1)}), bf16[2048,8192]{1,0:T(8,128)(2,1)}) %all-gather.24.cloned.1.call-update) | async-done | bytes 33554448 | tf_op jit(solution)/shard_map/all_gather | solution.py:191
  2828.8 27.2 multiply_convert_fusion.1
  2856.0 17.1 fusion.82
  2873.1 17.5 multiply_reduce_fusion.1
  2900.2 290.5 %while.31 = (s32[]{:T(128)}, f32[16,256,128]{1,2,0:T(8,128)}, f32[16,2304,128]{1,2,0:T(8,128)}, f32[16,2304,128]{1,2,0:T(8,128)}, bf16[16,256,128]{2,1,0:T(8,128...) while((s32[]{:T(128)}, f32[16,256,128]{1,2,0:T(8,128)}, ...), condition=%wide.region_14.15_spmd.clone.clone, body=%wide.region_12.14_spmd.clone.sunk.clone | while | flops 764149504 | bytes 27618952 | solution.py:240
  3217.0 16.2 convolution_convert_fusion.2
  3252.1 51.2 collective-permute-done.15
  3329.4 55.1 reshape.541
  3384.5 55.2 reshape.542
  3439.7 16.4 convolution_convert_fusion
  3456.2 55.1 reshape.543
  3511.2 68.9 %collective-permute-done.11 = bf16[2,256,2048]{1,2,0:T(8,128)(2,1)} collective-permute-done((bf16[2,256,2048]{1,2,0:T(8,128)(2,1)}, bf16[2,256,2048]{1,2,0:T(8,128)(2,1)}, u32[]{:S(2)}, u32[]{:S(2)}) %collective-permute-start.11) | collective-permute-done | bytes 2097184 | tf_op jit(solution)/shard_map/ppermute | solution.py:22
  3699.1 23.1 constant_dynamic-update-slice_fusion.14
  3722.2 23.0 constant_dynamic-update-slice_fusion.13
  3745.2 23.0 constant_dynamic-update-slice_fusion.12
  3768.2 2219.6 %reduce-scatter.2.cloned.1.call-done = bf16[256,32768]{1,0:T(8,128)(2,1)} async-done(((bf16[2048,32768]{1,0:T(8,128)(2,1)}), bf16[256,32768]{1,0:T(8,128)(2,1)}) %reduce-scatter.2.cloned.1.call-update) | async-done | bytes 16777232 | tf_op jit(solution)/shard_map/reduce_scatter | solution.py:294
  5989.7 33.5 all-reduce.4
  6049.2 229.1 %all-reduce.8.cloned.1.call-done = bf16[256,32768]{1,0:T(8,128)(2,1)} async-done(((bf16[256,32768]{1,0:T(8,128)(2,1)}), bf16[256,32768]{1,0:T(8,128)(2,1)}) %all-reduce.8.cloned.1.call-update) | async-done | bytes 16777232 | tf_op jit(solution)/shard_map/psum | solution.py:312
  (772 shorter events, 843.1 us)
Async XLA Ops:
  7.2 130.3 %all-gather.14.cloned.1.call-start = ((), (), s32[]{:S(2)}) async-start(), calls=%async_computation.2 | async-start | bytes 9437184 | tf_op jit(solution)/shard_map/all_gather | solution.py:119
  7.9 254.4 %all-gather.12.cloned.1.call-start = ((), (), s32[]{:S(2)}) async-start(), calls=%async_computation.1 | async-start | bytes 9437184 | tf_op jit(solution)/shard_map/all_gather | solution.py:118
  8.7 378.4 %all-gather.16.cloned.1.call-start = ((), (), s32[]{:S(2)}) async-start(), calls=%async_computation.3 | async-start | bytes 9437184 | tf_op jit(solution)/shard_map/all_gather | solution.py:120
  9.4 1266.5 %all-gather.18.cloned.1.call-start = ((), (), s32[]{:S(2)}) async-start(), calls=%async_computation.4 | async-start | bytes 9437184 | tf_op jit(solution)/shard_map/all_gather | solution.py:177
  10.0 1485.8 %all-gather.20.cloned.1.call-start = ((), (), s32[]{:S(2)}) async-start(), calls=%async_computation.5 | async-start | bytes 37748736 | tf_op jit(solution)/shard_map/all_gather | solution.py:189
  10.6 2162.1 %all-gather.22.cloned.1.call-start = ((), (), s32[]{:S(2)}) async-start(), calls=%async_computation.6 | async-start | bytes 37748736 | tf_op jit(solution)/shard_map/all_gather | solution.py:190
  11.2 126.3 %copy-start = (bf16[256,2048]{1,0:T(8,128)(2,1)S(1)}, bf16[256,2048]{1,0:T(8,128)(2,1)}, u32[]{:S(2)}) copy-start(bf16[256,2048]{1,0:T(8,128)(2,1)} %param.18) | copy-start | bytes 3145732
  11.2 2800.7 %all-gather.24.cloned.1.call-start = ((), (), s32[]{:S(2)}) async-start(), calls=%async_computation.7 | async-start | bytes 37748736 | tf_op jit(solution)/shard_map/all_gather | solution.py:191
  11.9 5975.9 %reduce-scatter.2.cloned.1.call-start = ((), (), s32[]{:S(2)}) async-start(), calls=%async_computation.8 | async-start | bytes 150994944 | tf_op jit(solution)/shard_map/reduce_scatter | solution.py:294
  34.8 109.1 %copy-start.37 = (f32[8,1,256]{2,1,0:T(1,128)}, f32[8,1,256]{2,1,0:T(1,128)S(1)}, u32[]{:S(2)}) copy-start(f32[8,1,256]{2,1,0:T(1,128)S(1)} %convert_element_type.213) | copy-start | bytes 24580
  52.2 216.5 %copy-start.39 = (f32[8,1,256]{2,1,0:T(1,128)}, f32[8,1,256]{2,1,0:T(1,128)S(1)}, u32[]{:S(2)}) copy-start(f32[8,1,256]{2,1,0:T(1,128)S(1)} %convert_element_type.212) | copy-start | bytes 24580
  53.2 220.7 %copy-start.34 = (f32[256,64]{0,1:T(8,128)}, f32[256,64]{0,1:T(8,128)S(1)}, u32[]{:S(2)}) copy-start(f32[256,64]{0,1:T(8,128)S(1)} %get-tuple-element.425) | copy-start | bytes 196612
  392.9 389.0 %copy-start.74 = (bf16[256]{0:T(256)(128)(2,1)S(1)}, bf16[256]{0:T(256)(128)(2,1)}, u32[]{:S(2)}) copy-start(bf16[256]{0:T(256)(128)(2,1)} %param.29) | copy-start | bytes 1540
  394.5 81.3 %collective-permute-start = (bf16[2,256,2048]{2,1,0:T(8,128)(2,1)}, bf16[2,256,2048]{2,1,0:T(8,128)(2,1)}, u32[]{:S(2)}, u32[]{:S(2)}) collective-permute-start(bf16[2,256,2048]{2,1,0:T(8,128)(2,1)} %pad_maximum_fusion.1), channel_id=1, source_target_pairs={{0,7},{8,15},{16,23},{24,31}} | collective-permute-start | bytes 6291464 | tf_op jit(solution)/shard_map/ppermute | solution.py:22
  399.2 544.2 %collective-permute-start.1 = (bf16[2,256,2048]{2,1,0:T(8,128)(2,1)}, bf16[2,256,2048]{2,1,0:T(8,128)(2,1)}, u32[]{:S(2)}, u32[]{:S(2)}) collective-permute-start(bf16[2,256,2048]{2,1,0:T(8,128)(2,1)} %pad_maximum_fusion.1), channel_id=1, source_target_pairs={{0,6},{1,7},{8,14},{9,15},{16,22},{17,23},{24,30},{25,31}} | collective-permute-start | bytes 6291464 | tf_op jit(solution)/shard_map/ppermute | solution.py:22
  401.9 548.8 %collective-permute-start.2 = (bf16[2,256,2048]{2,1,0:T(8,128)(2,1)}, bf16[2,256,2048]{2,1,0:T(8,128)(2,1)}, u32[]{:S(2)}, u32[]{:S(2)}) collective-permute-start(bf16[2,256,2048]{2,1,0:T(8,128)(2,1)} %pad_maximum_fusion.1), channel_id=1, source_target_pairs={{0,5},{1,6},{2,7},{8,13},{9,14},{10,15},{16,21},{17,22},{18,23},{2... | collective-permute-start | bytes 6291464 | tf_op jit(solution)/shard_map/ppermute | solution.py:22
  404.8 552.9 %collective-permute-start.3 = (bf16[2,256,2048]{2,1,0:T(8,128)(2,1)}, bf16[2,256,2048]{2,1,0:T(8,128)(2,1)}, u32[]{:S(2)}, u32[]{:S(2)}) collective-permute-start(bf16[2,256,2048]{2,1,0:T(8,128)(2,1)} %pad_maximum_fusion.1), channel_id=1, source_target_pairs={{0,4},{1,5},{2,6},{3,7},{8,12},{9,13},{10,14},{11,15},{16,20},{17,... | collective-permute-start | bytes 6291464 | tf_op jit(solution)/shard_map/ppermute | solution.py:22
  407.4 552.2 %collective-permute-start.4 = (bf16[2,256,2048]{2,1,0:T(8,128)(2,1)}, bf16[2,256,2048]{2,1,0:T(8,128)(2,1)}, u32[]{:S(2)}, u32[]{:S(2)}) collective-permute-start(bf16[2,256,2048]{2,1,0:T(8,128)(2,1)} %pad_maximum_fusion.1), channel_id=1, source_target_pairs={{0,3},{1,4},{2,5},{3,6},{4,7},{8,11},{9,12},{10,13},{11,14},{12,15... | collective-permute-start | bytes 6291464 | tf_op jit(solution)/shard_map/ppermute | solution.py:22
  475.8 485.6 %collective-permute-start.5 = (bf16[2,256,2048]{2,1,0:T(8,128)(2,1)}, bf16[2,256,2048]{2,1,0:T(8,128)(2,1)}, u32[]{:S(2)}, u32[]{:S(2)}) collective-permute-start(bf16[2,256,2048]{2,1,0:T(8,128)(2,1)} %pad_maximum_fusion.1), channel_id=1, source_target_pairs={{0,2},{1,3},{2,4},{3,5},{4,6},{5,7},{8,10},{9,11},{10,12},{11,13},... | collective-permute-start | bytes 6291464 | tf_op jit(solution)/shard_map/ppermute | solution.py:22
  943.4 181.7 %collective-permute-start.6 = (bf16[2,256,2048]{2,1,0:T(8,128)(2,1)}, bf16[2,256,2048]{2,1,0:T(8,128)(2,1)}, u32[]{:S(2)}, u32[]{:S(2)}) collective-permute-start(bf16[2,256,2048]{2,1,0:T(8,128)(2,1)} %pad_maximum_fusion.1), channel_id=1, source_target_pairs={{0,1},{1,2},{2,3},{3,4},{4,5},{5,6},{6,7},{8,9},{9,10},{10,11},{11... | collective-permute-start | bytes 6291464 | tf_op jit(solution)/shard_map/ppermute | solution.py:22
  950.7 181.0 %collective-permute-start.7 = (bf16[2,256,2048]{2,1,0:T(8,128)(2,1)}, bf16[2,256,2048]{2,1,0:T(8,128)(2,1)S(1)}, u32[]{:S(2)}, u32[]{:S(2)}) collective-permute-start(bf16[2,256,2048]{2,1,0:T(8,128)(2,1)} %pad_maximum_fusion.1), channel_id=1, source_target_pairs={{1,0},{2,1},{3,2},{4,3},{5,4},{6,5},{7,6},{9,8},{10,9},{11,10},{12... | collective-permute-start | bytes 6291464 | tf_op jit(solution)/shard_map/ppermute | solution.py:22
  963.3 163.7 %copy-start.28 = (bf16[1,256,2048]{2,1,0:T(8,128)(2,1)S(1)}, bf16[1,256,2048]{2,1,0:T(8,128)(2,1)}, u32[]{:S(2)}) copy-start(bf16[1,256,2048]{2,1,0:T(8,128)(2,1)} %copy-done.27) | copy-start | bytes 3145732
  1283.9 888.7 %copy-start.17 = (bf16[256,2048]{1,0:T(8,128)(2,1)}, bf16[256,2048]{1,0:T(8,128)(2,1)S(1)}, u32[]{:S(2)}) copy-start(bf16[256,2048]{1,0:T(8,128)(2,1)S(1)} %fusion.65) | copy-start | bytes 3145732
  3210.9 92.4 %collective-permute-start.15 = (bf16[2,256,2048]{1,2,0:T(8,128)(2,1)}, bf16[2,256,2048]{1,2,0:T(8,128)(2,1)}, u32[]{:S(2)}, u32[]{:S(2)}) collective-permute-start(bf16[2,256,2048]{1,2,0:T(8,128)(2,1)} %get-tuple-element.391), channel_id=1, source_target_pairs={{0,1},{1,2},{2,3},{3,4},{4,5},{5,6},{6,7},{8,9},{9,10},{10,11},{11... | collective-permute-start | bytes 6291464 | tf_op jit(solution)/shard_map/ppermute | solution.py:22
  3214.4 90.1 %collective-permute-start.14 = (bf16[2,256,2048]{1,2,0:T(8,128)(2,1)}, bf16[2,256,2048]{1,2,0:T(8,128)(2,1)}, u32[]{:S(2)}, u32[]{:S(2)}) collective-permute-start(bf16[2,256,2048]{1,2,0:T(8,128)(2,1)} %get-tuple-element.392), channel_id=1, source_target_pairs={{1,0},{2,1},{3,2},{4,3},{5,4},{6,5},{7,6},{9,8},{10,9},{11,10},{12... | collective-permute-start | bytes 6291464 | tf_op jit(solution)/shard_map/ppermute | solution.py:22
  3215.7 94.1 %collective-permute-start.13 = (bf16[2,256,2048]{1,2,0:T(8,128)(2,1)}, bf16[2,256,2048]{1,2,0:T(8,128)(2,1)}, u32[]{:S(2)}, u32[]{:S(2)}) collective-permute-start(bf16[2,256,2048]{1,2,0:T(8,128)(2,1)} %get-tuple-element.393), channel_id=1, source_target_pairs={{2,0},{3,1},{4,2},{5,3},{6,4},{7,5},{10,8},{11,9},{12,10},{13,11},... | collective-permute-start | bytes 6291464 | tf_op jit(solution)/shard_map/ppermute | solution.py:22
  3233.2 278.0 %collective-permute-start.12 = (bf16[2,256,2048]{1,2,0:T(8,128)(2,1)}, bf16[2,256,2048]{1,2,0:T(8,128)(2,1)}, u32[]{:S(2)}, u32[]{:S(2)}) collective-permute-start(bf16[2,256,2048]{1,2,0:T(8,128)(2,1)} %get-tuple-element.394), channel_id=1, source_target_pairs={{3,0},{4,1},{5,2},{6,3},{7,4},{11,8},{12,9},{13,10},{14,11},{15,12... | collective-permute-start | bytes 6291464 | tf_op jit(solution)/shard_map/ppermute | solution.py:22
  3234.5 345.6 %collective-permute-start.11 = (bf16[2,256,2048]{1,2,0:T(8,128)(2,1)}, bf16[2,256,2048]{1,2,0:T(8,128)(2,1)}, u32[]{:S(2)}, u32[]{:S(2)}) collective-permute-start(bf16[2,256,2048]{1,2,0:T(8,128)(2,1)} %get-tuple-element.395), channel_id=1, source_target_pairs={{4,0},{5,1},{6,2},{7,3},{12,8},{13,9},{14,10},{15,11},{20,16},{21,... | collective-permute-start | bytes 6291464 | tf_op jit(solution)/shard_map/ppermute | solution.py:22
  3303.3 278.8 %collective-permute-start.10 = (bf16[2,256,2048]{1,2,0:T(8,128)(2,1)}, bf16[2,256,2048]{1,2,0:T(8,128)(2,1)}, u32[]{:S(2)}, u32[]{:S(2)}) collective-permute-start(bf16[2,256,2048]{1,2,0:T(8,128)(2,1)} %get-tuple-element.396), channel_id=1, source_target_pairs={{5,0},{6,1},{7,2},{13,8},{14,9},{15,10},{21,16},{22,17},{23,18},{2... | collective-permute-start | bytes 6291464 | tf_op jit(solution)/shard_map/ppermute | solution.py:22
  3304.6 277.5 %collective-permute-start.9 = (bf16[2,256,2048]{1,2,0:T(8,128)(2,1)}, bf16[2,256,2048]{1,2,0:T(8,128)(2,1)}, u32[]{:S(2)}, u32[]{:S(2)}) collective-permute-start(bf16[2,256,2048]{1,2,0:T(8,128)(2,1)} %get-tuple-element.397), channel_id=1, source_target_pairs={{6,0},{7,1},{14,8},{15,9},{22,16},{23,17},{30,24},{31,25}} | collective-permute-start | bytes 6291464 | tf_op jit(solution)/shard_map/ppermute | solution.py:22
  3309.8 272.3 %collective-permute-start.8 = (bf16[2,256,2048]{1,2,0:T(8,128)(2,1)}, bf16[2,256,2048]{1,2,0:T(8,128)(2,1)}, u32[]{:S(2)}, u32[]{:S(2)}) collective-permute-start(bf16[2,256,2048]{1,2,0:T(8,128)(2,1)} %get-tuple-element.390), channel_id=1, source_target_pairs={{7,0},{15,8},{23,16},{31,24}} | collective-permute-start | bytes 6291464 | tf_op jit(solution)/shard_map/ppermute | solution.py:22
  3768.2 2510.1 %all-reduce.8.cloned.1.call-start = ((), (), s32[]{:S(2)}) async-start(), calls=%async_computation.9 | async-start | bytes 33554432 | tf_op jit(solution)/shard_map/psum | solution.py:312
  (164 other events, 1178.0 us)
Sparse Core Ops, SparseCore 0:
  10.1 127.3 all-gather.13
  139.6 122.6 all-gather.11
  264.4 122.6 all-gather.15
  389.1 378.5 all-gather.17
  769.1 726.6 all-gather.19
  1497.2 675.4 all-gather.21
  2174.2 637.6 all-gather.23
  3768.3 2219.4 reduce-scatter.1
  5990.3 287.9 all-reduce.7
where the time goes:
time: 6380 us; the launch traced here: 6360 us
  waiting for transfers between devices  4610 us (72%)
  local copies, waits for them, and re-layouts  613 us (10%)
  blocking collectives  545 us (9%)
  matrix products  480 us (8%)
  other arithmetic  64.4 us (1%)
    reduce_scatter x1, waiting for transfers between devices, body(): lax.psum_scatter(jnp.concatenate([across(tokens, query_grad), across(toke...  2220 us
    all_gather x1, waiting for transfers between devices, body(): lax.all_gather(up_weight, 'fsdp', axis=1, tiled=True)  660 us
    all_gather x1, waiting for transfers between devices, body(): lax.all_gather(down_weight, 'fsdp', axis=1, tiled=True)  615 us
    ppermute x16, waiting for transfers between devices, passed_along(): return lax.ppermute(block, axis, route)  358 us
    all_gather x1, blocking collectives, body(): lax.all_gather(mixer_norm, 'fsdp', axis=0, tiled=True)  303 us
    psum x1, waiting for transfers between devices, body(): lax.psum(stacked.astype(jnp.bfloat16), 'rep').astype(jnp.float32)  229 us
    all_gather x1, waiting for transfers between devices, body(): lax.all_gather(gate_weight, 'fsdp', axis=1, tiled=True)  212 us
    dot_general x55, matrix products, against(): lax.dot_general(first_op, second_op, (((1,), (1,)), ((), ())), preferred_...  178 us
  transfers between devices with their start and end apart: 25, of which 15 were waited for; matrix products, arithmetic and copies ran while one was open for 8% of the time, Pallas kernels for 0%

commit v1 on v0

v1 whole, which is shorter than its diff:
```python
import functools

import jax
import jax.numpy as jnp
from jax import lax
from jax.experimental import pallas as pl
from jax.experimental.pallas import tpu as pltpu
from jax.sharding import PartitionSpec as P

HEADS = 16
HEAD_DIM = 128
SEQ = 2048
PIECE = 256
BLOCK = 512

norm_epsilon = 1e-06
rope_base = 500000.0
masked_score = -1e30
score_factor = HEAD_DIM ** (-0.5)
f32 = jnp.float32
bf16 = jnp.bfloat16


def matmul(a, b):
    return jnp.dot(a, b, preferred_element_type=f32)


def against(a, b):
    return lax.dot_general(a, b, (((1,), (1,)), ((), ())), preferred_element_type=f32)


def across(a, b):
    return lax.dot_general(a, b, (((0,), (0,)), ((), ())), preferred_element_type=f32)


def inverse_rms(values):
    return lax.rsqrt(jnp.mean(values * values, axis=-1, keepdims=True) + norm_epsilon)


def norm_backward(values, factor, gain_row, upstream):
    weighted = upstream * gain_row
    inner_mean = jnp.mean(weighted * values, axis=-1, keepdims=True)
    return factor * weighted - values * (factor * factor * factor) * inner_mean


def swapped(block, axis, bit):
    size = lax.axis_size(axis)
    return lax.ppermute(block, axis, [(i, i ^ bit) for i in range(size)])


def xor_sum(block, axis, size):
    bit = 1
    while bit < size:
        block = block + swapped(block, axis, bit)
        bit *= 2
    return block


def rep_sum(block):
    size = lax.axis_size("rep")
    me = lax.axis_index("rep")
    bits = []
    bit = 1
    while bit < size:
        bits.append(bit)
        bit *= 2
    for bit in bits:
        half = block.shape[0] // 2
        side = (me // bit) % 2
        keep = lax.dynamic_slice_in_dim(block, side * half, half, 0)
        send = lax.dynamic_slice_in_dim(block, (1 - side) * half, half, 0)
        got = swapped(send.astype(bf16), "rep", bit)
        block = keep.astype(f32) + got.astype(f32)
    block = block.astype(bf16)
    for bit in reversed(bits):
        side = (me // bit) % 2
        got = swapped(block, "rep", bit)
        block = jnp.where(
            side == 0, jnp.concatenate([block, got]), jnp.concatenate([got, block])
        )
    return block.astype(f32)


def piece_label(places, starts_ref):
    label = jnp.where((places >= starts_ref[0]) & (places < starts_ref[0] + PIECE), 1, 0)
    for j in range(1, starts_ref.shape[0]):
        inside = (places >= starts_ref[j]) & (places < starts_ref[j] + PIECE)
        label = jnp.where(inside, j + 1, label)
    return label


def allowed_block(starts_ref, query_start, query_count, key_start, key_count):
    query_places = query_start + lax.broadcasted_iota(jnp.int32, (query_count, 1), 0)
    key_places = key_start + lax.broadcasted_iota(jnp.int32, (1, key_count), 1)
    query_labels = piece_label(query_places, starts_ref)
    key_labels = piece_label(key_places, starts_ref)
    return (key_places <= query_places) | (
        (query_labels == key_labels) & (query_labels > 0)
    )


def straddles(starts_ref, edge):
    hit = jnp.int32(0)
    for j in range(starts_ref.shape[0]):
        begin = starts_ref[j]
        hit = jnp.where((begin < edge) & (begin + PIECE > edge), 1, hit)
    return hit


def prep_kernel(pre_ref, square_ref, gain_ref, cos_ref, sin_ref, q_ref, k_ref, v_ref):
    rows = pre_ref.shape[0]
    width = q_ref.shape[1]
    cosine, sine = cos_ref[...], sin_ref[...]
    for which, out_ref in ((0, q_ref), (1, k_ref)):
        square = jnp.broadcast_to(square_ref[which : which + 1, :], (HEAD_DIM, rows)).T
        factor = lax.rsqrt(square * (1.0 / (HEADS * HEAD_DIM)) + norm_epsilon)
        for at in range(0, width, HEAD_DIM):
            low, high = which * width + at, which * width + at + HEAD_DIM
            x = pre_ref[:, low:high] * factor * gain_ref[:, low:high]
            x = x * cosine + pltpu.roll(x, HEAD_DIM // 2, 1) * sine
            out_ref[:, at : at + HEAD_DIM] = x.astype(bf16)
    v_ref[...] = pre_ref[:, 2 * width :].astype(bf16)


def prep(pre, square, gains, cosine, sine):
    rows, triple = pre.shape
    width = triple // 3
    step = 512
    return pl.pallas_call(
        prep_kernel,
        grid=(rows // step,),
        in_specs=[
            pl.BlockSpec((step, triple), lambda i: (i, 0)),
            pl.BlockSpec((2, step), lambda i: (0, i)),
            pl.BlockSpec((1, 2 * width), lambda i: (0, 0)),
            pl.BlockSpec((step, HEAD_DIM), lambda i: (i, 0)),
            pl.BlockSpec((step, HEAD_DIM), lambda i: (i, 0)),
        ],
        out_specs=[pl.BlockSpec((step, width), lambda i: (i, 0))] * 3,
        out_shape=[jax.ShapeDtypeStruct((rows, width), bf16)] * 3,
        cost_estimate=pl.CostEstimate(
            flops=rows * triple * 8, bytes_accessed=rows * triple * 6, transcendentals=0
        ),
        name="prep",
    )(pre, square, gains, cosine, sine)


def attend_kernel(starts_ref, q_ref, k_ref, v_ref, low_ref, mixed_ref, total_ref):
    at = pl.program_id(1)
    query = q_ref[...]
    rows = query.shape[0]

    def step(carry, key_start, key_count, masked):
        row_max, row_sum, mixed = carry
        key = k_ref[pl.ds(key_start, key_count), :]
        value = v_ref[pl.ds(key_start, key_count), :]
        scores = against(query, key) * score_factor
        if masked:
            allowed = allowed_block(starts_ref, at * rows, rows, key_start, key_count)
            scores = jnp.where(allowed, scores, masked_score)
        new_max = jnp.maximum(row_max, jnp.max(scores, axis=1, keepdims=True))
        fade = jnp.exp(row_max - new_max)
        exponent = jnp.exp(scores - new_max)
        row_sum = row_sum * fade + jnp.sum(exponent, axis=1, keepdims=True)
        mixed = mixed * fade + matmul(exponent.astype(bf16), value)
        return new_max, row_sum, mixed

    carry = (
        jnp.full((rows, 1), masked_score, f32),
        jnp.zeros((rows, 1), f32),
        jnp.zeros((rows, HEAD_DIM), f32),
    )
    carry = step(carry, pl.multiple_of(at * rows, rows), rows, True)
    carry = lax.fori_loop(
        0,
        at,
        lambda j, c: step(c, pl.multiple_of(j * rows, rows), rows, False),
        carry,
    )
    edge = (at + 1) * rows
    carry = lax.fori_loop(
        0,
        straddles(starts_ref, edge),
        lambda j, c: step(c, pl.multiple_of(edge, rows), PIECE, True),
        carry,
    )
    row_max, row_sum, mixed = carry
    mixed = mixed / row_sum
    low_ref[...] = mixed.astype(bf16)
    mixed_ref[...] = mixed
    total_ref[...] = jnp.broadcast_to(row_max + jnp.log(row_sum), (rows, HEAD_DIM))


def attend(starts, query, key, value):
    rows, width = query.shape
    heads = width // HEAD_DIM
    block = pl.BlockSpec((BLOCK, HEAD_DIM), lambda h, i, s: (i, h))
    column = pl.BlockSpec((rows, HEAD_DIM), lambda h, i, s: (0, h))
    return pl.pallas_call(
        attend_kernel,
        grid_spec=pltpu.PrefetchScalarGridSpec(
            num_scalar_prefetch=1,
            grid=(heads, rows // BLOCK),
            in_specs=[block, column, column],
            out_specs=[block, block, block],
        ),
        out_shape=[
            jax.ShapeDtypeStruct((rows, width), bf16),
            jax.ShapeDtypeStruct((rows, width), f32),
            jax.ShapeDtypeStruct((rows, width), f32),
        ],
        cost_estimate=pl.CostEstimate(
            flops=heads * rows * rows * HEAD_DIM * 2,
            bytes_accessed=rows * width * 16,
            transcendentals=heads * rows * rows // 2,
        ),
        name="attend",
    )(starts, query, key, value)


def attend_back_kernel(
    starts_ref,
    q_ref,
    grad_ref,
    mixed_ref,
    total_ref,
    k_ref,
    v_ref,
    cos_ref,
    sin_ref,
    dq_ref,
    dk_ref,
    dv_ref,
    dv_total,
):
    at = pl.program_id(1)
    query = q_ref[...]
    grad = grad_ref[...]
    rows = query.shape[0]
    total = total_ref[:, 0:1]
    inner = jnp.sum(grad.astype(f32) * mixed_ref[...], axis=1, keepdims=True)

    @pl.when(at == 0)
    def _():
        dk_ref[...] = jnp.zeros_like(dk_ref)
        dv_total[...] = jnp.zeros_like(dv_total)

    def step(dq, key_start, key_count, masked):
        here = pl.ds(key_start, key_count)
        key = k_ref[here, :]
        value = v_ref[here, :]
        scores = against(query, key) * score_factor
        if masked:
            allowed = allowed_block(starts_ref, at * rows, rows, key_start, key_count)
            scores = jnp.where(allowed, scores, masked_score)
        shares = jnp.exp(scores - total)
        share_grad = against(grad, value)
        score_grad = (shares * (share_grad - inner)).astype(bf16)
        dk_ref[here, :] += across(score_grad, query)
        dv_total[here, :] += across(shares.astype(bf16), grad)
        return dq + matmul(score_grad, key)

    dq = jnp.zeros((rows, HEAD_DIM), f32)
    dq = step(dq, pl.multiple_of(at * rows, rows), rows, True)
    dq = lax.fori_loop(
        0, at, lambda j, c: step(c, pl.multiple_of(j * rows, rows), rows, False), dq
    )
    edge = (at + 1) * rows
    dq = lax.fori_loop(
        0,
        straddles(starts_ref, edge),
        lambda j, c: step(c, pl.multiple_of(edge, rows), PIECE, True),
        dq,
    )

    def unrotated(x, cosine, sine):
        x = x * score_factor
        return x * cosine - pltpu.roll(x, HEAD_DIM // 2, 1) * sine

    mine = pl.ds(pl.multiple_of(at * rows, rows), rows)
    dq_ref[...] = unrotated(dq, cos_ref[mine, :], sin_ref[mine, :])

    @pl.when(at == pl.num_programs(1) - 1)
    def _():
        dk_ref[...] = unrotated(dk_ref[...], cos_ref[...], sin_ref[...])
        dv_ref[...] = dv_total[...].astype(bf16)


def attend_back(starts, query, grad, mixed, total, key, value, cosine, sine):
    rows, width = query.shape
    heads = width // HEAD_DIM
    block = pl.BlockSpec((BLOCK, HEAD_DIM), lambda h, i, s: (i, h))
    column = pl.BlockSpec((rows, HEAD_DIM), lambda h, i, s: (0, h))
    table = pl.BlockSpec((rows, HEAD_DIM), lambda h, i, s: (0, 0))
    return pl.pallas_call(
        attend_back_kernel,
        grid_spec=pltpu.PrefetchScalarGridSpec(
            num_scalar_prefetch=1,
            grid=(heads, rows // BLOCK),
            in_specs=[block, block, block, block, column, column, table, table],
            out_specs=[block, column, column],
            scratch_shapes=[pltpu.VMEM((rows, HEAD_DIM), f32)],
        ),
        out_shape=[
            jax.ShapeDtypeStruct((rows, width), f32),
            jax.ShapeDtypeStruct((rows, width), f32),
            jax.ShapeDtypeStruct((rows, width), bf16),
        ],
        cost_estimate=pl.CostEstimate(
            flops=heads * rows * rows * HEAD_DIM * 5,
            bytes_accessed=rows * width * 28,
            transcendentals=heads * rows * rows // 2,
        ),
        name="attend_back",
    )(starts, query, grad, mixed, total, key, value, cosine, sine)


def body(
    tokens,
    query_weight,
    key_weight,
    value_weight,
    query_norm,
    key_norm,
    output_weight,
    mixer_norm,
    gate_weight,
    up_weight,
    down_weight,
    feeder_norm,
    piece_starts,
    cotangent,
):
    own_rows, model_width = tokens.shape
    group = lax.axis_size("fsdp")
    me = lax.axis_index("fsdp")
    chain = SEQ // own_rows
    spot = me % chain
    width = model_width // chain
    shard = model_width // group
    sequence = ((lax.axis_index("rep") * group + me) * own_rows) // SEQ
    starts = lax.dynamic_index_in_dim(piece_starts, sequence, 0, keepdims=False)
    teams = None
    if group != chain:
        teams = [[b * chain + i for i in range(chain)] for b in range(group // chain)]

    def of_sequence(block):
        return lax.all_gather(block, "fsdp", axis=0, tiled=True, axis_index_groups=teams)

    def to_sequence_rows(block):
        return lax.psum_scatter(
            block.astype(bf16),
            "fsdp",
            scatter_dimension=0,
            tiled=True,
            axis_index_groups=teams,
        ).astype(f32)

    def of_group(block):
        return lax.all_gather(block, "fsdp", axis=0, tiled=True)

    def to_group_rows(block):
        return lax.psum_scatter(
            block.astype(bf16), "fsdp", scatter_dimension=0, tiled=True
        ).astype(f32)

    def placed(block, start, length, axis):
        shape = list(block.shape)
        shape[axis] = length
        return lax.dynamic_update_slice_in_dim(
            jnp.zeros(shape, block.dtype), block, start, axis
        )

    half = HEAD_DIM // 2
    frequency = rope_base ** (-(jnp.arange(half, dtype=f32) * (2.0 / HEAD_DIM)))
    angles = jnp.arange(SEQ, dtype=jnp.int32).astype(f32)[:, None] * frequency[None, :]
    cosine, sine = jnp.cos(angles), jnp.sin(angles)
    cosine = jnp.concatenate([cosine, cosine], axis=1)
    sine = jnp.concatenate([-sine, sine], axis=1)

    own_gains = jnp.stack([query_norm, key_norm, mixer_norm, feeder_norm]).astype(f32)
    gains = xor_sum(placed(own_gains, me * shard, model_width, 1), "fsdp", group)
    pair_gains = lax.dynamic_slice_in_dim(gains[:2], spot * width, width, 1)
    mixer_gain = gains[2:3]
    feeder_gain = gains[3:4]

    rows_weight = jnp.stack([query_weight, key_weight, value_weight], axis=1)
    rows_weight = rows_weight.reshape(shard, 3, chain, width).transpose(2, 0, 1, 3)
    rows_weight = rows_weight.reshape(chain, shard, 3 * width)
    if group != chain:
        rows_weight = jnp.tile(rows_weight, (group // chain, 1, 1))
    triple_weight = lax.all_to_all(rows_weight, "fsdp", 0, 0).reshape(
        model_width, 3 * width
    )
    if group == chain:
        head_output = output_weight
    else:
        head_output = lax.dynamic_slice_in_dim(
            lax.all_gather(output_weight, "fsdp", axis=0, tiled=True),
            spot * width,
            width,
            0,
        )

    all_tokens = of_sequence(tokens)
    pre = matmul(all_tokens, triple_weight)
    query_pre, key_pre = pre[:, :width], pre[:, width : 2 * width]
    squares = jnp.stack(
        [jnp.sum(query_pre * query_pre, axis=1), jnp.sum(key_pre * key_pre, axis=1)]
    )
    squares = xor_sum(squares, "fsdp", chain)
    query_low, key_low, value_low = prep(
        pre, squares, pair_gains.reshape(1, 2 * width), cosine, sine
    )
    mixed_low, mixed, log_total = attend(starts, query_low, key_low, value_low)
    branch_pre = to_sequence_rows(matmul(mixed_low, head_output))
    branch_factor = inverse_rms(branch_pre)
    hidden = tokens.astype(f32) + branch_pre * branch_factor * mixer_gain

    all_hidden = of_group(hidden.astype(bf16))
    gate = matmul(all_hidden, gate_weight).astype(bf16)
    up = matmul(all_hidden, up_weight).astype(bf16)
    gate_wide, up_wide = gate.astype(f32), up.astype(f32)
    sigmoid = jax.nn.sigmoid(gate_wide)
    inner = (gate_wide * sigmoid * up_wide).astype(bf16)
    down_pre = to_group_rows(against(inner, down_weight))
    down_factor = inverse_rms(down_pre)
    result = (hidden + down_pre * down_factor * feeder_gain).astype(bf16)

    tangent = cotangent.astype(f32)
    feeder_part = jnp.sum(tangent * down_pre * down_factor, axis=0)
    down_grad = norm_backward(down_pre, down_factor, feeder_gain, tangent).astype(bf16)
    all_down_grad = of_group(down_grad)
    inner_grad = matmul(all_down_grad, down_weight)
    gate_grad = (
        inner_grad * up_wide * sigmoid * (1.0 + gate_wide * (1.0 - sigmoid))
    ).astype(bf16)
    up_grad = (inner_grad * gate_wide * sigmoid).astype(bf16)
    feed_back = to_group_rows(
        against(gate_grad, gate_weight) + against(up_grad, up_weight)
    )
    hidden_grad = tangent + feed_back
    mixer_part = jnp.sum(hidden_grad * branch_pre * branch_factor, axis=0)
    branch_grad = norm_backward(
        branch_pre, branch_factor, mixer_gain, hidden_grad
    ).astype(bf16)
    gradient_down = rep_sum(across(all_down_grad, inner))
    gradient_gate = rep_sum(across(all_hidden, gate_grad))
    gradient_up = rep_sum(across(all_hidden, up_grad))

    all_branch_grad = of_sequence(branch_grad)
    mixed_grad = against(all_branch_grad, head_output).astype(bf16)
    query_turn, key_turn, value_grad = attend_back(
        starts,
        query_low,
        mixed_grad,
        mixed,
        log_total,
        key_low,
        value_low,
        cosine,
        sine,
    )
    query_gain, key_gain = pair_gains[0:1], pair_gains[1:2]
    means = jnp.stack(
        [
            jnp.sum(query_gain * query_turn * query_pre, axis=1),
            jnp.sum(key_gain * key_turn * key_pre, axis=1),
        ]
    )
    means = xor_sum(means, "fsdp", chain) * (1.0 / model_width)
    factors = lax.rsqrt(squares * (1.0 / model_width) + norm_epsilon)

    def pair_back(turn, pre_part, gain, at):
        factor = factors[at][:, None]
        grad = factor * gain * turn - pre_part * factor * factor * factor * means[at][:, None]
        return grad.astype(bf16), jnp.sum(turn * pre_part * factor, axis=0)

    query_grad, query_part = pair_back(query_turn, query_pre, query_gain, 0)
    key_grad, key_part = pair_back(key_turn, key_pre, key_gain, 1)
    triple_grad = jnp.concatenate([query_grad, key_grad, value_grad], axis=1)
    gradient_tokens = (
        hidden_grad + to_sequence_rows(against(triple_grad, triple_weight))
    ).astype(bf16)

    output_part = across(mixed_low, all_branch_grad)
    triple_part = across(all_tokens, triple_grad)
    if group == chain:
        output_rows = output_part
        triple_rows = lax.all_to_all(
            triple_part.astype(bf16).reshape(chain, shard, 3 * width), "fsdp", 0, 0
        )
        triple_rows = triple_rows.reshape(chain, shard, 3, width).transpose(2, 1, 0, 3)
    else:
        output_rows = to_group_rows(placed(output_part, spot * width, model_width, 0))
        triple_rows = to_group_rows(
            placed(
                triple_part.reshape(model_width, 3, 1, width), spot, chain, 2
            ).reshape(model_width, 3 * model_width)
        )
        triple_rows = triple_rows.reshape(shard, 3, chain, width).transpose(1, 0, 2, 3)
    triple_rows = triple_rows.reshape(3 * shard, model_width)
    triple_rows = jnp.concatenate([triple_rows.astype(bf16), output_rows.astype(bf16)])
    four = rep_sum(triple_rows)

    gain_parts = jnp.stack(
        [
            lax.dynamic_update_slice_in_dim(
                jnp.zeros((model_width,), f32), query_part, spot * width, 0
            ),
            lax.dynamic_update_slice_in_dim(
                jnp.zeros((model_width,), f32), key_part, spot * width, 0
            ),
            mixer_part,
            feeder_part,
        ]
    )
    gain_parts = xor_sum(xor_sum(gain_parts, "fsdp", group), "rep", lax.axis_size("rep"))
    gain_own = lax.dynamic_slice_in_dim(gain_parts, me * shard, shard, 1)
    return (
        result,
        gradient_tokens,
        four[:shard],
        four[shard : 2 * shard],
        four[2 * shard : 3 * shard],
        gain_own[0],
        gain_own[1],
        four[3 * shard :],
        gain_own[2],
        gradient_gate,
        gradient_up,
        gradient_down,
        gain_own[3],
    )


def solution(mesh):
    rows, ends = P(("rep", "fsdp"), None), P(None, "fsdp")
    tops, line = P("fsdp", None), P("fsdp")
    return jax.shard_map(
        body,
        mesh=mesh,
        in_specs=(
            rows, tops, tops, tops, line, line, tops, line, ends, ends, ends, line, P(), rows,
        ),
        out_specs=(
            rows, rows, tops, tops, tops, line, line, tops, line, ends, ends, ends, line,
        ),
        check_vma=False,
    )
```

time: 6380 us -> 1640 us (0.26)
  waiting for transfers between devices: 4610 us -> 1190 us
  local copies, waits for them, and re-layouts: 613 us -> 54.4 us
  blocking collectives: 545 us -> 0 us
  matrix products: 480 us -> 167 us
    reduce_scatter x1 -> x4, waiting for transfers between devices: 2220 us -> 440 us  [the longest x2 291 us: to_group_rows(): lax.psum_scatter(block.astype(bf16), 'fsdp', scatter_dimension=0, tiled=T...]
    all_gather x7 -> x4, waiting for transfers between devices: 1790 us -> 391 us  [the longest x2 247 us: of_group(): return lax.all_gather(block, 'fsdp', axis=0, tiled=True)]
    all_gather x4 -> x0, blocking collectives: 505 us -> none  [the longest x1 303 us: body(): lax.all_gather(mixer_norm, 'fsdp', axis=0, tiled=True)]
    dot_general x133 -> x15, matrix products: 480 us -> 167 us  [the longest x5 57.1 us: matmul(): return jnp.dot(a, b, preferred_element_type=f32)]
    psum x1 -> x0, waiting for transfers between devices: 229 us -> none  [body(): lax.psum(stacked.astype(jnp.bfloat16), 'rep').astype(jnp.float32)]
    reshape x9 -> x1, local copies, waits for them, and re-layouts: 202 us -> 1.88 us  [body(): triple_part.astype(bf16).reshape(chain, shard, 3 * width)]
    ppermute x16 -> x30, waiting for transfers between devices: 358 us -> 178 us  [swapped(): return lax.ppermute(block, axis, [(i, i ^ bit) for i in range(size)])]
    all_to_all x0 -> x2, waiting for transfers between devices: none -> 178 us  [the longest x1 111 us: body(): lax.all_to_all(rows_weight, 'fsdp', 0, 0).reshape(model_width, 3 * width)]
  transfers between devices with their start and end apart: 25 -> 40, of which waited for: 15 -> 24; matrix products, arithmetic and copies ran while one was open for 8% -> 10% of each run, Pallas kernels for 0% -> 0%
where the time goes in v1:
time: 1640 us; the launch traced here: 1630 us
  waiting for transfers between devices  1190 us (73%)
  matrix products  167 us (10%)
  other arithmetic  99.3 us (6%)
  Pallas kernels  58.2 us (4%)
  local copies, waits for them, and re-layouts  54.4 us (3%)
  starting transfers between devices  44.1 us (3%)
    reduce_scatter x2, waiting for transfers between devices, to_group_rows(): lax.psum_scatter(block.astype(bf16), 'fsdp', scatter_dimension=0, tiled=T...  291 us
    all_gather x2, waiting for transfers between devices, of_group(): return lax.all_gather(block, 'fsdp', axis=0, tiled=True)  247 us
    ppermute x30, waiting for transfers between devices, swapped(): return lax.ppermute(block, axis, [(i, i ^ bit) for i in range(size)])  178 us
    reduce_scatter x2, waiting for transfers between devices, to_sequence_rows(): lax.psum_scatter(block.astype(bf16), 'fsdp', scatter_dimension=0, tiled=T...  149 us
    all_gather x2, waiting for transfers between devices, of_sequence(): lax.all_gather(block, 'fsdp', axis=0, tiled=True, axis_index_groups=teams)  144 us
    all_to_all x1, waiting for transfers between devices, body(): lax.all_to_all(rows_weight, 'fsdp', 0, 0).reshape(model_width, 3 * width)  111 us
    all_to_all x1, waiting for transfers between devices, body(): lax.all_to_all(triple_part.astype(bf16).reshape(chain, shard, 3 * width),...  67.3 us
    dot_general x5, matrix products, matmul(): return jnp.dot(a, b, preferred_element_type=f32)  57.1 us
  transfers between devices with their start and end apart: 40, of which 24 were waited for; matrix products, arithmetic and copies ran while one was open for 10% of the time, Pallas kernels for 0%

profile of v1, /device:TPU:0, one launch (start us, length us, event | category | flops | bytes accessed | tf_op | source)
XLA Modules:
  0.0 1628.4 jit_solution(14343622019565831384)
XLA Ops:
  26.1 29.6 %collective-permute-done.3 = f32[4,2048]{1,0:T(4,128)S(1)} collective-permute-done((f32[4,2048]{1,0:T(4,128)S(1)}, f32[4,2048]{1,0:T(4,128)S(1)}, u32[]{:S(2)}, u32[]{:S(2)}) %collective-permute-start.3) | collective-permute-done | bytes 32800 | tf_op jit(solution)/shard_map/ppermute | solution.py:48
  60.7 111.1 %all-to-all-done = bf16[8,256,768]{1,2,0:T(8,128)(2,1)} async-done(((bf16[8,256,768]{1,2,0:T(8,128)(2,1)}), bf16[8,256,768]{1,2,0:T(8,128)(2,1)}, u32[]{:S(2)}, u32[]{:S(2)}) %all-to-all-start) | async-done | bytes 3145760 | tf_op jit(solution)/shard_map/all_to_all | solution.py:392
  176.5 21.1 %all-gather.5.cloned.1.call-done = bf16[2048,2048]{1,0:T(8,128)(2,1)} async-done(((bf16[256,2048]{1,0:T(8,128)(2,1)}), bf16[2048,2048]{1,0:T(8,128)(2,1)}) %all-gather.5.cloned.1.call-update) | async-done | bytes 8388624 | tf_op jit(solution)/shard_map/all_gather | solution.py:348
  197.6 10.0 convolution_bitcast_fusion.pre_ref
  231.5 20.1 %attend.1 = (bf16[2048,256]{1,0:T(8,128)(2,1)}, f32[2048,256]{1,0:T(8,128)}, f32[2048,256]{1,0:T(8,128)}) custom-call(s32[2]{0:T(128)} %fusion.40.starts_ref, bf16[2048,256]{1,0:T(8,128)(2,1)} %get-tuple-element.22.q_ref, bf16[2048,256]{1,0:T(8,128)(2,1)} %get-tuple-element.23.k_ref, bf16[2048,256]{1,0:T(8,128)(2,1)} %get-tuple-element.24.v_ref), custom_call_target="tpu_custom_call" | custom-call | flops 2147483648 | bytes 8388608 | tf_op jit(solution)/shard_map/attend/pallas_call | solution.py:199
  258.7 149.0 %reduce-scatter.5.cloned.1.call-done = bf16[256,2048]{1,0:T(8,128)(2,1)} async-done(((bf16[2048,2048]{1,0:T(8,128)(2,1)}), bf16[256,2048]{1,0:T(8,128)(2,1)}) %reduce-scatter.5.cloned.1.call-update) | async-done | bytes 1048592 | tf_op jit(solution)/shard_map/reduce_scatter | solution.py:351
  411.9 123.7 %all-gather.7.cloned.1.call-done = bf16[2048,2048]{1,0:T(8,128)(2,1)} async-done(((bf16[256,2048]{1,0:T(8,128)(2,1)}), bf16[2048,2048]{1,0:T(8,128)(2,1)}) %all-gather.7.cloned.1.call-update) | async-done | bytes 8388624 | tf_op jit(solution)/shard_map/all_gather | solution.py:360
  535.6 12.6 convolution_convert_fusion.3
  548.2 9.1 convolution_convert_fusion.4
  559.4 11.6 convolution_convert_fusion.1
  571.0 145.7 %reduce-scatter.7.cloned.1.call-done = bf16[256,2048]{1,0:T(8,128)(2,1)} async-done(((bf16[2048,2048]{1,0:T(8,128)(2,1)}), bf16[256,2048]{1,0:T(8,128)(2,1)}) %reduce-scatter.7.cloned.1.call-update) | async-done | bytes 1048592 | tf_op jit(solution)/shard_map/reduce_scatter | solution.py:363
  723.5 123.7 %all-gather.9.cloned.1.call-done = bf16[2048,2048]{1,0:T(8,128)(2,1)} async-done(((bf16[256,2048]{1,0:T(8,128)(2,1)}), bf16[2048,2048]{1,0:T(8,128)(2,1)}) %all-gather.9.cloned.1.call-update) | async-done | bytes 8388624 | tf_op jit(solution)/shard_map/all_gather | solution.py:360
  847.2 18.5 %fusion.9 = (bf16[2048,1024]{1,0:T(8,128)(2,1)}, bf16[2048,1024]{1,0:T(8,128)(2,1)S(1)}) fusion(bf16[2048,1024]{1,0:T(8,128)(2,1)} %copy-done.42, bf16[2048,1024]{1,0:T(8,128)(2,1)} %copy-done.41, bf16[2048,2048]{1,0:T(8,128)(2,1)} %all-gather.9.cloned.1.call-done, bf16[2048,1024]{1,0:T(8,128)(2,1)} %param.24), kind=kOutput, calls=%fused_computation.16 | convolution fusion | flops 8621391872 | bytes 29360128 | tf_op jit(solution)/shard_map/dot_general | solution.py:25
  865.7 11.8 fusion.55
  877.5 15.9 add_convert_fusion
  893.4 145.7 %reduce-scatter.9.cloned.1.call-done = bf16[256,2048]{1,0:T(8,128)(2,1)} async-done(((bf16[2048,2048]{1,0:T(8,128)(2,1)}), bf16[256,2048]{1,0:T(8,128)(2,1)}) %reduce-scatter.9.cloned.1.call-update) | async-done | bytes 1048592 | tf_op jit(solution)/shard_map/reduce_scatter | solution.py:363
  1046.8 122.9 %all-gather.11.cloned.1.call-done = bf16[2048,2048]{1,0:T(8,128)(2,1)} async-done(((bf16[256,2048]{1,0:T(8,128)(2,1)}), bf16[2048,2048]{1,0:T(8,128)(2,1)}) %all-gather.11.cloned.1.call-update) | async-done | bytes 8388624 | tf_op jit(solution)/shard_map/all_gather | solution.py:348
  1176.4 31.8 %attend_back.1 = (f32[2048,256]{1,0:T(8,128)}, f32[2048,256]{1,0:T(8,128)}, bf16[2048,256]{1,0:T(8,128)(2,1)}) custom-call(s32[2]{0:T(128)} %fusion.40.starts_ref, bf16[2048,256]{1,0:T(8,128)(2,1)} %get-tuple-element.22.q_ref, bf16[2048,256]{1,0:T(8,128)(2,1)} %convolution_convert_fusion.7.grad_ref, f32[2048,256]{1,0:T(8,128)} %get-tuple-element.26.mixed_ref, ...), custom_call_target="tpu_custom_call" | custom-call | flops 5368709120 | bytes 14680064 | tf_op jit(solution)/shard_map/attend_back/pallas_call | solution.py:295
  1230.6 9.1 convolution_convert_fusion
  1239.7 9.5 convolution_convert_fusion.5
  1256.3 17.6 %fusion.46 = f32[2048,1024]{1,0:T(8,128)S(1)} fusion(bf16[2048,2048]{1,0:T(8,128)(2,1)} %all-gather.9.cloned.1.call-done, bf16[2048,1024]{1,0:T(8,128)(2,1)} %copy-done.41, bf16[2048,1024]{1,0:T(8,128)(2,1)} %copy-done.42), kind=kOutput, calls=%fused_computation.142 | convolution fusion | flops 8606711808 | bytes 25165824 | tf_op jit(solution)/shard_map/dot_general | solution.py:33
  1278.9 11.7 fusion.57
  1296.1 14.1 fusion.56
  1316.0 67.3 %all-to-all-done.1 = bf16[8,256,768]{1,2,0:T(8,128)(2,1)} async-done(((bf16[8,256,768]{1,2,0:T(8,128)(2,1)}), bf16[8,256,768]{1,2,0:T(8,128)(2,1)}, u32[]{:S(2)}, u32[]{:S(2)}) %all-to-all-start.1) | async-done | bytes 3145760 | tf_op jit(solution)/shard_map/all_to_all | solution.py:490
  1416.1 13.3 collective-permute-done.27
  1433.1 18.8 %collective-permute-done.23 = bf16[512,1024]{1,0:T(8,128)(2,1)} collective-permute-done((bf16[512,1024]{1,0:T(8,128)(2,1)}, bf16[512,1024]{1,0:T(8,128)(2,1)}, u32[]{:S(2)}, u32[]{:S(2)}) %collective-permute-start.23) | collective-permute-done | bytes 1048608 | tf_op jit(solution)/shard_map/ppermute | solution.py:48
  1462.5 11.7 collective-permute-done.19
  1477.6 19.2 %collective-permute-done.28 = bf16[512,1024]{1,0:T(8,128)(2,1)} collective-permute-done((bf16[512,1024]{1,0:T(8,128)(2,1)S(1)}, bf16[512,1024]{1,0:T(8,128)(2,1)}, u32[]{:S(2)}, u32[]{:S(2)}) %collective-permute-start.28) | collective-permute-done | bytes 1048608 | tf_op jit(solution)/shard_map/ppermute | solution.py:48
  1500.8 18.5 %collective-permute-done.24 = bf16[512,1024]{1,0:T(8,128)(2,1)} collective-permute-done((bf16[512,1024]{1,0:T(8,128)(2,1)S(1)}, bf16[512,1024]{1,0:T(8,128)(2,1)}, u32[]{:S(2)}, u32[]{:S(2)}) %collective-permute-start.24) | collective-permute-done | bytes 1048608 | tf_op jit(solution)/shard_map/ppermute | solution.py:48
  1522.1 19.7 %collective-permute-done.10 = bf16[256,2048]{1,0:T(8,128)(2,1)} collective-permute-done((bf16[256,2048]{1,0:T(8,128)(2,1)}, bf16[256,2048]{1,0:T(8,128)(2,1)}, u32[]{:S(2)}, u32[]{:S(2)}) %collective-permute-start.10) | collective-permute-done | bytes 1048608 | tf_op jit(solution)/shard_map/ppermute | solution.py:48
  1545.4 18.8 %collective-permute-done.20 = bf16[512,1024]{1,0:T(8,128)(2,1)} collective-permute-done((bf16[512,1024]{1,0:T(8,128)(2,1)}, bf16[512,1024]{1,0:T(8,128)(2,1)}, u32[]{:S(2)}, u32[]{:S(2)}) %collective-permute-start.20) | collective-permute-done | bytes 1048608 | tf_op jit(solution)/shard_map/ppermute | solution.py:48
  1573.8 12.5 collective-permute-done.11
  (265 shorter events, 237.7 us)
Async XLA Ops:
  7.2 190.4 %all-gather.5.cloned.1.call-start = ((), (), s32[]{:S(2)}) async-start(), calls=%async_computation.6 | async-start | bytes 9437184 | tf_op jit(solution)/shard_map/all_gather | solution.py:348
  16.4 155.4 %all-to-all-start = ((bf16[8,256,768]{1,2,0:T(8,128)(2,1)}), bf16[8,256,768]{1,2,0:T(8,128)(2,1)}, u32[]{:S(2)}, u32[]{:S(2)}) async-start(bf16[8,256,768]{1,2,0:T(8,128)(2,1)} %bitcast.74), calls=%async_computation | async-start | bytes 6291456 | tf_op jit(solution)/shard_map/all_to_all | solution.py:392
  23.9 383.8 %reduce-scatter.5.cloned.1.call-start = ((), (), s32[]{:S(2)}) async-start(), calls=%async_computation.7 | async-start | bytes 9437184 | tf_op jit(solution)/shard_map/reduce_scatter | solution.py:351
  24.0 31.6 %collective-permute-start.3 = (f32[4,2048]{1,0:T(4,128)S(1)}, f32[4,2048]{1,0:T(4,128)S(1)}, u32[]{:S(2)}, u32[]{:S(2)}) collective-permute-start(f32[4,2048]{1,0:T(4,128)S(1)} %constant_dynamic-update-slice_fusion.3), channel_id=1, source_target_pairs={{0,1},{1,0},{2,3},{3,2},{4,5},{5,4},{6,7},{7,6},{8,9},{9,8},{10,11... | collective-permute-start | bytes 98312 | tf_op jit(solution)/shard_map/ppermute | solution.py:48
  55.7 159.1 %collective-permute-start.4 = (f32[4,2048]{1,0:T(4,128)S(1)}, f32[4,2048]{1,0:T(4,128)S(1)}, u32[]{:S(2)}, u32[]{:S(2)}) collective-permute-start(f32[4,2048]{1,0:T(4,128)S(1)} %constant_dynamic-update-slice_fusion.2), channel_id=1, source_target_pairs={{0,2},{1,3},{2,0},{3,1},{4,6},{5,7},{6,4},{7,5},{8,10},{9,11},{10,... | collective-permute-start | bytes 98312 | tf_op jit(solution)/shard_map/ppermute | solution.py:48
  258.6 277.0 %all-gather.7.cloned.1.call-start = ((), (), s32[]{:S(2)}) async-start(), calls=%async_computation.8 | async-start | bytes 9437184 | tf_op jit(solution)/shard_map/all_gather | solution.py:360
  411.8 304.9 %reduce-scatter.7.cloned.1.call-start = ((), (), s32[]{:S(2)}) async-start(), calls=%async_computation.9 | async-start | bytes 9437184 | tf_op jit(solution)/shard_map/reduce_scatter | solution.py:363
  571.0 276.3 %all-gather.9.cloned.1.call-start = ((), (), s32[]{:S(2)}) async-start(), calls=%async_computation.10 | async-start | bytes 9437184 | tf_op jit(solution)/shard_map/all_gather | solution.py:360
  723.5 315.7 %reduce-scatter.9.cloned.1.call-start = ((), (), s32[]{:S(2)}) async-start(), calls=%async_computation.11 | async-start | bytes 9437184 | tf_op jit(solution)/shard_map/reduce_scatter | solution.py:363
  893.4 276.3 %all-gather.11.cloned.1.call-start = ((), (), s32[]{:S(2)}) async-start(), calls=%async_computation.12 | async-start | bytes 9437184 | tf_op jit(solution)/shard_map/all_gather | solution.py:348
  1251.1 132.2 %all-to-all-start.1 = ((bf16[8,256,768]{1,2,0:T(8,128)(2,1)}), bf16[8,256,768]{1,2,0:T(8,128)(2,1)}, u32[]{:S(2)}, u32[]{:S(2)}) async-start(bf16[8,256,768]{1,2,0:T(8,128)(2,1)} %bitcast.75), calls=%async_computation.5 | async-start | bytes 6291456 | tf_op jit(solution)/shard_map/all_to_all | solution.py:490
  1255.5 363.1 %reduce-scatter.11.cloned.1.call-start = ((), (), s32[]{:S(2)}) async-start(), calls=%async_computation.13 | async-start | bytes 9437184 | tf_op jit(solution)/shard_map/reduce_scatter | solution.py:351
  1278.8 117.6 %collective-permute-start.26 = (bf16[1024,1024]{1,0:T(8,128)(2,1)}, bf16[1024,1024]{1,0:T(8,128)(2,1)}, u32[]{:S(2)}, u32[]{:S(2)}) collective-permute-start(bf16[1024,1024]{1,0:T(8,128)(2,1)} %dynamic-slice_convert_fusion), channel_id=1, source_target_pairs={{0,8},{8,0},{16,24},{24,16},{1,9},{9,1},{17,25},{25,17},{2,10},{10... | collective-permute-start | bytes 6291464 | tf_op jit(solution)/shard_map/ppermute | solution.py:48
  1295.6 109.5 %collective-permute-start.22 = (bf16[1024,1024]{1,0:T(8,128)(2,1)}, bf16[1024,1024]{1,0:T(8,128)(2,1)}, u32[]{:S(2)}, u32[]{:S(2)}) collective-permute-start(bf16[1024,1024]{1,0:T(8,128)(2,1)} %dynamic-slice_convert_fusion.1), channel_id=1, source_target_pairs={{0,8},{8,0},{16,24},{24,16},{1,9},{9,1},{17,25},{25,17},{2,10},{10... | collective-permute-start | bytes 6291464 | tf_op jit(solution)/shard_map/ppermute | solution.py:48
  1313.6 97.1 %collective-permute-start.18 = (bf16[1024,1024]{1,0:T(8,128)(2,1)S(1)}, bf16[1024,1024]{1,0:T(8,128)(2,1)}, u32[]{:S(2)}, u32[]{:S(2)}) collective-permute-start(bf16[1024,1024]{1,0:T(8,128)(2,1)S(1)} %dynamic-slice_convert_fusion.2), channel_id=1, source_target_pairs={{0,8},{8,0},{16,24},{24,16},{1,9},{9,1},{17,25},{25,17},{2,10},{10... | collective-permute-start | bytes 6291464 | tf_op jit(solution)/shard_map/ppermute | solution.py:48
  1396.4 59.2 %collective-permute-start.9 = (bf16[512,2048]{1,0:T(8,128)(2,1)}, bf16[512,2048]{1,0:T(8,128)(2,1)}, u32[]{:S(2)}, u32[]{:S(2)}) collective-permute-start(bf16[512,2048]{1,0:T(8,128)(2,1)} %fusion.34), channel_id=1, source_target_pairs={{0,8},{8,0},{16,24},{24,16},{1,9},{9,1},{17,25},{25,17},{2,10},{10... | collective-permute-start | bytes 6291464 | tf_op jit(solution)/shard_map/ppermute | solution.py:48
  1401.3 28.1 %collective-permute-start.27 = (bf16[512,1024]{1,0:T(8,128)(2,1)}, bf16[512,1024]{1,0:T(8,128)(2,1)}, u32[]{:S(2)}, u32[]{:S(2)}) collective-permute-start(bf16[512,1024]{1,0:T(8,128)(2,1)} %dynamic-slice_convert_fusion.3), channel_id=1, source_target_pairs={{0,16},{8,24},{16,0},{24,8},{1,17},{9,25},{17,1},{25,9},{2,18},{10... | collective-permute-start | bytes 3145736 | tf_op jit(solution)/shard_map/ppermute | solution.py:48
  1410.2 41.7 %collective-permute-start.23 = (bf16[512,1024]{1,0:T(8,128)(2,1)}, bf16[512,1024]{1,0:T(8,128)(2,1)}, u32[]{:S(2)}, u32[]{:S(2)}) collective-permute-start(bf16[512,1024]{1,0:T(8,128)(2,1)} %dynamic-slice_convert_fusion.4), channel_id=1, source_target_pairs={{0,16},{8,24},{16,0},{24,8},{1,17},{9,25},{17,1},{25,9},{2,18},{10... | collective-permute-start | bytes 3145736 | tf_op jit(solution)/shard_map/ppermute | solution.py:48
  1414.6 59.7 %collective-permute-start.19 = (bf16[512,1024]{1,0:T(8,128)(2,1)S(1)}, bf16[512,1024]{1,0:T(8,128)(2,1)S(1)}, u32[]{:S(2)}, u32[]{:S(2)}) collective-permute-start(bf16[512,1024]{1,0:T(8,128)(2,1)S(1)} %dynamic-slice_convert_fusion.5), channel_id=1, source_target_pairs={{0,16},{8,24},{16,0},{24,8},{1,17},{9,25},{17,1},{25,9},{2,18},{10... | collective-permute-start | bytes 3145736 | tf_op jit(solution)/shard_map/ppermute | solution.py:48
  1431.0 65.8 %collective-permute-start.28 = (bf16[512,1024]{1,0:T(8,128)(2,1)S(1)}, bf16[512,1024]{1,0:T(8,128)(2,1)}, u32[]{:S(2)}, u32[]{:S(2)}) collective-permute-start(bf16[512,1024]{1,0:T(8,128)(2,1)S(1)} %add_convert_fusion.1), channel_id=1, source_target_pairs={{0,16},{8,24},{16,0},{24,8},{1,17},{9,25},{17,1},{25,9},{2,18},{10... | collective-permute-start | bytes 3145736 | tf_op jit(solution)/shard_map/ppermute | solution.py:48
  1453.5 65.8 %collective-permute-start.24 = (bf16[512,1024]{1,0:T(8,128)(2,1)S(1)}, bf16[512,1024]{1,0:T(8,128)(2,1)}, u32[]{:S(2)}, u32[]{:S(2)}) collective-permute-start(bf16[512,1024]{1,0:T(8,128)(2,1)S(1)} %add_convert_fusion.2), channel_id=1, source_target_pairs={{0,16},{8,24},{16,0},{24,8},{1,17},{9,25},{17,1},{25,9},{2,18},{10... | collective-permute-start | bytes 3145736 | tf_op jit(solution)/shard_map/ppermute | solution.py:48
  1462.3 79.5 %collective-permute-start.10 = (bf16[256,2048]{1,0:T(8,128)(2,1)}, bf16[256,2048]{1,0:T(8,128)(2,1)}, u32[]{:S(2)}, u32[]{:S(2)}) collective-permute-start(bf16[256,2048]{1,0:T(8,128)(2,1)} %dynamic-slice_convert_fusion.6), channel_id=1, source_target_pairs={{0,16},{8,24},{16,0},{24,8},{1,17},{9,25},{17,1},{25,9},{2,18},{10... | collective-permute-start | bytes 3145736 | tf_op jit(solution)/shard_map/ppermute | solution.py:48
  1475.6 88.7 %collective-permute-start.20 = (bf16[512,1024]{1,0:T(8,128)(2,1)}, bf16[512,1024]{1,0:T(8,128)(2,1)}, u32[]{:S(2)}, u32[]{:S(2)}) collective-permute-start(bf16[512,1024]{1,0:T(8,128)(2,1)} %add_convert_fusion.3), channel_id=1, source_target_pairs={{0,16},{8,24},{16,0},{24,8},{1,17},{9,25},{17,1},{25,9},{2,18},{10... | collective-permute-start | bytes 3145736 | tf_op jit(solution)/shard_map/ppermute | solution.py:48
  1500.8 88.0 %collective-permute-start.29 = (bf16[1024,1024]{1,0:T(8,128)(2,1)}, bf16[1024,1024]{1,0:T(8,128)(2,1)}, u32[]{:S(2)}, u32[]{:S(2)}) collective-permute-start(bf16[1024,1024]{1,0:T(8,128)(2,1)} %maximum_select_fusion.7), channel_id=1, source_target_pairs={{0,8},{8,0},{16,24},{24,16},{1,9},{9,1},{17,25},{25,17},{2,10},{10... | collective-permute-start | bytes 6291464 | tf_op jit(solution)/shard_map/ppermute | solution.py:48
  1522.0 73.6 %collective-permute-start.25 = (bf16[1024,1024]{1,0:T(8,128)(2,1)S(1)}, bf16[1024,1024]{1,0:T(8,128)(2,1)}, u32[]{:S(2)}, u32[]{:S(2)}) collective-permute-start(bf16[1024,1024]{1,0:T(8,128)(2,1)S(1)} %maximum_select_fusion.6), channel_id=1, source_target_pairs={{0,8},{8,0},{16,24},{24,16},{1,9},{9,1},{17,25},{25,17},{2,10},{10... | collective-permute-start | bytes 6291464 | tf_op jit(solution)/shard_map/ppermute | solution.py:48
  1543.3 42.9 %collective-permute-start.11 = (bf16[256,2048]{1,0:T(8,128)(2,1)S(1)}, bf16[256,2048]{1,0:T(8,128)(2,1)S(1)}, u32[]{:S(2)}, u32[]{:S(2)}) collective-permute-start(bf16[256,2048]{1,0:T(8,128)(2,1)S(1)} %add_convert_fusion.4), channel_id=1, source_target_pairs={{0,16},{8,24},{16,0},{24,8},{1,17},{9,25},{17,1},{25,9},{2,18},{10... | collective-permute-start | bytes 3145736 | tf_op jit(solution)/shard_map/ppermute | solution.py:48
  1569.0 34.2 %collective-permute-start.21 = (bf16[1024,1024]{1,0:T(8,128)(2,1)}, bf16[1024,1024]{1,0:T(8,128)(2,1)}, u32[]{:S(2)}, u32[]{:S(2)}) collective-permute-start(bf16[1024,1024]{1,0:T(8,128)(2,1)} %maximum_select_fusion.5), channel_id=1, source_target_pairs={{0,8},{8,0},{16,24},{24,16},{1,9},{9,1},{17,25},{25,17},{2,10},{10... | collective-permute-start | bytes 6291464 | tf_op jit(solution)/shard_map/ppermute | solution.py:48
  1573.7 14.9 collective-permute-start.14
  1588.6 21.7 %collective-permute-start.12 = (bf16[512,2048]{1,0:T(8,128)(2,1)}, bf16[512,2048]{1,0:T(8,128)(2,1)}, u32[]{:S(2)}, u32[]{:S(2)}) collective-permute-start(bf16[512,2048]{1,0:T(8,128)(2,1)} %maximum_select_fusion.4), channel_id=1, source_target_pairs={{0,8},{8,0},{16,24},{24,16},{1,9},{9,1},{17,25},{25,17},{2,10},{10... | collective-permute-start | bytes 6291464 | tf_op jit(solution)/shard_map/ppermute | solution.py:48
  1588.6 6.4 collective-permute-start.15
  1595.1 6.4 collective-permute-start.16
  1601.4 8.2 collective-permute-start.17
  (58 other events, 1366.4 us)
Sparse Core Ops, SparseCore 0:
  10.1 187.4 all-gather.4
  258.7 148.9 reduce-scatter.4
  412.0 123.5 all-gather.6
  571.1 145.5 reduce-scatter.6
  723.6 123.5 all-gather.8
  893.5 145.6 reduce-scatter.8
  1046.1 123.5 all-gather.10
  1260.0 204.2 reduce-scatter.10

commit v2 on v1

--- a/solution.py
+++ b/solution.py
@@ -1,5 +1,3 @@
-import functools
-
 import jax
 import jax.numpy as jnp
 from jax import lax
@@ -48,6 +46,10 @@
     return lax.ppermute(block, axis, [(i, i ^ bit) for i in range(size)])
 
 
+def after(block, *others):
+    return lax.optimization_barrier((block,) + others)[0]
+
+
 def xor_sum(block, axis, size):
     bit = 1
     while bit < size:
@@ -56,29 +58,27 @@
     return block
 
 
-def rep_sum(block):
-    size = lax.axis_size("rep")
+def replica_bits():
     me = lax.axis_index("rep")
-    bits = []
-    bit = 1
-    while bit < size:
-        bits.append(bit)
-        bit *= 2
-    for bit in bits:
-        half = block.shape[0] // 2
-        side = (me // bit) % 2
-        keep = lax.dynamic_slice_in_dim(block, side * half, half, 0)
-        send = lax.dynamic_slice_in_dim(block, (1 - side) * half, half, 0)
-        got = swapped(send.astype(bf16), "rep", bit)
-        block = keep.astype(f32) + got.astype(f32)
-    block = block.astype(bf16)
-    for bit in reversed(bits):
-        side = (me // bit) % 2
-        got = swapped(block, "rep", bit)
-        block = jnp.where(
-            side == 0, jnp.concatenate([block, got]), jnp.concatenate([got, block])
-        )
-    return block.astype(f32)
+    return (me & 1) == 1, (me & 2) == 2
+
+
+def shared(piece):
+    far = swapped(piece, "rep", 2)
+    near = swapped(piece, "rep", 1)
+    return [piece, near, far, swapped(far, "rep", 1)]
+
+
+def in_order(slots):
+    odd, high = replica_bits()
+    paired = [jnp.where(odd, slots[v ^ 1], slots[v]) for v in range(4)]
+    return [jnp.where(high, paired[q ^ 2], paired[q]) for q in range(4)]
+
+
+def own_part(block, count, which, axis):
+    size = block.shape[axis] // count
+    start = (lax.axis_index("rep") ^ which) * size
+    return lax.dynamic_slice_in_dim(block, start, size, axis)
 
 
 def piece_label(places, starts_ref):
@@ -333,16 +333,19 @@
 ):
     own_rows, model_width = tokens.shape
     group = lax.axis_size("fsdp")
+    assert lax.axis_size("rep") == 4 and group % 4 == 0
     me = lax.axis_index("fsdp")
     chain = SEQ // own_rows
     spot = me % chain
     width = model_width // chain
     shard = model_width // group
+    part = shard // 4
     sequence = ((lax.axis_index("rep") * group + me) * own_rows) // SEQ
     starts = lax.dynamic_index_in_dim(piece_starts, sequence, 0, keepdims=False)
     teams = None
     if group != chain:
         teams = [[b * chain + i for i in range(chain)] for b in range(group // chain)]
+    strides = [[r + 4 * m for m in range(group // 4)] for r in range(4)]
 
     def of_sequence(block):
         return lax.all_gather(block, "fsdp", axis=0, tiled=True, axis_index_groups=teams)
@@ -356,20 +359,86 @@
             axis_index_groups=teams,
         ).astype(f32)
 
-    def of_group(block):
-        return lax.all_gather(block, "fsdp", axis=0, tiled=True)
-
     def to_group_rows(block):
         return lax.psum_scatter(
             block.astype(bf16), "fsdp", scatter_dimension=0, tiled=True
         ).astype(f32)
 
-    def placed(block, start, length, axis):
-        shape = list(block.shape)
-        shape[axis] = length
-        return lax.dynamic_update_slice_in_dim(
-            jnp.zeros(shape, block.dtype), block, start, axis
+    def exchanged(block):
+        return lax.all_to_all(block, "fsdp", 0, 0, axis_index_groups=teams)
+
+    def of_quad(block):
+        half = block.shape[0] // 2
+        along_y = swapped(block, "fsdp", 1)
+        along_z = swapped(block, "fsdp", 2)
+        top = swapped(along_y[:half], "fsdp", 2)
+        bottom = swapped(along_z[half:], "fsdp", 1)
+        return jnp.concatenate([block, along_y, along_z, top, bottom])
+
+    def to_quad_rows(terms, fill=None):
+        half = own_rows // 2
+        across_rows = terms(3 * own_rows, 4 * own_rows).astype(bf16)
+        top = swapped(across_rows[:half], "fsdp", 2)
+        bottom = swapped(across_rows[half:], "fsdp", 1)
+        middle = terms(own_rows, 3 * own_rows)
+        y_rows = jnp.concatenate(
+            [middle[:half] + top.astype(f32), middle[half:own_rows]]
+        ).astype(bf16)
+        z_rows = jnp.concatenate(
+            [
+                middle[own_rows : own_rows + half],
+                middle[own_rows + half :] + bottom.astype(f32),
+            ]
+        ).astype(bf16)
+        from_y = swapped(y_rows, "fsdp", 1)
+        from_z = swapped(z_rows, "fsdp", 2)
+        own = terms(0, own_rows, y_rows, z_rows)
+        if fill is not None:
+            from_y = after(from_y, *fill(own))
+        return own + from_y.astype(f32) + from_z.astype(f32)
+
+    def widened(weight, first, second):
+        if group != 8:
+            return lax.all_gather(
+                weight, "fsdp", axis=1, tiled=True, axis_index_groups=strides
+            )
+        theirs = swapped(after(own_part(weight, 4, 0, 1), first), "fsdp", 4)
+        theirs = shared(after(theirs, second))
+        blocks = []
+        for v in (0, 2, 1, 3):
+            blocks += [own_part(weight, 4, v, 1), theirs[v]]
+        return jnp.concatenate(blocks, axis=1)
+
+    def replica_columns(pieces):
+        size = pieces[0].shape[1]
+        whole = jnp.zeros((pieces[0].shape[0], 4 * size), f32)
+        for v, block in enumerate(pieces):
+            start = (lax.axis_index("rep") ^ v) * size
+            whole = lax.dynamic_update_slice_in_dim(whole, block.astype(f32), start, 1)
+        return whole
+
+    def send_terms(rows, units):
+        return across(rows, units[:, units.shape[1] // 2 :]).astype(bf16)
+
+    def keep_terms(rows, units, near):
+        total = across(rows, units[:, : units.shape[1] // 2]) + near.astype(f32)
+        half = total.shape[1] // 2
+        return total[:, :half], total[:, half:].astype(bf16)
+
+    def to_partner(kept, far):
+        total = kept + far.astype(f32)
+        half = total.shape[1] // 2
+        return total[:, :half], total[:, half:].astype(bf16)
+
+    def narrowed_whole(rows, units):
+        total = lax.psum_scatter(
+            across(rows, units).astype(bf16),
+            "fsdp",
+            scatter_dimension=1,
+            tiled=True,
+            axis_index_groups=strides,
         )
+        return lax.psum(total, "rep").astype(f32)
 
     half = HEAD_DIM // 2
     frequency = rope_base ** (-(jnp.arange(half, dtype=f32) * (2.0 / HEAD_DIM)))
@@ -378,31 +447,31 @@
     cosine = jnp.concatenate([cosine, cosine], axis=1)
     sine = jnp.concatenate([-sine, sine], axis=1)
 
+    rows_weight = jnp.stack(
+        [own_part(w, 4, 0, 0) for w in (query_weight, key_weight, value_weight)], axis=1
+    )
+    rows_weight = rows_weight.reshape(part, 3, chain, width).transpose(2, 0, 1, 3)
+    rows_weight = rows_weight.reshape(chain, part, 3 * width)
+    if group != chain:
+        rows_weight = jnp.tile(rows_weight, (group // chain, 1, 1))
+    columns_weight = lax.all_to_all(rows_weight, "fsdp", 0, 0)
+    triple_weight = jnp.stack(in_order(shared(columns_weight)), axis=1).reshape(
+        model_width, 3 * width
+    )
+    all_tokens = of_sequence(tokens)
+
     own_gains = jnp.stack([query_norm, key_norm, mixer_norm, feeder_norm]).astype(f32)
-    gains = xor_sum(placed(own_gains, me * shard, model_width, 1), "fsdp", group)
-    pair_gains = lax.dynamic_slice_in_dim(gains[:2], spot * width, width, 1)
+    gains = lax.dynamic_update_slice_in_dim(
+        jnp.zeros((4, model_width), f32), own_gains, me * shard, 1
+    )
+    gains = xor_sum(gains, "fsdp", group)
+    if group == chain:
+        pair_gains = own_gains[:2]
+    else:
+        pair_gains = lax.dynamic_slice_in_dim(gains[:2], spot * width, width, 1)
     mixer_gain = gains[2:3]
     feeder_gain = gains[3:4]
 
-    rows_weight = jnp.stack([query_weight, key_weight, value_weight], axis=1)
-    rows_weight = rows_weight.reshape(shard, 3, chain, width).transpose(2, 0, 1, 3)
-    rows_weight = rows_weight.reshape(chain, shard, 3 * width)
-    if group != chain:
-        rows_weight = jnp.tile(rows_weight, (group // chain, 1, 1))
-    triple_weight = lax.all_to_all(rows_weight, "fsdp", 0, 0).reshape(
-        model_width, 3 * width
-    )
-    if group == chain:
-        head_output = output_weight
-    else:
-        head_output = lax.dynamic_slice_in_dim(
-            lax.all_gather(output_weight, "fsdp", axis=0, tiled=True),
-            spot * width,
-            width,
-            0,
-        )
-
-    all_tokens = of_sequence(tokens)
     pre = matmul(all_tokens, triple_weight)
     query_pre, key_pre = pre[:, :width], pre[:, width : 2 * width]
     squares = jnp.stack(
@@ -412,44 +481,99 @@
     query_low, key_low, value_low = prep(
         pre, squares, pair_gains.reshape(1, 2 * width), cosine, sine
     )
+    output_piece = lax.all_gather(
+        after(own_part(output_weight, 4, 0, 1), all_tokens), "fsdp", axis=0, tiled=True
+    )
+    output_slots = shared(after(output_piece, query_low))
+    whole_output = jnp.concatenate([output_slots[v] for v in (0, 2, 1, 3)], axis=1)
+
     mixed_low, mixed, log_total = attend(starts, query_low, key_low, value_low)
-    branch_pre = to_sequence_rows(matmul(mixed_low, head_output))
+    mixed_rows = exchanged(mixed_low.reshape(chain, own_rows, width))
+    mixed_rows = mixed_rows.transpose(1, 0, 2).reshape(own_rows, model_width)
+    branch_near = matmul(mixed_rows, whole_output)
+    quarter = model_width // 4
+    branch_slots = [branch_near[:, i * quarter : (i + 1) * quarter] for i in (0, 2, 1, 3)]
+    branch_pre = jnp.concatenate(in_order(branch_slots), axis=1)
     branch_factor = inverse_rms(branch_pre)
     hidden = tokens.astype(f32) + branch_pre * branch_factor * mixer_gain
 
-    all_hidden = of_group(hidden.astype(bf16))
-    gate = matmul(all_hidden, gate_weight).astype(bf16)
-    up = matmul(all_hidden, up_weight).astype(bf16)
+    wide_gate = widened(gate_weight, columns_weight, mixed_low)
+    wide_up = widened(up_weight, all_tokens, mixed_rows)
+    wide_down = widened(down_weight, query_low, hidden)
+    all_hidden = of_quad(hidden.astype(bf16))
+    gate = matmul(all_hidden, wide_gate).astype(bf16)
+    up = matmul(all_hidden, wide_up).astype(bf16)
     gate_wide, up_wide = gate.astype(f32), up.astype(f32)
     sigmoid = jax.nn.sigmoid(gate_wide)
     inner = (gate_wide * sigmoid * up_wide).astype(bf16)
-    down_pre = to_group_rows(against(inner, down_weight))
+    def down_terms(low, high, *deps):
+        return against(after(inner[low:high], *deps), wide_down)
+
+    down_pre = to_quad_rows(down_terms)
     down_factor = inverse_rms(down_pre)
     result = (hidden + down_pre * down_factor * feeder_gain).astype(bf16)
 
     tangent = cotangent.astype(f32)
     feeder_part = jnp.sum(tangent * down_pre * down_factor, axis=0)
     down_grad = norm_backward(down_pre, down_factor, feeder_gain, tangent).astype(bf16)
-    all_down_grad = of_group(down_grad)
-    inner_grad = matmul(all_down_grad, down_weight)
+    all_down_grad = of_quad(down_grad)
+    inner_grad = matmul(all_down_grad, wide_down)
     gate_grad = (
         inner_grad * up_wide * sigmoid * (1.0 + gate_wide * (1.0 - sigmoid))
     ).astype(bf16)
     up_grad = (inner_grad * gate_wide * sigmoid).astype(bf16)
-    feed_back = to_group_rows(
-        against(gate_grad, gate_weight) + against(up_grad, up_weight)
-    )
+    stage = {}
+
+    def early_gradients(own):
+        if group != 8:
+            return ()
+        down_send = send_terms(all_down_grad, after(inner, own))
+        down_near = swapped(down_send, "rep", 1)
+        gate_send = send_terms(all_hidden, after(gate_grad, down_send))
+        stage["gate_near"] = swapped(gate_send, "rep", 1)
+        stage["down_kept"], down_pass = keep_terms(
+            all_down_grad, after(inner, gate_send), down_near
+        )
+        stage["down_far"] = swapped(down_pass, "rep", 2)
+        return (down_pass,)
+
+    def back_terms(low, high, *deps):
+        return against(after(gate_grad[low:high], *deps), wide_gate) + against(
+            after(up_grad[low:high], *deps), wide_up
+        )
+
+    feed_back = to_quad_rows(back_terms, early_gradients)
     hidden_grad = tangent + feed_back
     mixer_part = jnp.sum(hidden_grad * branch_pre * branch_factor, axis=0)
     branch_grad = norm_backward(
         branch_pre, branch_factor, mixer_gain, hidden_grad
     ).astype(bf16)
-    gradient_down = rep_sum(across(all_down_grad, inner))
-    gradient_gate = rep_sum(across(all_hidden, gate_grad))
-    gradient_up = rep_sum(across(all_hidden, up_grad))
-
-    all_branch_grad = of_sequence(branch_grad)
-    mixed_grad = against(all_branch_grad, head_output).astype(bf16)
+
+    grad_near = jnp.concatenate(
+        [own_part(branch_grad, 4, v, 1) for v in (0, 2, 1, 3)], axis=1
+    )
+    mixed_grad_rows = against(grad_near, whole_output).astype(bf16)
+    mixed_grad = exchanged(
+        mixed_grad_rows.reshape(own_rows, chain, width).transpose(1, 0, 2)
+    ).reshape(chain * own_rows, width)
+    output_half = model_width // 2
+    late_rows = after(mixed_rows, mixed_grad_rows)
+    output_send = across(late_rows, grad_near[:, output_half:]).astype(bf16)
+    output_near = swapped(output_send, "rep", 1)
+    if group == 8:
+        gate_kept, gate_pass = keep_terms(
+            all_hidden, after(gate_grad, output_send), stage["gate_near"]
+        )
+        late_rows = after(mixed_rows, gate_pass)
+    output_kept = across(late_rows, grad_near[:, :output_half]) + output_near.astype(f32)
+    output_pass = output_kept[:, quarter:].astype(bf16)
+    output_kept = output_kept[:, :quarter]
+    output_far = swapped(output_pass, "rep", 2)
+    if group == 8:
+        gate_far = swapped(after(gate_pass, output_pass), "rep", 2)
+        up_send = send_terms(all_hidden, after(up_grad, output_pass))
+        up_near = swapped(up_send, "rep", 1)
+        mixed_grad = after(mixed_grad, up_send)
     query_turn, key_turn, value_grad = attend_back(
         starts,
         query_low,
@@ -468,6 +592,12 @@
             jnp.sum(key_gain * key_turn * key_pre, axis=1),
         ]
     )
+    if group == 8:
+        down_kept, down_pass = to_partner(
+            stage["down_kept"], after(stage["down_far"], value_grad)
+        )
+        down_theirs = swapped(down_pass, "fsdp", 4)
+        means = after(means, down_pass)
     means = xor_sum(means, "fsdp", chain) * (1.0 / model_width)
     factors = lax.rsqrt(squares * (1.0 / model_width) + norm_epsilon)
 
@@ -479,29 +609,73 @@
     query_grad, query_part = pair_back(query_turn, query_pre, query_gain, 0)
     key_grad, key_part = pair_back(key_turn, key_pre, key_gain, 1)
     triple_grad = jnp.concatenate([query_grad, key_grad, value_grad], axis=1)
-    gradient_tokens = (
-        hidden_grad + to_sequence_rows(against(triple_grad, triple_weight))
-    ).astype(bf16)
-
-    output_part = across(mixed_low, all_branch_grad)
-    triple_part = across(all_tokens, triple_grad)
+    output_part = (output_kept + after(output_far, triple_grad).astype(f32)).astype(bf16)
+    token_terms = against(triple_grad, triple_weight).astype(bf16)
+    output_part = to_group_rows(output_part)
+    token_rows = to_sequence_rows(token_terms)
+    gradient_tokens = (hidden_grad + token_rows).astype(bf16)
+
+    triple_part = across(all_tokens, after(triple_grad, token_terms))
     if group == chain:
-        output_rows = output_part
-        triple_rows = lax.all_to_all(
-            triple_part.astype(bf16).reshape(chain, shard, 3 * width), "fsdp", 0, 0
+        triple_part = triple_part.reshape(chain, 4, part, 3 * width)
+        slots = [own_part(triple_part, 4, v, 1)[:, 0] for v in range(4)]
+        sends = [slots[v].astype(bf16) for v in (3, 1)]
+        near = [swapped(x, "rep", 1) for x in sends]
+        if group == 8:
+            up_kept, up_pass = keep_terms(all_hidden, after(up_grad, *sends), up_near)
+            up_far = swapped(up_pass, "rep", 2)
+            near = [after(x, up_pass) for x in near]
+        passed = (slots[2] + near[0].astype(f32)).astype(bf16)
+        kept = slots[0] + near[1].astype(f32)
+        passed_far = swapped(passed, "rep", 2)
+        if group == 8:
+            gate_kept, gate_pass = to_partner(gate_kept, after(gate_far, passed))
+            gate_theirs = swapped(gate_pass, "fsdp", 4)
+            down_theirs = after(down_theirs, gate_pass)
+            down_total = (down_kept + down_theirs.astype(f32)).astype(bf16)
+            down_pieces = shared(down_total)
+            passed_far = after(passed_far, down_total)
+        kept = (kept + passed_far.astype(f32)).astype(bf16)
+        heads_rows = lax.all_to_all(kept, "fsdp", 0, 0)
+        if group == 8:
+            up_kept, up_pass = to_partner(up_kept, after(up_far, kept))
+            up_theirs = swapped(up_pass, "fsdp", 4)
+            output_part = after(output_part, up_pass)
+        output_total = output_part.astype(bf16)
+        output_pieces = shared(output_total)
+        if group == 8:
+            gate_theirs = after(gate_theirs, output_total)
+            gate_total = (gate_kept + gate_theirs.astype(f32)).astype(bf16)
+            gate_pieces = shared(gate_total)
+            heads_rows = after(heads_rows, gate_total)
+        triple_pieces = shared(heads_rows)
+        if group == 8:
+            up_theirs = after(up_theirs, heads_rows)
+            up_total = (up_kept + up_theirs.astype(f32)).astype(bf16)
+            up_pieces = shared(up_total)
+            gradient_down = replica_columns(down_pieces)
+            gradient_gate = replica_columns(gate_pieces)
+            gradient_up = replica_columns(up_pieces)
+        gradient_output = replica_columns(output_pieces)
+        triple_rows = jnp.stack(in_order(triple_pieces))
+        triple_rows = triple_rows.reshape(4, chain, part, 3, width)
+        triple_rows = triple_rows.transpose(3, 0, 2, 1, 4).reshape(3, shard, model_width)
+    else:
+        gradient_output = replica_columns(shared(output_part.astype(bf16)))
+        triple_rows = lax.dynamic_update_slice_in_dim(
+            jnp.zeros((model_width, 3, chain, width), f32),
+            triple_part.reshape(model_width, 3, 1, width),
+            spot,
+            2,
         )
-        triple_rows = triple_rows.reshape(chain, shard, 3, width).transpose(2, 1, 0, 3)
-    else:
-        output_rows = to_group_rows(placed(output_part, spot * width, model_width, 0))
-        triple_rows = to_group_rows(
-            placed(
-                triple_part.reshape(model_width, 3, 1, width), spot, chain, 2
-            ).reshape(model_width, 3 * model_width)
-        )
-        triple_rows = triple_rows.reshape(shard, 3, chain, width).transpose(1, 0, 2, 3)
-    triple_rows = triple_rows.reshape(3 * shard, model_width)
-    triple_rows = jnp.concatenate([triple_rows.astype(bf16), output_rows.astype(bf16)])
-    four = rep_sum(triple_rows)
+        triple_rows = to_group_rows(triple_rows.reshape(model_width, 3 * model_width))
+        triple_rows = lax.psum(triple_rows.astype(bf16), "rep")
+        triple_rows = triple_rows.reshape(shard, 3, model_width).transpose(1, 0, 2)
+    if group != 8:
+        gradient_down = narrowed_whole(all_down_grad, inner)
+        gradient_gate = narrowed_whole(all_hidden, gate_grad)
+        gradient_up = narrowed_whole(all_hidden, up_grad)
+    triple_rows = triple_rows.astype(f32)
 
     gain_parts = jnp.stack(
         [
@@ -515,17 +689,17 @@
             feeder_part,
         ]
     )
-    gain_parts = xor_sum(xor_sum(gain_parts, "fsdp", group), "rep", lax.axis_size("rep"))
+    gain_parts = xor_sum(xor_sum(gain_parts, "fsdp", group), "rep", 4)
     gain_own = lax.dynamic_slice_in_dim(gain_parts, me * shard, shard, 1)
     return (
         result,
         gradient_tokens,
-        four[:shard],
-        four[shard : 2 * shard],
-        four[2 * shard : 3 * shard],
+        triple_rows[0],
+        triple_rows[1],
+        triple_rows[2],
         gain_own[0],
         gain_own[1],
-        four[3 * shard :],
+        gradient_output,
         gain_own[2],
         gradient_gate,
         gradient_up,

time: 1640 us -> 1140 us (0.70)
  waiting for transfers between devices: 1190 us -> 511 us
  local copies, waits for them, and re-layouts: 54.4 us -> 145 us
  blocking collectives: 0 us -> 45.9 us
  starting transfers between devices: 44.1 us -> 75.4 us
  matrix products: 167 us -> 194 us
    reduce_scatter x2 -> x1, waiting for transfers between devices: 291 us -> 0.01 us  [to_group_rows(): lax.psum_scatter(block.astype(bf16), 'fsdp', scatter_dimension=0, tiled=T...]
    ppermute x30 -> x77, waiting for transfers between devices: 178 us -> 427 us  [swapped(): return lax.ppermute(block, axis, [(i, i ^ bit) for i in range(size)])]
    all_gather x2 -> x1, waiting for transfers between devices: 247 us -> 0.02 us  [body(): lax.all_gather(after(own_part(output_weight, 4, 0, 1), all_tokens), 'fsdp...]
    all_to_all x2 -> x3, waiting for transfers between devices: 178 us -> 13.4 us  [the longest x1 13.4 us: body(): heads_rows = lax.all_to_all(kept, 'fsdp', 0, 0)]
    reduce_scatter x2 -> x1, waiting for transfers between devices: 149 us -> 0.01 us  [to_sequence_rows(): lax.psum_scatter(block.astype(bf16), 'fsdp', scatter_dimension=0, tiled=T...]
    all_gather x2 -> x1, waiting for transfers between devices: 144 us -> 70.2 us  [of_sequence(): lax.all_gather(block, 'fsdp', axis=0, tiled=True, axis_index_groups=teams)]
    all_to_all x0 -> x1, blocking collectives: none -> 45.9 us  [body(): columns_weight = lax.all_to_all(rows_weight, 'fsdp', 0, 0)]
    unnamed x106 -> x197, local copies, waits for them, and re-layouts: 29.1 us -> 69.9 us
  transfers between devices with their start and end apart: 40 -> 84, of which waited for: 24 -> 36; matrix products, arithmetic and copies ran while one was open for 10% -> 29% of each run, Pallas kernels for 0% -> 5%
where the time goes in v2:
time: 1140 us; the launch traced here: 1130 us
  waiting for transfers between devices  511 us (45%)
  matrix products  194 us (17%)
  local copies, waits for them, and re-layouts  145 us (13%)
  other arithmetic  87.6 us (8%)
  starting transfers between devices  75.4 us (7%)
  Pallas kernels  57.4 us (5%)
  blocking collectives  45.9 us (4%)
  between operations  16 us (1%)
    ppermute x77, waiting for transfers between devices, swapped(): return lax.ppermute(block, axis, [(i, i ^ bit) for i in range(size)])  427 us
    dot_general x11, matrix products, against(): lax.dot_general(a, b, (((1,), (1,)), ((), ())), preferred_element_type=f32)  72.7 us
    all_gather x1, waiting for transfers between devices, of_sequence(): lax.all_gather(block, 'fsdp', axis=0, tiled=True, axis_index_groups=teams)  70.2 us
    unnamed x197, local copies, waits for them, and re-layouts  69.9 us
    dot_general x9, matrix products, across(): lax.dot_general(a, b, (((0,), (0,)), ((), ())), preferred_element_type=f32)  67.5 us
    ppermute x77, starting transfers between devices, swapped(): return lax.ppermute(block, axis, [(i, i ^ bit) for i in range(size)])  63.3 us
    dot_general x5, matrix products, matmul(): return jnp.dot(a, b, preferred_element_type=f32)  53.5 us
    all_to_all x1, blocking collectives, body(): columns_weight = lax.all_to_all(rows_weight, 'fsdp', 0, 0)  45.9 us
  transfers between devices with their start and end apart: 84, of which 36 were waited for; matrix products, arithmetic and copies ran while one was open for 29% of the time, Pallas kernels for 5%

profile of v2, /device:TPU:0, one launch (start us, length us, event | category | flops | bytes accessed | tf_op | source)
XLA Modules:
  0.0 1132.1 jit_solution(1745034478632265370)
XLA Ops:
  11.1 45.9 %all_to_all.20 = bf16[8,64,768]{2,1,0:T(8,128)(2,1)S(1)} all-to-all(bf16[8,64,768]{2,1,0:T(8,128)(2,1)S(1)} %reshape.130), channel_id=1, replica_groups=mesh['rep'=4,'fsdp'=8] {'fsdp'}, dimensions={0} | all-to-all | bytes 1572864 | tf_op jit(solution)/shard_map/all_to_all | solution.py:457
  80.0 70.2 %all-gather.3.cloned.1.call-done = bf16[2048,2048]{1,0:T(8,128)(2,1)} async-done(((bf16[256,2048]{1,0:T(8,128)(2,1)}), bf16[2048,2048]{1,0:T(8,128)(2,1)}) %all-gather.3.cloned.1.call-update) | async-done | bytes 8388624 | tf_op jit(solution)/shard_map/all_gather | solution.py:351
  150.3 10.0 convolution_bitcast_fusion.pre_ref
  173.6 61.6 %collective-permute-done.5 = f32[2,2048]{1,0:T(2,128)S(1)} collective-permute-done((f32[2,2048]{1,0:T(2,128)S(1)}, f32[2,2048]{1,0:T(2,128)S(1)}, u32[]{:S(2)}, u32[]{:S(2)}) %collective-permute-start.5) | collective-permute-done | bytes 16416 | tf_op jit(solution)/shard_map/ppermute | solution.py:46
  242.2 19.6 %attend.1 = (bf16[2048,256]{1,0:T(8,128)(2,1)}, f32[2048,256]{1,0:T(8,128)}, f32[2048,256]{1,0:T(8,128)}) custom-call(s32[2]{0:T(128)} %fusion.57.starts_ref, bf16[2048,256]{1,0:T(8,128)(2,1)} %get-tuple-element.58.q_ref, bf16[2048,256]{1,0:T(8,128)(2,1)} %get-tuple-element.59.k_ref, bf16[2048,256]{1,0:T(8,128)(2,1)} %get-tuple-element.60.v_ref), custom_call_target="tpu_custom_call" | custom-call | flops 2147483648 | bytes 8388608 | tf_op jit(solution)/shard_map/attend/pallas_call | solution.py:199
  272.8 14.9 %collective-permute-done.10 = f32[4,2048]{1,0:T(4,128)S(1)} collective-permute-done((f32[4,2048]{1,0:T(4,128)S(1)}, f32[4,2048]{1,0:T(4,128)S(1)}, u32[]{:S(2)}, u32[]{:S(2)}) %collective-permute-start.10) | collective-permute-done | bytes 32800 | tf_op jit(solution)/shard_map/ppermute | solution.py:46
  304.3 35.1 %collective-permute-done.17 = bf16[2048,256]{1,0:T(8,128)(2,1)} collective-permute-done((bf16[2048,256]{1,0:T(8,128)(2,1)}, bf16[2048,256]{1,0:T(8,128)(2,1)}, u32[]{:S(2)}, u32[]{:S(2)}) %collective-permute-start.17) | collective-permute-done | bytes 1048608 | tf_op jit(solution)/shard_map/ppermute | solution.py:46
  343.9 23.5 %collective-permute-done.20 = bf16[2048,256]{1,0:T(8,128)(2,1)} collective-permute-done((bf16[2048,256]{1,0:T(8,128)(2,1)}, bf16[2048,256]{1,0:T(8,128)(2,1)}, u32[]{:S(2)}, u32[]{:S(2)}) %collective-permute-start.20) | collective-permute-done | bytes 1048608 | tf_op jit(solution)/shard_map/ppermute | solution.py:46
  379.2 13.5 %collective-permute-done.21 = bf16[2048,256]{1,0:T(8,128)(2,1)S(1)} collective-permute-done((bf16[2048,256]{1,0:T(8,128)(2,1)}, bf16[2048,256]{1,0:T(8,128)(2,1)S(1)}, u32[]{:S(2)}, u32[]{:S(2)}) %collective-permute-start.21) | collective-permute-done | bytes 1048608 | tf_op jit(solution)/shard_map/ppermute | solution.py:46
  410.8 17.7 %collective-permute-done.12 = bf16[256,2048]{1,0:T(8,128)(2,1)S(1)} collective-permute-done((bf16[256,2048]{1,0:T(8,128)(2,1)S(1)}, bf16[256,2048]{1,0:T(8,128)(2,1)S(1)}, u32[]{:S(2)}, u32[]{:S(2)}) %collective-permute-start.12) | collective-permute-done | bytes 1048608 | tf_op jit(solution)/shard_map/ppermute | solution.py:46
  434.7 9.5 collective-permute-done.14
  446.7 9.2 convolution_convert_fusion.3
  455.9 15.1 %fusion = (bf16[1024,2048]{1,0:T(8,128)(2,1)S(1)}, bf16[1024,2048]{1,0:T(8,128)(2,1)}) fusion(bf16[1024,2048]{1,0:T(8,128)(2,1)S(1)} %convolution_convert_fusion.3, bf16[1024,2048]{1,0:T(8,128)(2,1)S(1)} %constant_dynamic-update-slice_fusion.4, bf16[2048,2048]{1,0:T(8,128)(2,1)} %constant_dynamic-update-slice_fusion.14), kind=kOutput, calls=%fused_computation.6 | convolution fusion | flops 8608808960 | bytes 25165824 | tf_op jit(solution)/shard_map/dot_general | solution.py:23
  494.0 20.7 %collective-permute-done.30 = bf16[256,2048]{1,0:T(8,128)(2,1)S(1)} collective-permute-done((bf16[256,2048]{1,0:T(8,128)(2,1)S(1)}, bf16[256,2048]{1,0:T(8,128)(2,1)S(1)}, u32[]{:S(2)}, u32[]{:S(2)}) %collective-permute-start.30) | collective-permute-done | bytes 1048608 | tf_op jit(solution)/shard_map/ppermute | solution.py:46
  526.7 20.4 %collective-permute-done.32 = bf16[256,2048]{1,0:T(8,128)(2,1)S(1)} collective-permute-done((bf16[256,2048]{1,0:T(8,128)(2,1)S(1)}, bf16[256,2048]{1,0:T(8,128)(2,1)S(1)}, u32[]{:S(2)}, u32[]{:S(2)}) %collective-permute-start.32) | collective-permute-done | bytes 1048608 | tf_op jit(solution)/shard_map/ppermute | solution.py:46
  559.5 16.8 %fusion.3 = (bf16[1024,2048]{1,0:T(8,128)(2,1)S(1)}, bf16[1024,2048]{1,0:T(8,128)(2,1)S(1)}) fusion(bf16[1024,2048]{1,0:T(8,128)(2,1)} %get-tuple-element.199, bf16[1024,2048]{1,0:T(8,128)(2,1)} %copy-done.67, bf16[1024,2048]{1,0:T(8,128)(2,1)S(1)} %constant_dynamic-update-slice_fusion.24, bf16[2048,2048]{1,0:T(8,128)(2,1)} %constant_dynamic-update-slice_fusion.19), kind=kOutput, calls=%fused_computation.9 | convolution fusion | flops 8621391872 | bytes 29360128 | tf_op jit(solution)/shard_map/dot_general | solution.py:23
  592.5 9.4 fusion.83
  601.9 9.3 fusion.81
  633.2 9.5 convolution_convert_fusion.5
  642.8 8.8 convert_add_fusion.3
  672.5 8.8 convert_add_fusion.2
  701.9 31.4 %attend_back.1 = (f32[2048,256]{1,0:T(8,128)}, f32[2048,256]{1,0:T(8,128)}, bf16[2048,256]{1,0:T(8,128)(2,1)}) custom-call(s32[2]{0:T(128)} %fusion.57.starts_ref, bf16[2048,256]{1,0:T(8,128)(2,1)} %get-tuple-element.58.q_ref, bf16[2048,256]{1,0:T(8,128)(2,1)} %bitcast.18.grad_ref, f32[2048,256]{1,0:T(8,128)} %get-tuple-element.82.mixed_ref, ...), custom_call_target="tpu_custom_call" | custom-call | flops 5368709120 | bytes 14680064 | tf_op jit(solution)/shard_map/attend_back/pallas_call | solution.py:295
  764.1 11.4 %convolution_convert_fusion = bf16[2048,2048]{1,0:T(8,128)(2,1)} fusion(bf16[2048,768]{1,0:T(8,128)(2,1)} %bitcast.152, bf16[2048,256]{1,0:T(8,128)(2,1)} %get-tuple-element.86, bf16[2048,256]{1,0:T(8,128)(2,1)} %copy-done.39, bf16[2048,256]{1,0:T(8,128)(2,1)S(1)} %get-tuple-element.142), kind=kOutput, calls=%fused_computation.21 | convolution fusion | flops 6456082432 | bytes 14680064 | tf_op jit(solution)/shard_map/dot_general | solution.py:27
  787.9 11.8 %convolution_bitcast_fusion.1 = f32[2048,768]{0,1:T(8,128)} fusion(bf16[2048,768]{1,0:T(8,128)(2,1)} %pad_maximum_fusion.1, bf16[2048,2048]{1,0:T(8,128)(2,1)} %all-gather.3.cloned.1.call-done), kind=kOutput, calls=%fused_computation.32 | convolution fusion | flops 6442450944 | bytes 17825792 | tf_op jit(solution)/shard_map/dot_general | solution.py:31
  806.5 35.2 %collective-permute-done.61 = f32[4,2048]{1,0:T(4,128)S(1)} collective-permute-done((f32[4,2048]{1,0:T(4,128)S(1)}, f32[4,2048]{1,0:T(4,128)S(1)}, u32[]{:S(2)}, u32[]{:S(2)}) %collective-permute-start.61) | collective-permute-done | bytes 32800 | tf_op jit(solution)/shard_map/ppermute | solution.py:46
  847.2 8.9 convert_add_fusion
  889.4 15.5 %collective-permute-done.75 = bf16[2048,256]{1,0:T(8,128)(2,1)} collective-permute-done((bf16[2048,256]{1,0:T(8,128)(2,1)}, bf16[2048,256]{1,0:T(8,128)(2,1)}, u32[]{:S(2)}, u32[]{:S(2)}) %collective-permute-start.75) | collective-permute-done | bytes 1048608 | tf_op jit(solution)/shard_map/ppermute | solution.py:46
  910.3 38.6 %collective-permute-done.55 = bf16[2048,512]{1,0:T(8,128)(2,1)} collective-permute-done((bf16[2048,512]{1,0:T(8,128)(2,1)}, bf16[2048,512]{1,0:T(8,128)(2,1)}, u32[]{:S(2)}, u32[]{:S(2)}) %collective-permute-start.55) | collective-permute-done | bytes 2097184 | tf_op jit(solution)/shard_map/ppermute | solution.py:46
  956.3 47.6 %collective-permute-done.53 = bf16[2048,256]{1,0:T(8,128)(2,1)} collective-permute-done((bf16[2048,256]{1,0:T(8,128)(2,1)}, bf16[2048,256]{1,0:T(8,128)(2,1)}, u32[]{:S(2)}, u32[]{:S(2)}) %collective-permute-start.53) | collective-permute-done | bytes 1048608 | tf_op jit(solution)/shard_map/ppermute | solution.py:46
  1014.4 13.4 %all-to-all-done.3 = bf16[8,64,768]{2,1,0:T(8,128)(2,1)S(1)} async-done(((bf16[8,64,768]{2,1,0:T(8,128)(2,1)}), bf16[8,64,768]{2,1,0:T(8,128)(2,1)S(1)}, u32[]{:S(2)}, u32[]{:S(2)}) %all-to-all-start.3) | async-done | bytes 786464 | tf_op jit(solution)/shard_map/all_to_all | solution.py:639
  1032.0 16.2 %collective-permute-done.56 = bf16[8,64,768]{2,1,0:T(8,128)(2,1)S(1)} collective-permute-done((bf16[8,64,768]{2,1,0:T(8,128)(2,1)S(1)}, bf16[8,64,768]{2,1,0:T(8,128)(2,1)S(1)}, u32[]{:S(2)}, u32[]{:S(2)}) %collective-permute-start.56) | collective-permute-done | bytes 786464 | tf_op jit(solution)/shard_map/ppermute | solution.py:46
  1062.3 8.5 collective-permute-done.68
  (509 shorter events, 427.8 us)
Async XLA Ops:
  7.2 143.0 %all-gather.3.cloned.1.call-start = ((), (), s32[]{:S(2)}) async-start(), calls=%async_computation.6 | async-start | bytes 9437184 | tf_op jit(solution)/shard_map/all_gather | solution.py:351
  7.9 259.9 %all-gather.5.cloned.1.call-start = ((), (), s32[]{:S(2)}) async-start(), calls=%async_computation.7 | async-start | bytes 2359296 | tf_op jit(solution)/shard_map/all_gather | solution.py:484
  58.6 212.1 %collective-permute-start.9 = (f32[4,2048]{1,0:T(4,128)S(1)}, f32[4,2048]{1,0:T(4,128)S(1)}, u32[]{:S(2)}, u32[]{:S(2)}) collective-permute-start(f32[4,2048]{1,0:T(4,128)S(1)} %constant_dynamic-update-slice_fusion.32), channel_id=1, source_target_pairs={{0,1},{1,0},{2,3},{3,2},{4,5},{5,4},{6,7},{7,6},{8,9},{9,8},{10,11... | collective-permute-start | bytes 98312 | tf_op jit(solution)/shard_map/ppermute | solution.py:46
  166.5 125.3 %collective-permute-start.16 = (bf16[2048,256]{1,0:T(8,128)(2,1)}, bf16[2048,256]{1,0:T(8,128)(2,1)}, u32[]{:S(2)}, u32[]{:S(2)}) collective-permute-start(bf16[2048,256]{1,0:T(8,128)(2,1)} %get-tuple-element.64), channel_id=1, source_target_pairs={{0,4},{1,5},{2,6},{3,7},{4,0},{5,1},{6,2},{7,3},{8,12},{9,13},{10,... | collective-permute-start | bytes 3145736 | tf_op jit(solution)/shard_map/ppermute | solution.py:46
  170.6 64.6 %collective-permute-start.5 = (f32[2,2048]{1,0:T(2,128)S(1)}, f32[2,2048]{1,0:T(2,128)S(1)}, u32[]{:S(2)}, u32[]{:S(2)}) collective-permute-start(f32[2,2048]{1,0:T(2,128)S(1)} %fusion.127), channel_id=1, source_target_pairs={{0,4},{1,5},{2,6},{3,7},{4,0},{5,1},{6,2},{7,3},{8,12},{9,13},{10,... | collective-permute-start | bytes 49160 | tf_op jit(solution)/shard_map/ppermute | solution.py:46
  264.0 103.4 %all-to-all-start.1 = ((bf16[8,256,256]{1,2,0:T(8,128)(2,1)}), bf16[8,256,256]{1,2,0:T(8,128)(2,1)S(1)}, u32[]{:S(2)}, u32[]{:S(2)}) async-start(bf16[8,256,256]{1,2,0:T(8,128)(2,1)} %copy.55), calls=%async_computation.1 | async-start | bytes 2097152 | tf_op jit(solution)/shard_map/all_to_all | solution.py:368
  267.8 102.7 %collective-permute-start.6 = (bf16[2048,512]{1,0:T(8,128)(2,1)}, bf16[2048,512]{1,0:T(8,128)(2,1)}, u32[]{:S(2)}, u32[]{:S(2)}) collective-permute-start(bf16[2048,512]{1,0:T(8,128)(2,1)} %all-gather.5.cloned.1.call-done), channel_id=1, source_target_pairs={{0,16},{8,24},{16,0},{24,8},{1,17},{9,25},{17,1},{25,9},{2,18},{10... | collective-permute-start | bytes 6291464 | tf_op jit(solution)/shard_map/ppermute | solution.py:46
  291.8 47.6 %collective-permute-start.17 = (bf16[2048,256]{1,0:T(8,128)(2,1)}, bf16[2048,256]{1,0:T(8,128)(2,1)}, u32[]{:S(2)}, u32[]{:S(2)}) collective-permute-start(bf16[2048,256]{1,0:T(8,128)(2,1)} %collective-permute-done.16), channel_id=1, source_target_pairs={{0,16},{8,24},{16,0},{24,8},{1,17},{9,25},{17,1},{25,9},{2,18},{10... | collective-permute-start | bytes 3145736 | tf_op jit(solution)/shard_map/ppermute | solution.py:46
  296.5 70.9 %collective-permute-start.20 = (bf16[2048,256]{1,0:T(8,128)(2,1)}, bf16[2048,256]{1,0:T(8,128)(2,1)}, u32[]{:S(2)}, u32[]{:S(2)}) collective-permute-start(bf16[2048,256]{1,0:T(8,128)(2,1)} %get-tuple-element.66), channel_id=1, source_target_pairs={{0,4},{1,5},{2,6},{3,7},{4,0},{5,1},{6,2},{7,3},{8,12},{9,13},{10,... | collective-permute-start | bytes 3145736 | tf_op jit(solution)/shard_map/ppermute | solution.py:46
  296.7 71.0 %collective-permute-start.18 = (bf16[2048,256]{1,0:T(8,128)(2,1)}, bf16[2048,256]{1,0:T(8,128)(2,1)}, u32[]{:S(2)}, u32[]{:S(2)}) collective-permute-start(bf16[2048,256]{1,0:T(8,128)(2,1)} %collective-permute-done.16), channel_id=1, source_target_pairs={{0,8},{8,0},{16,24},{24,16},{1,9},{9,1},{17,25},{25,17},{2,10},{10... | collective-permute-start | bytes 3145736 | tf_op jit(solution)/shard_map/ppermute | solution.py:46
  296.8 106.0 %collective-permute-start.24 = (bf16[2048,256]{1,0:T(8,128)(2,1)}, bf16[2048,256]{1,0:T(8,128)(2,1)}, u32[]{:S(2)}, u32[]{:S(2)}) collective-permute-start(bf16[2048,256]{1,0:T(8,128)(2,1)} %get-tuple-element.68), channel_id=1, source_target_pairs={{0,4},{1,5},{2,6},{3,7},{4,0},{5,1},{6,2},{7,3},{8,12},{9,13},{10,... | collective-permute-start | bytes 3145736 | tf_op jit(solution)/shard_map/ppermute | solution.py:46
  665.7 67.6 %collective-permute-start.43 = (bf16[2048,512]{1,0:T(8,128)(2,1)}, bf16[2048,512]{1,0:T(8,128)(2,1)}, u32[]{:S(2)}, u32[]{:S(2)}) collective-permute-start(bf16[2048,512]{1,0:T(8,128)(2,1)} %slice.447), channel_id=1, source_target_pairs={{0,16},{8,24},{16,0},{24,8},{1,17},{9,25},{17,1},{25,9},{2,18},{10... | collective-permute-start | bytes 6291464 | tf_op jit(solution)/shard_map/ppermute | solution.py:46
  672.4 283.2 %reduce-scatter.5.cloned.1.call-start = ((), (), s32[]{:S(2)}) async-start(), calls=%async_computation.9 | async-start | bytes 2359296 | tf_op jit(solution)/shard_map/reduce_scatter | solution.py:363
  694.1 65.7 %collective-permute-start.54 = (bf16[2048,512]{1,0:T(8,128)(2,1)}, bf16[2048,512]{1,0:T(8,128)(2,1)}, u32[]{:S(2)}, u32[]{:S(2)}) collective-permute-start(bf16[2048,512]{1,0:T(8,128)(2,1)} %slice.445), channel_id=1, source_target_pairs={{0,16},{8,24},{16,0},{24,8},{1,17},{9,25},{17,1},{25,9},{2,18},{10... | collective-permute-start | bytes 6291464 | tf_op jit(solution)/shard_map/ppermute | solution.py:46
  763.9 358.7 %reduce-scatter.3.cloned.1.call-start = ((), (), s32[]{:S(2)}) async-start(), calls=%async_computation.8 | async-start | bytes 9437184 | tf_op jit(solution)/shard_map/reduce_scatter | solution.py:354
  763.9 81.6 %collective-permute-start.48 = (bf16[2048,1024]{1,0:T(8,128)(2,1)}, bf16[2048,1024]{1,0:T(8,128)(2,1)}, u32[]{:S(2)}, u32[]{:S(2)}) collective-permute-start(bf16[2048,1024]{1,0:T(8,128)(2,1)} %convolution_convert_fusion.4), channel_id=1, source_target_pairs={{0,8},{8,0},{16,24},{24,16},{1,9},{9,1},{17,25},{25,17},{2,10},{10... | collective-permute-start | bytes 12582920 | tf_op jit(solution)/shard_map/ppermute | solution.py:46
  782.1 84.1 %collective-permute-start.51 = (bf16[2048,256]{1,0:T(8,128)(2,1)}, bf16[2048,256]{1,0:T(8,128)(2,1)S(1)}, u32[]{:S(2)}, u32[]{:S(2)}) collective-permute-start(bf16[2048,256]{1,0:T(8,128)(2,1)} %slice.450), channel_id=1, source_target_pairs={{0,4},{1,5},{2,6},{3,7},{4,0},{5,1},{6,2},{7,3},{8,12},{9,13},{10,... | collective-permute-start | bytes 3145736 | tf_op jit(solution)/shard_map/ppermute | solution.py:46
  784.7 77.7 %collective-permute-start.52 = (bf16[2048,512]{1,0:T(8,128)(2,1)}, bf16[2048,512]{1,0:T(8,128)(2,1)}, u32[]{:S(2)}, u32[]{:S(2)}) collective-permute-start(bf16[2048,512]{1,0:T(8,128)(2,1)} %slice.446), channel_id=1, source_target_pairs={{0,16},{8,24},{16,0},{24,8},{1,17},{9,25},{17,1},{25,9},{2,18},{10... | collective-permute-start | bytes 6291464 | tf_op jit(solution)/shard_map/ppermute | solution.py:46
  787.1 54.6 %collective-permute-start.61 = (f32[4,2048]{1,0:T(4,128)S(1)}, f32[4,2048]{1,0:T(4,128)S(1)}, u32[]{:S(2)}, u32[]{:S(2)}) collective-permute-start(f32[4,2048]{1,0:T(4,128)S(1)} %fusion.126), channel_id=1, source_target_pairs={{0,4},{1,5},{2,6},{3,7},{4,0},{5,1},{6,2},{7,3},{8,12},{9,13},{10,... | collective-permute-start | bytes 98312 | tf_op jit(solution)/shard_map/ppermute | solution.py:46
  874.2 74.7 %collective-permute-start.55 = (bf16[2048,512]{1,0:T(8,128)(2,1)}, bf16[2048,512]{1,0:T(8,128)(2,1)}, u32[]{:S(2)}, u32[]{:S(2)}) collective-permute-start(bf16[2048,512]{1,0:T(8,128)(2,1)} %slice.444), channel_id=1, source_target_pairs={{0,16},{8,24},{16,0},{24,8},{1,17},{9,25},{17,1},{25,9},{2,18},{10... | collective-permute-start | bytes 6291464 | tf_op jit(solution)/shard_map/ppermute | solution.py:46
  875.5 128.5 %collective-permute-start.53 = (bf16[2048,256]{1,0:T(8,128)(2,1)}, bf16[2048,256]{1,0:T(8,128)(2,1)}, u32[]{:S(2)}, u32[]{:S(2)}) collective-permute-start(bf16[2048,256]{1,0:T(8,128)(2,1)} %slice.449), channel_id=1, source_target_pairs={{0,4},{1,5},{2,6},{3,7},{4,0},{5,1},{6,2},{7,3},{8,12},{9,13},{10,... | collective-permute-start | bytes 3145736 | tf_op jit(solution)/shard_map/ppermute | solution.py:46
  885.4 142.4 %all-to-all-start.3 = ((bf16[8,64,768]{2,1,0:T(8,128)(2,1)}), bf16[8,64,768]{2,1,0:T(8,128)(2,1)S(1)}, u32[]{:S(2)}, u32[]{:S(2)}) async-start(bf16[8,64,768]{2,1,0:T(8,128)(2,1)} %fusion.31), calls=%async_computation.4 | async-start | bytes 1572864 | tf_op jit(solution)/shard_map/all_to_all | solution.py:639
  904.9 106.8 %collective-permute-start.76 = (bf16[2048,256]{1,0:T(8,128)(2,1)}, bf16[2048,256]{1,0:T(8,128)(2,1)}, u32[]{:S(2)}, u32[]{:S(2)}) collective-permute-start(bf16[2048,256]{1,0:T(8,128)(2,1)} %collective-permute-done.75), channel_id=1, source_target_pairs={{0,8},{8,0},{16,24},{24,16},{1,9},{9,1},{17,25},{25,17},{2,10},{10... | collective-permute-start | bytes 3145736 | tf_op jit(solution)/shard_map/ppermute | solution.py:46
  955.6 97.5 %collective-permute-start.70 = (bf16[2048,256]{1,0:T(8,128)(2,1)}, bf16[2048,256]{1,0:T(8,128)(2,1)}, u32[]{:S(2)}, u32[]{:S(2)}) collective-permute-start(bf16[2048,256]{1,0:T(8,128)(2,1)} %slice.448), channel_id=1, source_target_pairs={{0,4},{1,5},{2,6},{3,7},{4,0},{5,1},{6,2},{7,3},{8,12},{9,13},{10,... | collective-permute-start | bytes 3145736 | tf_op jit(solution)/shard_map/ppermute | solution.py:46
  955.6 73.8 %collective-permute-start.64 = (bf16[256,512]{1,0:T(8,128)(2,1)}, bf16[256,512]{1,0:T(8,128)(2,1)}, u32[]{:S(2)}, u32[]{:S(2)}) collective-permute-start(bf16[256,512]{1,0:T(8,128)(2,1)} %reduce-scatter.5.cloned.1.call-done), channel_id=1, source_target_pairs={{0,8},{8,0},{16,24},{24,16},{1,9},{9,1},{17,25},{25,17},{2,10},{10... | collective-permute-start | bytes 786440 | tf_op jit(solution)/shard_map/ppermute | solution.py:46
  955.7 74.6 %collective-permute-start.65 = (bf16[256,512]{1,0:T(8,128)(2,1)}, bf16[256,512]{1,0:T(8,128)(2,1)S(1)}, u32[]{:S(2)}, u32[]{:S(2)}) collective-permute-start(bf16[256,512]{1,0:T(8,128)(2,1)} %reduce-scatter.5.cloned.1.call-done), channel_id=1, source_target_pairs={{0,16},{8,24},{16,0},{24,8},{1,17},{9,25},{17,1},{25,9},{2,18},{10... | collective-permute-start | bytes 786440 | tf_op jit(solution)/shard_map/ppermute | solution.py:46
  1011.6 49.3 %collective-permute-start.67 = (bf16[2048,256]{1,0:T(8,128)(2,1)}, bf16[2048,256]{1,0:T(8,128)(2,1)}, u32[]{:S(2)}, u32[]{:S(2)}) collective-permute-start(bf16[2048,256]{1,0:T(8,128)(2,1)} %get-tuple-element.120), channel_id=1, source_target_pairs={{0,8},{8,0},{16,24},{24,16},{1,9},{9,1},{17,25},{25,17},{2,10},{10... | collective-permute-start | bytes 3145736 | tf_op jit(solution)/shard_map/ppermute | solution.py:46
  1029.5 41.3 %collective-permute-start.68 = (bf16[2048,256]{1,0:T(8,128)(2,1)}, bf16[2048,256]{1,0:T(8,128)(2,1)}, u32[]{:S(2)}, u32[]{:S(2)}) collective-permute-start(bf16[2048,256]{1,0:T(8,128)(2,1)} %get-tuple-element.120), channel_id=1, source_target_pairs={{0,16},{8,24},{16,0},{24,8},{1,17},{9,25},{17,1},{25,9},{2,18},{10... | collective-permute-start | bytes 3145736 | tf_op jit(solution)/shard_map/ppermute | solution.py:46
  1031.8 44.5 %collective-permute-start.58 = (bf16[8,64,768]{2,1,0:T(8,128)(2,1)S(1)}, bf16[8,64,768]{2,1,0:T(8,128)(2,1)S(1)}, u32[]{:S(2)}, u32[]{:S(2)}) collective-permute-start(bf16[8,64,768]{2,1,0:T(8,128)(2,1)S(1)} %all-to-all-done.3), channel_id=1, source_target_pairs={{0,8},{8,0},{16,24},{24,16},{1,9},{9,1},{17,25},{25,17},{2,10},{10... | collective-permute-start | bytes 2359304 | tf_op jit(solution)/shard_map/ppermute | solution.py:46
  1060.9 52.0 %collective-permute-start.71 = (bf16[2048,256]{1,0:T(8,128)(2,1)}, bf16[2048,256]{1,0:T(8,128)(2,1)}, u32[]{:S(2)}, u32[]{:S(2)}) collective-permute-start(bf16[2048,256]{1,0:T(8,128)(2,1)} %get-tuple-element.118), channel_id=1, source_target_pairs={{0,8},{8,0},{16,24},{24,16},{1,9},{9,1},{17,25},{25,17},{2,10},{10... | collective-permute-start | bytes 3145736 | tf_op jit(solution)/shard_map/ppermute | solution.py:46
  1060.9 51.5 %collective-permute-start.72 = (bf16[2048,256]{1,0:T(8,128)(2,1)}, bf16[2048,256]{1,0:T(8,128)(2,1)}, u32[]{:S(2)}, u32[]{:S(2)}) collective-permute-start(bf16[2048,256]{1,0:T(8,128)(2,1)} %get-tuple-element.118), channel_id=1, source_target_pairs={{0,16},{8,24},{16,0},{24,8},{1,17},{9,25},{17,1},{25,9},{2,18},{10... | collective-permute-start | bytes 3145736 | tf_op jit(solution)/shard_map/ppermute | solution.py:46
  1070.8 47.5 %collective-permute-start.69 = (bf16[2048,256]{1,0:T(8,128)(2,1)}, bf16[2048,256]{1,0:T(8,128)(2,1)}, u32[]{:S(2)}, u32[]{:S(2)}) collective-permute-start(bf16[2048,256]{1,0:T(8,128)(2,1)} %collective-permute-done.68), channel_id=1, source_target_pairs={{0,8},{8,0},{16,24},{24,16},{1,9},{9,1},{17,25},{25,17},{2,10},{10... | collective-permute-start | bytes 3145736 | tf_op jit(solution)/shard_map/ppermute | solution.py:46
  (132 other events, 2187.3 us)
Sparse Core Ops, SparseCore 0:
  10.1 140.0 all-gather.2
  152.9 77.6 all-gather.4
  764.0 112.7 reduce-scatter.4
  880.2 222.8 reduce-scatter.2

commit v3 on v2

--- a/solution.py
+++ b/solution.py
@@ -402,7 +402,8 @@
             return lax.all_gather(
                 weight, "fsdp", axis=1, tiled=True, axis_index_groups=strides
             )
-        theirs = swapped(after(own_part(weight, 4, 0, 1), first), "fsdp", 4)
+        mine = after(own_part(weight, 4, 0, 1), first)
+        theirs = swapped(mine, "fsdp", 4)
         theirs = shared(after(theirs, second))
         blocks = []
         for v in (0, 2, 1, 3):
@@ -455,9 +456,9 @@
     if group != chain:
         rows_weight = jnp.tile(rows_weight, (group // chain, 1, 1))
     columns_weight = lax.all_to_all(rows_weight, "fsdp", 0, 0)
-    triple_weight = jnp.stack(in_order(shared(columns_weight)), axis=1).reshape(
-        model_width, 3 * width
-    )
+    column_slots = shared(columns_weight)
+    triple_weight = jnp.stack(in_order(column_slots), axis=1)
+    triple_weight = triple_weight.reshape(model_width, 3 * width)
     all_tokens = of_sequence(tokens)
 
     own_gains = jnp.stack([query_norm, key_norm, mixer_norm, feeder_norm]).astype(f32)
@@ -481,13 +482,14 @@
     query_low, key_low, value_low = prep(
         pre, squares, pair_gains.reshape(1, 2 * width), cosine, sine
     )
+    mixed_low, mixed, log_total = attend(starts, query_low, key_low, value_low)
     output_piece = lax.all_gather(
-        after(own_part(output_weight, 4, 0, 1), all_tokens), "fsdp", axis=0, tiled=True
-    )
-    output_slots = shared(after(output_piece, query_low))
+        after(own_part(output_weight, 4, 0, 1), squares), "fsdp", axis=0, tiled=True
+    )
+    output_piece = after(output_piece, mixed_low)
+    output_slots = shared(output_piece)
     whole_output = jnp.concatenate([output_slots[v] for v in (0, 2, 1, 3)], axis=1)
 
-    mixed_low, mixed, log_total = attend(starts, query_low, key_low, value_low)
     mixed_rows = exchanged(mixed_low.reshape(chain, own_rows, width))
     mixed_rows = mixed_rows.transpose(1, 0, 2).reshape(own_rows, model_width)
     branch_near = matmul(mixed_rows, whole_output)
@@ -497,15 +499,16 @@
     branch_factor = inverse_rms(branch_pre)
     hidden = tokens.astype(f32) + branch_pre * branch_factor * mixer_gain
 
-    wide_gate = widened(gate_weight, columns_weight, mixed_low)
-    wide_up = widened(up_weight, all_tokens, mixed_rows)
-    wide_down = widened(down_weight, query_low, hidden)
+    wide_gate = widened(gate_weight, squares, branch_near)
+    wide_up = widened(up_weight, mixed_low, branch_near)
     all_hidden = of_quad(hidden.astype(bf16))
     gate = matmul(all_hidden, wide_gate).astype(bf16)
+    wide_down = widened(down_weight, mixed_rows, gate)
     up = matmul(all_hidden, wide_up).astype(bf16)
     gate_wide, up_wide = gate.astype(f32), up.astype(f32)
     sigmoid = jax.nn.sigmoid(gate_wide)
     inner = (gate_wide * sigmoid * up_wide).astype(bf16)
+
     def down_terms(low, high, *deps):
         return against(after(inner[low:high], *deps), wide_down)
 
@@ -517,29 +520,43 @@
     feeder_part = jnp.sum(tangent * down_pre * down_factor, axis=0)
     down_grad = norm_backward(down_pre, down_factor, feeder_gain, tangent).astype(bf16)
     all_down_grad = of_quad(down_grad)
-    inner_grad = matmul(all_down_grad, wide_down)
+    if group == 8:
+        down_send = send_terms(all_down_grad, inner)
+        down_near = swapped(down_send, "rep", 1)
+        inner_grad = matmul(after(all_down_grad, down_send), wide_down)
+    else:
+        inner_grad = matmul(all_down_grad, wide_down)
     gate_grad = (
         inner_grad * up_wide * sigmoid * (1.0 + gate_wide * (1.0 - sigmoid))
     ).astype(bf16)
     up_grad = (inner_grad * gate_wide * sigmoid).astype(bf16)
+    if group == 8:
+        down_kept, down_pass = keep_terms(
+            all_down_grad, after(inner, gate_grad, up_grad), down_near
+        )
+        down_far = swapped(down_pass, "rep", 2)
+        back_gate, back_up = after(gate_grad, down_pass), after(up_grad, down_pass)
+    else:
+        back_gate, back_up = gate_grad, up_grad
     stage = {}
 
     def early_gradients(own):
         if group != 8:
             return ()
-        down_send = send_terms(all_down_grad, after(inner, own))
-        down_near = swapped(down_send, "rep", 1)
-        gate_send = send_terms(all_hidden, after(gate_grad, down_send))
-        stage["gate_near"] = swapped(gate_send, "rep", 1)
-        stage["down_kept"], down_pass = keep_terms(
-            all_down_grad, after(inner, gate_send), down_near
+        late_gate = after(gate_grad, own)
+        gate_send = send_terms(all_hidden, late_gate)
+        gate_near = swapped(gate_send, "rep", 1)
+        up_send = send_terms(all_hidden, after(up_grad, gate_send))
+        stage["up_near"] = swapped(up_send, "rep", 1)
+        gate_kept, gate_pass = keep_terms(
+            all_hidden, after(gate_grad, up_send), gate_near
         )
-        stage["down_far"] = swapped(down_pass, "rep", 2)
-        return (down_pass,)
+        stage["gate"] = gate_kept, swapped(gate_pass, "rep", 2)
+        return (gate_pass,)
 
     def back_terms(low, high, *deps):
-        return against(after(gate_grad[low:high], *deps), wide_gate) + against(
-            after(up_grad[low:high], *deps), wide_up
+        return against(after(back_gate[low:high], *deps), wide_gate) + against(
+            after(back_up[low:high], *deps), wide_up
         )
 
     feed_back = to_quad_rows(back_terms, early_gradients)
@@ -553,27 +570,27 @@
         [own_part(branch_grad, 4, v, 1) for v in (0, 2, 1, 3)], axis=1
     )
     mixed_grad_rows = against(grad_near, whole_output).astype(bf16)
-    mixed_grad = exchanged(
-        mixed_grad_rows.reshape(own_rows, chain, width).transpose(1, 0, 2)
-    ).reshape(chain * own_rows, width)
+    mixed_grad_rows = mixed_grad_rows.reshape(own_rows, chain, width).transpose(1, 0, 2)
+    mixed_grad = exchanged(mixed_grad_rows)
+    mixed_grad = mixed_grad.reshape(chain * own_rows, width)
     output_half = model_width // 2
     late_rows = after(mixed_rows, mixed_grad_rows)
     output_send = across(late_rows, grad_near[:, output_half:]).astype(bf16)
     output_near = swapped(output_send, "rep", 1)
+    late_rows = after(mixed_rows, output_send)
     if group == 8:
-        gate_kept, gate_pass = keep_terms(
-            all_hidden, after(gate_grad, output_send), stage["gate_near"]
-        )
-        late_rows = after(mixed_rows, gate_pass)
+        late_up = after(up_grad, output_send)
+        up_kept, up_pass = keep_terms(all_hidden, late_up, stage["up_near"])
+        up_far = swapped(up_pass, "rep", 2)
+        late_rows = after(mixed_rows, up_pass)
     output_kept = across(late_rows, grad_near[:, :output_half]) + output_near.astype(f32)
     output_pass = output_kept[:, quarter:].astype(bf16)
     output_kept = output_kept[:, :quarter]
     output_far = swapped(output_pass, "rep", 2)
     if group == 8:
-        gate_far = swapped(after(gate_pass, output_pass), "rep", 2)
-        up_send = send_terms(all_hidden, after(up_grad, output_pass))
-        up_near = swapped(up_send, "rep", 1)
-        mixed_grad = after(mixed_grad, up_send)
+        down_kept, down_pass = to_partner(down_kept, after(down_far, mixed_grad))
+        down_theirs = swapped(down_pass, "fsdp", 4)
+        mixed_grad = after(mixed_grad, output_pass)
     query_turn, key_turn, value_grad = attend_back(
         starts,
         query_low,
@@ -592,59 +609,70 @@
             jnp.sum(key_gain * key_turn * key_pre, axis=1),
         ]
     )
-    if group == 8:
-        down_kept, down_pass = to_partner(
-            stage["down_kept"], after(stage["down_far"], value_grad)
-        )
-        down_theirs = swapped(down_pass, "fsdp", 4)
-        means = after(means, down_pass)
-    means = xor_sum(means, "fsdp", chain) * (1.0 / model_width)
     factors = lax.rsqrt(squares * (1.0 / model_width) + norm_epsilon)
+
+    def gain_part(turn, pre_part, at):
+        own = jnp.sum(turn * pre_part * factors[at][:, None], axis=0)
+        whole = jnp.zeros((model_width,), f32)
+        return lax.dynamic_update_slice_in_dim(whole, own, spot * width, 0)
+
+    gain_parts = jnp.stack(
+        [
+            gain_part(query_turn, query_pre, 0),
+            gain_part(key_turn, key_pre, 1),
+            mixer_part,
+            feeder_part,
+        ]
+    )
+    if group == chain and model_width == means.shape[1]:
+        packed = xor_sum(jnp.concatenate([means, gain_parts]), "fsdp", group)
+        means, gain_parts = packed[:2], packed[2:]
+    else:
+        means = xor_sum(means, "fsdp", chain)
+        gain_parts = xor_sum(gain_parts, "fsdp", group)
+    means = means * (1.0 / model_width)
 
     def pair_back(turn, pre_part, gain, at):
         factor = factors[at][:, None]
         grad = factor * gain * turn - pre_part * factor * factor * factor * means[at][:, None]
-        return grad.astype(bf16), jnp.sum(turn * pre_part * factor, axis=0)
-
-    query_grad, query_part = pair_back(query_turn, query_pre, query_gain, 0)
-    key_grad, key_part = pair_back(key_turn, key_pre, key_gain, 1)
+        return grad.astype(bf16)
+
+    query_grad = pair_back(query_turn, query_pre, query_gain, 0)
+    key_grad = pair_back(key_turn, key_pre, key_gain, 1)
     triple_grad = jnp.concatenate([query_grad, key_grad, value_grad], axis=1)
-    output_part = (output_kept + after(output_far, triple_grad).astype(f32)).astype(bf16)
+    if group == 8:
+        down_total = (
+            down_kept + after(down_theirs, triple_grad).astype(f32)
+        ).astype(bf16)
+        down_pieces = shared(down_total)
+        gate_kept, gate_far = stage["gate"]
+        gate_kept, gate_pass = to_partner(gate_kept, after(gate_far, triple_grad))
+        gate_theirs = swapped(gate_pass, "fsdp", 4)
     token_terms = against(triple_grad, triple_weight).astype(bf16)
-    output_part = to_group_rows(output_part)
     token_rows = to_sequence_rows(token_terms)
     gradient_tokens = (hidden_grad + token_rows).astype(bf16)
 
-    triple_part = across(all_tokens, after(triple_grad, token_terms))
+    late_grad = after(triple_grad, token_terms)
+    triple_part = across(all_tokens, late_grad)
     if group == chain:
         triple_part = triple_part.reshape(chain, 4, part, 3 * width)
         slots = [own_part(triple_part, 4, v, 1)[:, 0] for v in range(4)]
         sends = [slots[v].astype(bf16) for v in (3, 1)]
         near = [swapped(x, "rep", 1) for x in sends]
-        if group == 8:
-            up_kept, up_pass = keep_terms(all_hidden, after(up_grad, *sends), up_near)
-            up_far = swapped(up_pass, "rep", 2)
-            near = [after(x, up_pass) for x in near]
         passed = (slots[2] + near[0].astype(f32)).astype(bf16)
         kept = slots[0] + near[1].astype(f32)
         passed_far = swapped(passed, "rep", 2)
         if group == 8:
-            gate_kept, gate_pass = to_partner(gate_kept, after(gate_far, passed))
-            gate_theirs = swapped(gate_pass, "fsdp", 4)
-            down_theirs = after(down_theirs, gate_pass)
-            down_total = (down_kept + down_theirs.astype(f32)).astype(bf16)
-            down_pieces = shared(down_total)
-            passed_far = after(passed_far, down_total)
+            up_kept, up_pass = to_partner(up_kept, after(up_far, passed))
+            up_theirs = swapped(up_pass, "fsdp", 4)
+            output_far = after(output_far, up_pass)
+        output_terms = (output_kept + output_far.astype(f32)).astype(bf16)
+        output_part = to_group_rows(output_terms).astype(bf16)
+        passed_far = after(passed_far, output_terms)
         kept = (kept + passed_far.astype(f32)).astype(bf16)
         heads_rows = lax.all_to_all(kept, "fsdp", 0, 0)
         if group == 8:
-            up_kept, up_pass = to_partner(up_kept, after(up_far, kept))
-            up_theirs = swapped(up_pass, "fsdp", 4)
-            output_part = after(output_part, up_pass)
-        output_total = output_part.astype(bf16)
-        output_pieces = shared(output_total)
-        if group == 8:
-            gate_theirs = after(gate_theirs, output_total)
+            gate_theirs = after(gate_theirs, kept)
             gate_total = (gate_kept + gate_theirs.astype(f32)).astype(bf16)
             gate_pieces = shared(gate_total)
             heads_rows = after(heads_rows, gate_total)
@@ -653,15 +681,17 @@
             up_theirs = after(up_theirs, heads_rows)
             up_total = (up_kept + up_theirs.astype(f32)).astype(bf16)
             up_pieces = shared(up_total)
+            output_part = after(output_part, up_total)
             gradient_down = replica_columns(down_pieces)
             gradient_gate = replica_columns(gate_pieces)
             gradient_up = replica_columns(up_pieces)
-        gradient_output = replica_columns(output_pieces)
+        output_pieces = shared(output_part)
         triple_rows = jnp.stack(in_order(triple_pieces))
         triple_rows = triple_rows.reshape(4, chain, part, 3, width)
         triple_rows = triple_rows.transpose(3, 0, 2, 1, 4).reshape(3, shard, model_width)
     else:
-        gradient_output = replica_columns(shared(output_part.astype(bf16)))
+        output_terms = (output_kept + output_far.astype(f32)).astype(bf16)
+        output_pieces = shared(to_group_rows(output_terms).astype(bf16))
         triple_rows = lax.dynamic_update_slice_in_dim(
             jnp.zeros((model_width, 3, chain, width), f32),
             triple_part.reshape(model_width, 3, 1, width),
@@ -671,25 +701,14 @@
         triple_rows = to_group_rows(triple_rows.reshape(model_width, 3 * model_width))
         triple_rows = lax.psum(triple_rows.astype(bf16), "rep")
         triple_rows = triple_rows.reshape(shard, 3, model_width).transpose(1, 0, 2)
+    gradient_output = replica_columns(output_pieces)
     if group != 8:
         gradient_down = narrowed_whole(all_down_grad, inner)
         gradient_gate = narrowed_whole(all_hidden, gate_grad)
         gradient_up = narrowed_whole(all_hidden, up_grad)
     triple_rows = triple_rows.astype(f32)
 
-    gain_parts = jnp.stack(
-        [
-            lax.dynamic_update_slice_in_dim(
-                jnp.zeros((model_width,), f32), query_part, spot * width, 0
-            ),
-            lax.dynamic_update_slice_in_dim(
-                jnp.zeros((model_width,), f32), key_part, spot * width, 0
-            ),
-            mixer_part,
-            feeder_part,
-        ]
-    )
-    gain_parts = xor_sum(xor_sum(gain_parts, "fsdp", group), "rep", 4)
+    gain_parts = xor_sum(gain_parts, "rep", 4)
     gain_own = lax.dynamic_slice_in_dim(gain_parts, me * shard, shard, 1)
     return (
         result,

time: 1140 us -> 1280 us (1.12)
  waiting for transfers between devices: 511 us -> 641 us
    ppermute x77 -> x74, waiting for transfers between devices: 427 us -> 541 us  [swapped(): return lax.ppermute(block, axis, [(i, i ^ bit) for i in range(size)])]
    all_gather x1, waiting for transfers between devices: 0.02 us -> 14 us  [body(): lax.all_gather(after(own_part(output_weight, 4, 0, 1), squares), 'fsdp',...]
    unnamed x197 -> x192, local copies, waits for them, and re-layouts: 69.9 us -> 63.7 us
    ppermute x77 -> x74, starting transfers between devices: 63.3 us -> 64.7 us  [swapped(): return lax.ppermute(block, axis, [(i, i ^ bit) for i in range(size)])]
  transfers between devices with their start and end apart: 84 -> 81, of which waited for: 36 -> 38; matrix products, arithmetic and copies ran while one was open for 29% -> 25% of each run, Pallas kernels for 5% -> 2%
where the time goes in v3:
time: 1280 us; the launch traced here: 1270 us
  waiting for transfers between devices  641 us (50%)
  matrix products  195 us (15%)
  local copies, waits for them, and re-layouts  140 us (11%)
  other arithmetic  89.6 us (7%)
  starting transfers between devices  81 us (6%)
  Pallas kernels  57.9 us (5%)
  blocking collectives  45.9 us (4%)
  between operations  16 us (1%)
    ppermute x74, waiting for transfers between devices, swapped(): return lax.ppermute(block, axis, [(i, i ^ bit) for i in range(size)])  541 us
    all_gather x1, waiting for transfers between devices, of_sequence(): lax.all_gather(block, 'fsdp', axis=0, tiled=True, axis_index_groups=teams)  75.1 us
    dot_general x11, matrix products, against(): lax.dot_general(a, b, (((1,), (1,)), ((), ())), preferred_element_type=f32)  70 us
    dot_general x9, matrix products, across(): lax.dot_general(a, b, (((0,), (0,)), ((), ())), preferred_element_type=f32)  69.6 us
    ppermute x74, starting transfers between devices, swapped(): return lax.ppermute(block, axis, [(i, i ^ bit) for i in range(size)])  64.7 us
    unnamed x192, local copies, waits for them, and re-layouts  63.7 us
    dot_general x5, matrix products, matmul(): return jnp.dot(a, b, preferred_element_type=f32)  55.6 us
    all_to_all x1, blocking collectives, body(): columns_weight = lax.all_to_all(rows_weight, 'fsdp', 0, 0)  45.9 us
  transfers between devices with their start and end apart: 81, of which 38 were waited for; matrix products, arithmetic and copies ran while one was open for 25% of the time, Pallas kernels for 2%

profile of v3, /device:TPU:0, one launch (start us, length us, event | category | flops | bytes accessed | tf_op | source)
XLA Modules:
  0.0 1266.8 jit_solution(18353529020233657211)
XLA Ops:
  11.0 45.9 %all_to_all.20 = bf16[8,64,768]{2,1,0:T(8,128)(2,1)S(1)} all-to-all(bf16[8,64,768]{2,1,0:T(8,128)(2,1)S(1)} %reshape.130), channel_id=1, replica_groups=mesh['rep'=4,'fsdp'=8] {'fsdp'}, dimensions={0} | all-to-all | bytes 1572864 | tf_op jit(solution)/shard_map/all_to_all | solution.py:458
  58.4 10.5 collective-permute-done
  75.1 75.1 %all-gather.3.cloned.1.call-done = bf16[2048,2048]{1,0:T(8,128)(2,1)} async-done(((bf16[256,2048]{1,0:T(8,128)(2,1)}), bf16[2048,2048]{1,0:T(8,128)(2,1)}) %all-gather.3.cloned.1.call-update) | async-done | bytes 8388624 | tf_op jit(solution)/shard_map/all_gather | solution.py:351
  150.2 10.0 convolution_bitcast_fusion.pre_ref
  190.1 19.8 %attend.1 = (bf16[2048,256]{1,0:T(8,128)(2,1)}, f32[2048,256]{1,0:T(8,128)}, f32[2048,256]{1,0:T(8,128)}) custom-call(s32[2]{0:T(128)} %fusion.58.starts_ref, bf16[2048,256]{1,0:T(8,128)(2,1)} %get-tuple-element.56.q_ref, bf16[2048,256]{1,0:T(8,128)(2,1)} %get-tuple-element.57.k_ref, bf16[2048,256]{1,0:T(8,128)(2,1)} %get-tuple-element.58.v_ref), custom_call_target="tpu_custom_call" | custom-call | flops 2147483648 | bytes 8388608 | tf_op jit(solution)/shard_map/attend/pallas_call | solution.py:199
  210.0 14.0 %all-gather.5.cloned.1.call-done = bf16[2048,512]{1,0:T(8,128)(2,1)} async-done(((bf16[256,512]{1,0:T(8,128)(2,1)}), bf16[2048,512]{1,0:T(8,128)(2,1)}) %all-gather.5.cloned.1.call-update) | async-done | bytes 2097168 | tf_op jit(solution)/shard_map/all_gather | solution.py:486
  233.3 36.4 %collective-permute-done.6 = bf16[2048,512]{1,0:T(8,128)(2,1)} collective-permute-done((bf16[2048,512]{1,0:T(8,128)(2,1)}, bf16[2048,512]{1,0:T(8,128)(2,1)}, u32[]{:S(2)}, u32[]{:S(2)}) %collective-permute-start.6) | collective-permute-done | bytes 2097184 | tf_op jit(solution)/shard_map/ppermute | solution.py:46
  294.8 59.0 %collective-permute-done.16 = bf16[2048,256]{1,0:T(8,128)(2,1)} collective-permute-done((bf16[2048,256]{1,0:T(8,128)(2,1)}, bf16[2048,256]{1,0:T(8,128)(2,1)}, u32[]{:S(2)}, u32[]{:S(2)}) %collective-permute-start.16) | collective-permute-done | bytes 1048608 | tf_op jit(solution)/shard_map/ppermute | solution.py:46
  357.7 17.9 %collective-permute-done.20 = bf16[2048,256]{1,0:T(8,128)(2,1)} collective-permute-done((bf16[2048,256]{1,0:T(8,128)(2,1)}, bf16[2048,256]{1,0:T(8,128)(2,1)}, u32[]{:S(2)}, u32[]{:S(2)}) %collective-permute-start.20) | collective-permute-done | bytes 1048608 | tf_op jit(solution)/shard_map/ppermute | solution.py:46
  386.0 11.9 collective-permute-done.13
  407.8 12.8 %collective-permute-done.14 = bf16[128,2048]{1,0:T(8,128)(2,1)S(1)} collective-permute-done((bf16[128,2048]{1,0:T(8,128)(2,1)S(1)}, bf16[128,2048]{1,0:T(8,128)(2,1)S(1)}, u32[]{:S(2)}, u32[]{:S(2)}) %collective-permute-start.14) | collective-permute-done | bytes 524320 | tf_op jit(solution)/shard_map/ppermute | solution.py:46
  421.9 13.2 %convolution_convert_fusion.3 = bf16[1024,2048]{1,0:T(8,128)(2,1)} fusion(bf16[1024,2048]{1,0:T(8,128)(2,1)S(1)} %constant_dynamic-update-slice_fusion.4, bf16[2048,2048]{1,0:T(8,128)(2,1)} %constant_dynamic-update-slice_fusion.9), kind=kOutput, calls=%fused_computation.35 | convolution fusion | flops 8592031744 | bytes 16777216 | tf_op jit(solution)/shard_map/dot_general | solution.py:23
  435.0 15.0 %collective-permute-start.25 = (bf16[2048,256]{1,0:T(8,128)(2,1)S(1)}, bf16[2048,256]{1,0:T(8,128)(2,1)S(1)}, u32[]{:S(2)}, u32[]{:S(2)}) collective-permute-start(bf16[2048,256]{1,0:T(8,128)(2,1)S(1)} %collective-permute-done.24), channel_id=1, source_target_pairs={{0,16},{8,24},{16,0},{24,8},{1,17},{9,25},{17,1},{25,9},{2,18},{10... | collective-permute-start | bytes 3145736 | tf_op jit(solution)/shard_map/ppermute | solution.py:46
  451.1 14.7 %fusion = (bf16[1024,2048]{1,0:T(8,128)(2,1)S(1)}, bf16[1024,2048]{1,0:T(8,128)(2,1)}) fusion(bf16[1024,2048]{1,0:T(8,128)(2,1)} %convolution_convert_fusion.3, bf16[1024,2048]{1,0:T(8,128)(2,1)S(1)} %constant_dynamic-update-slice_fusion.4, bf16[2048,2048]{1,0:T(8,128)(2,1)} %constant_dynamic-update-slice_fusion.14), kind=kOutput, calls=%fused_computation.6 | convolution fusion | flops 8608808960 | bytes 25165824 | tf_op jit(solution)/shard_map/dot_general | solution.py:23
  492.4 22.4 %collective-permute-done.30 = bf16[256,2048]{1,0:T(8,128)(2,1)S(1)} collective-permute-done((bf16[256,2048]{1,0:T(8,128)(2,1)S(1)}, bf16[256,2048]{1,0:T(8,128)(2,1)S(1)}, u32[]{:S(2)}, u32[]{:S(2)}) %collective-permute-start.30) | collective-permute-done | bytes 1048608 | tf_op jit(solution)/shard_map/ppermute | solution.py:46
  526.1 20.7 %collective-permute-done.32 = bf16[256,2048]{1,0:T(8,128)(2,1)S(1)} collective-permute-done((bf16[256,2048]{1,0:T(8,128)(2,1)S(1)}, bf16[256,2048]{1,0:T(8,128)(2,1)S(1)}, u32[]{:S(2)}, u32[]{:S(2)}) %collective-permute-start.32) | collective-permute-done | bytes 1048608 | tf_op jit(solution)/shard_map/ppermute | solution.py:46
  549.8 9.5 collective-permute-done.34
  565.6 15.3 %fusion.3 = (bf16[1024,2048]{1,0:T(8,128)(2,1)S(1)}, bf16[1024,2048]{1,0:T(8,128)(2,1)S(1)}) fusion(bf16[1024,2048]{1,0:T(8,128)(2,1)} %get-tuple-element.195, bf16[1024,2048]{1,0:T(8,128)(2,1)} %convolution_convert_fusion.3, bf16[1024,2048]{1,0:T(8,128)(2,1)S(1)} %constant_dynamic-update-slice_fusion.24, bf16[2048,2048]{1,0:T(8,128)(2,1)} %copy-done.52), kind=kOutput, calls=%fused_computation.9 | convolution fusion | flops 8621391872 | bytes 29360128 | tf_op jit(solution)/shard_map/dot_general | solution.py:23
  581.0 10.4 convert_add_fusion.3
  613.2 9.4 fusion.84
  654.0 10.2 convolution_convert_fusion.4
  725.0 31.6 %attend_back.1 = (f32[2048,256]{1,0:T(8,128)}, f32[2048,256]{1,0:T(8,128)}, bf16[2048,256]{1,0:T(8,128)(2,1)}) custom-call(s32[2]{0:T(128)} %fusion.58.starts_ref, bf16[2048,256]{1,0:T(8,128)(2,1)} %get-tuple-element.56.q_ref, bf16[2048,256]{1,0:T(8,128)(2,1)} %bitcast.18.grad_ref, f32[2048,256]{1,0:T(8,128)} %get-tuple-element.83.mixed_ref, ...), custom_call_target="tpu_custom_call" | custom-call | flops 5368709120 | bytes 14680064 | tf_op jit(solution)/shard_map/attend_back/pallas_call | solution.py:295
  782.8 9.1 convolution_convert_fusion
  791.9 11.9 convolution_bitcast_fusion.1
  825.7 34.5 %collective-permute-done.50 = bf16[2048,512]{1,0:T(8,128)(2,1)} collective-permute-done((bf16[2048,512]{1,0:T(8,128)(2,1)}, bf16[2048,512]{1,0:T(8,128)(2,1)}, u32[]{:S(2)}, u32[]{:S(2)}) %collective-permute-start.50) | collective-permute-done | bytes 2097184 | tf_op jit(solution)/shard_map/ppermute | solution.py:46
  866.7 46.7 %collective-permute-done.69 = bf16[2048,512]{1,0:T(8,128)(2,1)S(1)} collective-permute-done((bf16[2048,512]{1,0:T(8,128)(2,1)}, bf16[2048,512]{1,0:T(8,128)(2,1)S(1)}, u32[]{:S(2)}, u32[]{:S(2)}) %collective-permute-start.69) | collective-permute-done | bytes 2097184 | tf_op jit(solution)/shard_map/ppermute | solution.py:46
  921.0 47.5 %collective-permute-done.70 = bf16[2048,256]{1,0:T(8,128)(2,1)S(1)} collective-permute-done((bf16[2048,256]{1,0:T(8,128)(2,1)}, bf16[2048,256]{1,0:T(8,128)(2,1)S(1)}, u32[]{:S(2)}, u32[]{:S(2)}) %collective-permute-start.70) | collective-permute-done | bytes 1048608 | tf_op jit(solution)/shard_map/ppermute | solution.py:46
  986.2 16.9 %collective-permute-done.58 = f32[4,2048]{1,0:T(4,128)S(1)} collective-permute-done((f32[4,2048]{1,0:T(4,128)S(1)}, f32[4,2048]{1,0:T(4,128)S(1)}, u32[]{:S(2)}, u32[]{:S(2)}) %collective-permute-start.58) | collective-permute-done | bytes 32800 | tf_op jit(solution)/shard_map/ppermute | solution.py:46
  1007.0 15.3 %collective-permute-done.49 = bf16[8,64,768]{2,1,0:T(8,128)(2,1)S(1)} collective-permute-done((bf16[8,64,768]{2,1,0:T(8,128)(2,1)S(1)}, bf16[8,64,768]{2,1,0:T(8,128)(2,1)S(1)}, u32[]{:S(2)}, u32[]{:S(2)}) %collective-permute-start.49) | collective-permute-done | bytes 786464 | tf_op jit(solution)/shard_map/ppermute | solution.py:46
  1028.7 86.4 %collective-permute-done.53 = bf16[2048,256]{1,0:T(8,128)(2,1)} collective-permute-done((bf16[2048,256]{1,0:T(8,128)(2,1)}, bf16[2048,256]{1,0:T(8,128)(2,1)}, u32[]{:S(2)}, u32[]{:S(2)}) %collective-permute-start.53) | collective-permute-done | bytes 1048608 | tf_op jit(solution)/shard_map/ppermute | solution.py:46
  1129.5 18.6 %collective-permute-done.64 = bf16[2048,256]{1,0:T(8,128)(2,1)} collective-permute-done((bf16[2048,256]{1,0:T(8,128)(2,1)S(1)}, bf16[2048,256]{1,0:T(8,128)(2,1)}, u32[]{:S(2)}, u32[]{:S(2)}) %collective-permute-start.64) | collective-permute-done | bytes 1048608 | tf_op jit(solution)/shard_map/ppermute | solution.py:46
  1170.1 34.8 %collective-permute-done.54 = bf16[8,64,768]{2,1,0:T(8,128)(2,1)S(1)} collective-permute-done((bf16[8,64,768]{2,1,0:T(8,128)(2,1)S(1)}, bf16[8,64,768]{2,1,0:T(8,128)(2,1)S(1)}, u32[]{:S(2)}, u32[]{:S(2)}) %collective-permute-start.54) | collective-permute-done | bytes 786464 | tf_op jit(solution)/shard_map/ppermute | solution.py:46
  (493 shorter events, 443.4 us)
Async XLA Ops:
  7.2 143.0 %all-gather.3.cloned.1.call-start = ((), (), s32[]{:S(2)}) async-start(), calls=%async_computation.6 | async-start | bytes 9437184 | tf_op jit(solution)/shard_map/all_gather | solution.py:351
  7.9 216.0 %all-gather.5.cloned.1.call-start = ((), (), s32[]{:S(2)}) async-start(), calls=%async_computation.7 | async-start | bytes 2359296 | tf_op jit(solution)/shard_map/all_gather | solution.py:486
  223.9 45.8 %collective-permute-start.6 = (bf16[2048,512]{1,0:T(8,128)(2,1)}, bf16[2048,512]{1,0:T(8,128)(2,1)}, u32[]{:S(2)}, u32[]{:S(2)}) collective-permute-start(bf16[2048,512]{1,0:T(8,128)(2,1)} %all-gather.5.cloned.1.call-done), channel_id=1, source_target_pairs={{0,16},{8,24},{16,0},{24,8},{1,17},{9,25},{17,1},{25,9},{2,18},{10... | collective-permute-start | bytes 6291464 | tf_op jit(solution)/shard_map/ppermute | solution.py:46
  227.7 57.8 %all-to-all-start.1 = ((bf16[8,256,256]{1,2,0:T(8,128)(2,1)}), bf16[8,256,256]{1,2,0:T(8,128)(2,1)S(1)}, u32[]{:S(2)}, u32[]{:S(2)}) async-start(bf16[8,256,256]{1,2,0:T(8,128)(2,1)} %copy.55), calls=%async_computation.1 | async-start | bytes 2097152 | tf_op jit(solution)/shard_map/all_to_all | solution.py:368
  231.2 56.5 %collective-permute-start.7 = (bf16[2048,512]{1,0:T(8,128)(2,1)S(1)}, bf16[2048,512]{1,0:T(8,128)(2,1)}, u32[]{:S(2)}, u32[]{:S(2)}) collective-permute-start(bf16[2048,512]{1,0:T(8,128)(2,1)S(1)} %copy-done.37), channel_id=1, source_target_pairs={{0,8},{8,0},{16,24},{24,16},{1,9},{9,1},{17,25},{25,17},{2,10},{10... | collective-permute-start | bytes 6291464 | tf_op jit(solution)/shard_map/ppermute | solution.py:46
  231.4 41.0 %collective-permute-start.9 = (f32[4,2048]{1,0:T(4,128)S(1)}, f32[4,2048]{1,0:T(4,128)S(1)}, u32[]{:S(2)}, u32[]{:S(2)}) collective-permute-start(f32[4,2048]{1,0:T(4,128)S(1)} %constant_dynamic-update-slice_fusion.32), channel_id=1, source_target_pairs={{0,1},{1,0},{2,3},{3,2},{4,5},{5,4},{6,7},{7,6},{8,9},{9,8},{10,11... | collective-permute-start | bytes 98312 | tf_op jit(solution)/shard_map/ppermute | solution.py:46
  282.5 71.3 %collective-permute-start.16 = (bf16[2048,256]{1,0:T(8,128)(2,1)}, bf16[2048,256]{1,0:T(8,128)(2,1)}, u32[]{:S(2)}, u32[]{:S(2)}) collective-permute-start(bf16[2048,256]{1,0:T(8,128)(2,1)} %get-tuple-element.62), channel_id=1, source_target_pairs={{0,4},{1,5},{2,6},{3,7},{4,0},{5,1},{6,2},{7,3},{8,12},{9,13},{10,... | collective-permute-start | bytes 3145736 | tf_op jit(solution)/shard_map/ppermute | solution.py:46
  284.5 91.1 %collective-permute-start.20 = (bf16[2048,256]{1,0:T(8,128)(2,1)}, bf16[2048,256]{1,0:T(8,128)(2,1)}, u32[]{:S(2)}, u32[]{:S(2)}) collective-permute-start(bf16[2048,256]{1,0:T(8,128)(2,1)} %get-tuple-element.64), channel_id=1, source_target_pairs={{0,4},{1,5},{2,6},{3,7},{4,0},{5,1},{6,2},{7,3},{8,12},{9,13},{10,... | collective-permute-start | bytes 3145736 | tf_op jit(solution)/shard_map/ppermute | solution.py:46
  355.3 47.5 %collective-permute-start.18 = (bf16[2048,256]{1,0:T(8,128)(2,1)}, bf16[2048,256]{1,0:T(8,128)(2,1)S(1)}, u32[]{:S(2)}, u32[]{:S(2)}) collective-permute-start(bf16[2048,256]{1,0:T(8,128)(2,1)} %collective-permute-done.16), channel_id=1, source_target_pairs={{0,8},{8,0},{16,24},{24,16},{1,9},{9,1},{17,25},{25,17},{2,10},{10... | collective-permute-start | bytes 3145736 | tf_op jit(solution)/shard_map/ppermute | solution.py:46
  357.7 40.2 %collective-permute-start.13 = (bf16[256,2048]{1,0:T(8,128)(2,1)S(1)}, bf16[256,2048]{1,0:T(8,128)(2,1)S(1)}, u32[]{:S(2)}, u32[]{:S(2)}) collective-permute-start(bf16[256,2048]{1,0:T(8,128)(2,1)S(1)} %get-tuple-element.129), channel_id=1, source_target_pairs={{0,2},{1,3},{2,0},{3,1},{4,6},{5,7},{6,4},{7,5},{8,10},{9,11},{10,... | collective-permute-start | bytes 3145736 | tf_op jit(solution)/shard_map/ppermute | solution.py:46
  386.0 49.1 %collective-permute-start.24 = (bf16[2048,256]{1,0:T(8,128)(2,1)S(1)}, bf16[2048,256]{1,0:T(8,128)(2,1)S(1)}, u32[]{:S(2)}, u32[]{:S(2)}) collective-permute-start(bf16[2048,256]{1,0:T(8,128)(2,1)S(1)} %copy-done.42), channel_id=1, source_target_pairs={{0,4},{1,5},{2,6},{3,7},{4,0},{5,1},{6,2},{7,3},{8,12},{9,13},{10,... | collective-permute-start | bytes 3145736 | tf_op jit(solution)/shard_map/ppermute | solution.py:46
  407.1 43.0 %collective-permute-start.23 = (bf16[2048,256]{1,0:T(8,128)(2,1)S(1)}, bf16[2048,256]{1,0:T(8,128)(2,1)S(1)}, u32[]{:S(2)}, u32[]{:S(2)}) collective-permute-start(bf16[2048,256]{1,0:T(8,128)(2,1)S(1)} %collective-permute-done.21), channel_id=1, source_target_pairs={{0,8},{8,0},{16,24},{24,16},{1,9},{9,1},{17,25},{25,17},{2,10},{10... | collective-permute-start | bytes 3145736 | tf_op jit(solution)/shard_map/ppermute | solution.py:46
  435.0 31.2 %collective-permute-start.25 = (bf16[2048,256]{1,0:T(8,128)(2,1)S(1)}, bf16[2048,256]{1,0:T(8,128)(2,1)S(1)}, u32[]{:S(2)}, u32[]{:S(2)}) collective-permute-start(bf16[2048,256]{1,0:T(8,128)(2,1)S(1)} %collective-permute-done.24), channel_id=1, source_target_pairs={{0,16},{8,24},{16,0},{24,8},{1,17},{9,25},{17,1},{25,9},{2,18},{10... | collective-permute-start | bytes 3145736 | tf_op jit(solution)/shard_map/ppermute | solution.py:46
  664.2 34.8 %collective-permute-start.42 = (bf16[2048,1024]{1,0:T(8,128)(2,1)}, bf16[2048,1024]{1,0:T(8,128)(2,1)}, u32[]{:S(2)}, u32[]{:S(2)}) collective-permute-start(bf16[2048,1024]{1,0:T(8,128)(2,1)} %convolution_convert_fusion.4), channel_id=1, source_target_pairs={{0,8},{8,0},{16,24},{24,16},{1,9},{9,1},{17,25},{25,17},{2,10},{10... | collective-permute-start | bytes 12582920 | tf_op jit(solution)/shard_map/ppermute | solution.py:46
  690.2 34.8 %all-to-all-start.2 = ((bf16[8,256,256]{2,1,0:T(8,128)(2,1)}), bf16[8,256,256]{2,1,0:T(8,128)(2,1)}, u32[]{:S(2)}, u32[]{:S(2)}) async-start(bf16[8,256,256]{2,1,0:T(8,128)(2,1)} %bitcast.146), calls=%async_computation.2 | async-start | bytes 2097152 | tf_op jit(solution)/shard_map/all_to_all | solution.py:368
  698.9 546.8 %reduce-scatter.5.cloned.1.call-start = ((), (), s32[]{:S(2)}) async-start(), calls=%async_computation.9 | async-start | bytes 2359296 | tf_op jit(solution)/shard_map/reduce_scatter | solution.py:363
  769.7 49.1 %collective-permute-start.51 = (bf16[2048,512]{1,0:T(8,128)(2,1)}, bf16[2048,512]{1,0:T(8,128)(2,1)}, u32[]{:S(2)}, u32[]{:S(2)}) collective-permute-start(bf16[2048,512]{1,0:T(8,128)(2,1)} %slice.454), channel_id=1, source_target_pairs={{0,16},{8,24},{16,0},{24,8},{1,17},{9,25},{17,1},{25,9},{2,18},{10... | collective-permute-start | bytes 6291464 | tf_op jit(solution)/shard_map/ppermute | solution.py:46
  771.5 88.8 %collective-permute-start.50 = (bf16[2048,512]{1,0:T(8,128)(2,1)}, bf16[2048,512]{1,0:T(8,128)(2,1)}, u32[]{:S(2)}, u32[]{:S(2)}) collective-permute-start(bf16[2048,512]{1,0:T(8,128)(2,1)} %slice.453), channel_id=1, source_target_pairs={{0,16},{8,24},{16,0},{24,8},{1,17},{9,25},{17,1},{25,9},{2,18},{10... | collective-permute-start | bytes 6291464 | tf_op jit(solution)/shard_map/ppermute | solution.py:46
  864.1 393.2 %reduce-scatter.3.cloned.1.call-start = ((), (), s32[]{:S(2)}) async-start(), calls=%async_computation.8 | async-start | bytes 9437184 | tf_op jit(solution)/shard_map/reduce_scatter | solution.py:354
  864.6 48.8 %collective-permute-start.69 = (bf16[2048,512]{1,0:T(8,128)(2,1)}, bf16[2048,512]{1,0:T(8,128)(2,1)S(1)}, u32[]{:S(2)}, u32[]{:S(2)}) collective-permute-start(bf16[2048,512]{1,0:T(8,128)(2,1)} %slice.456), channel_id=1, source_target_pairs={{0,16},{8,24},{16,0},{24,8},{1,17},{9,25},{17,1},{25,9},{2,18},{10... | collective-permute-start | bytes 6291464 | tf_op jit(solution)/shard_map/ppermute | solution.py:46
  866.5 112.1 %collective-permute-start.52 = (bf16[2048,512]{1,0:T(8,128)(2,1)}, bf16[2048,512]{1,0:T(8,128)(2,1)}, u32[]{:S(2)}, u32[]{:S(2)}) collective-permute-start(bf16[2048,512]{1,0:T(8,128)(2,1)} %slice.455), channel_id=1, source_target_pairs={{0,16},{8,24},{16,0},{24,8},{1,17},{9,25},{17,1},{25,9},{2,18},{10... | collective-permute-start | bytes 6291464 | tf_op jit(solution)/shard_map/ppermute | solution.py:46
  919.5 49.0 %collective-permute-start.70 = (bf16[2048,256]{1,0:T(8,128)(2,1)}, bf16[2048,256]{1,0:T(8,128)(2,1)S(1)}, u32[]{:S(2)}, u32[]{:S(2)}) collective-permute-start(bf16[2048,256]{1,0:T(8,128)(2,1)} %slice.457), channel_id=1, source_target_pairs={{0,4},{1,5},{2,6},{3,7},{4,0},{5,1},{6,2},{7,3},{8,12},{9,13},{10,... | collective-permute-start | bytes 3145736 | tf_op jit(solution)/shard_map/ppermute | solution.py:46
  985.8 129.4 %collective-permute-start.53 = (bf16[2048,256]{1,0:T(8,128)(2,1)}, bf16[2048,256]{1,0:T(8,128)(2,1)}, u32[]{:S(2)}, u32[]{:S(2)}) collective-permute-start(bf16[2048,256]{1,0:T(8,128)(2,1)} %slice.458), channel_id=1, source_target_pairs={{0,4},{1,5},{2,6},{3,7},{4,0},{5,1},{6,2},{7,3},{8,12},{9,13},{10,... | collective-permute-start | bytes 3145736 | tf_op jit(solution)/shard_map/ppermute | solution.py:46
  986.2 36.2 %collective-permute-start.47 = (bf16[8,64,768]{2,1,0:T(8,128)(2,1)S(1)}, bf16[8,64,768]{2,1,0:T(8,128)(2,1)S(1)}, u32[]{:S(2)}, u32[]{:S(2)}) collective-permute-start(bf16[8,64,768]{2,1,0:T(8,128)(2,1)S(1)} %copy-done.46), channel_id=1, source_target_pairs={{0,8},{8,0},{16,24},{24,16},{1,9},{9,1},{17,25},{25,17},{2,10},{10... | collective-permute-start | bytes 2359304 | tf_op jit(solution)/shard_map/ppermute | solution.py:46
  1005.4 149.7 %collective-permute-start.59 = (bf16[2048,256]{1,0:T(8,128)(2,1)}, bf16[2048,256]{1,0:T(8,128)(2,1)}, u32[]{:S(2)}, u32[]{:S(2)}) collective-permute-start(bf16[2048,256]{1,0:T(8,128)(2,1)} %slice.459), channel_id=1, source_target_pairs={{0,4},{1,5},{2,6},{3,7},{4,0},{5,1},{6,2},{7,3},{8,12},{9,13},{10,... | collective-permute-start | bytes 3145736 | tf_op jit(solution)/shard_map/ppermute | solution.py:46
  1005.5 121.3 %collective-permute-start.73 = (bf16[2048,256]{1,0:T(8,128)(2,1)}, bf16[2048,256]{1,0:T(8,128)(2,1)}, u32[]{:S(2)}, u32[]{:S(2)}) collective-permute-start(bf16[2048,256]{1,0:T(8,128)(2,1)} %collective-permute-done.72), channel_id=1, source_target_pairs={{0,8},{8,0},{16,24},{24,16},{1,9},{9,1},{17,25},{25,17},{2,10},{10... | collective-permute-start | bytes 3145736 | tf_op jit(solution)/shard_map/ppermute | solution.py:46
  1024.9 130.2 %all-to-all-start.3 = ((bf16[8,64,768]{2,1,0:T(8,128)(2,1)}), bf16[8,64,768]{2,1,0:T(8,128)(2,1)S(1)}, u32[]{:S(2)}, u32[]{:S(2)}) async-start(bf16[8,64,768]{2,1,0:T(8,128)(2,1)} %fusion.31), calls=%async_computation.4 | async-start | bytes 1572864 | tf_op jit(solution)/shard_map/all_to_all | solution.py:673
  1162.5 42.9 %collective-permute-start.66 = (bf16[2048,256]{1,0:T(8,128)(2,1)S(1)}, bf16[2048,256]{1,0:T(8,128)(2,1)S(1)}, u32[]{:S(2)}, u32[]{:S(2)}) collective-permute-start(bf16[2048,256]{1,0:T(8,128)(2,1)S(1)} %get-tuple-element.114), channel_id=1, source_target_pairs={{0,8},{8,0},{16,24},{24,16},{1,9},{9,1},{17,25},{25,17},{2,10},{10... | collective-permute-start | bytes 3145736 | tf_op jit(solution)/shard_map/ppermute | solution.py:46
  1162.5 42.4 %collective-permute-start.67 = (bf16[2048,256]{1,0:T(8,128)(2,1)S(1)}, bf16[2048,256]{1,0:T(8,128)(2,1)}, u32[]{:S(2)}, u32[]{:S(2)}) collective-permute-start(bf16[2048,256]{1,0:T(8,128)(2,1)S(1)} %get-tuple-element.114), channel_id=1, source_target_pairs={{0,16},{8,24},{16,0},{24,8},{1,17},{9,25},{17,1},{25,9},{2,18},{10... | collective-permute-start | bytes 3145736 | tf_op jit(solution)/shard_map/ppermute | solution.py:46
  1163.9 41.0 %collective-permute-start.54 = (bf16[8,64,768]{2,1,0:T(8,128)(2,1)S(1)}, bf16[8,64,768]{2,1,0:T(8,128)(2,1)S(1)}, u32[]{:S(2)}, u32[]{:S(2)}) collective-permute-start(bf16[8,64,768]{2,1,0:T(8,128)(2,1)S(1)} %all-to-all-done.3), channel_id=1, source_target_pairs={{0,16},{8,24},{16,0},{24,8},{1,17},{9,25},{17,1},{25,9},{2,18},{10... | collective-permute-start | bytes 2359304 | tf_op jit(solution)/shard_map/ppermute | solution.py:46
  1167.3 42.3 %collective-permute-start.56 = (bf16[8,64,768]{2,1,0:T(8,128)(2,1)S(1)}, bf16[8,64,768]{2,1,0:T(8,128)(2,1)S(1)}, u32[]{:S(2)}, u32[]{:S(2)}) collective-permute-start(bf16[8,64,768]{2,1,0:T(8,128)(2,1)S(1)} %all-to-all-done.3), channel_id=1, source_target_pairs={{0,8},{8,0},{16,24},{24,16},{1,9},{9,1},{17,25},{25,17},{2,10},{10... | collective-permute-start | bytes 2359304 | tf_op jit(solution)/shard_map/ppermute | solution.py:46
  1204.9 42.4 %collective-permute-start.68 = (bf16[2048,256]{1,0:T(8,128)(2,1)}, bf16[2048,256]{1,0:T(8,128)(2,1)}, u32[]{:S(2)}, u32[]{:S(2)}) collective-permute-start(bf16[2048,256]{1,0:T(8,128)(2,1)} %collective-permute-done.67), channel_id=1, source_target_pairs={{0,8},{8,0},{16,24},{24,16},{1,9},{9,1},{17,25},{25,17},{2,10},{10... | collective-permute-start | bytes 3145736 | tf_op jit(solution)/shard_map/ppermute | solution.py:46
  (126 other events, 2060.7 us)
Sparse Core Ops, SparseCore 0:
  10.1 140.0 all-gather.2
  176.6 47.2 all-gather.4
  864.2 87.4 reduce-scatter.4
  955.2 247.1 reduce-scatter.2

commit v4 on v3

--- a/solution.py
+++ b/solution.py
@@ -499,8 +499,8 @@
     branch_factor = inverse_rms(branch_pre)
     hidden = tokens.astype(f32) + branch_pre * branch_factor * mixer_gain
 
-    wide_gate = widened(gate_weight, squares, branch_near)
-    wide_up = widened(up_weight, mixed_low, branch_near)
+    wide_gate = widened(gate_weight, mixed_low, branch_near)
+    wide_up = widened(up_weight, mixed_rows, branch_near)
     all_hidden = of_quad(hidden.astype(bf16))
     gate = matmul(all_hidden, wide_gate).astype(bf16)
     wide_down = widened(down_weight, mixed_rows, gate)
@@ -667,7 +667,10 @@
             up_theirs = swapped(up_pass, "fsdp", 4)
             output_far = after(output_far, up_pass)
         output_terms = (output_kept + output_far.astype(f32)).astype(bf16)
-        output_part = to_group_rows(output_terms).astype(bf16)
+        output_part = lax.all_to_all(
+            output_terms.reshape(group, shard, quarter), "fsdp", 0, 0
+        )
+        output_part = jnp.sum(output_part.astype(f32), axis=0).astype(bf16)
         passed_far = after(passed_far, output_terms)
         kept = (kept + passed_far.astype(f32)).astype(bf16)
         heads_rows = lax.all_to_all(kept, "fsdp", 0, 0)

time: 1280 us -> 1210 us (0.945)
  waiting for transfers between devices: 641 us -> 596 us
  local copies, waits for them, and re-layouts: 140 us -> 127 us
    ppermute x74, waiting for transfers between devices: 541 us -> 503 us  [swapped(): return lax.ppermute(block, axis, [(i, i ^ bit) for i in range(size)])]
    unnamed x192 -> x193, local copies, waits for them, and re-layouts: 63.7 us -> 52 us
  transfers between devices with their start and end apart: 81 -> 81, of which waited for: 38 -> 37; matrix products, arithmetic and copies ran while one was open for 25% -> 25% of each run, Pallas kernels for 2% -> 5%
where the time goes in v4:
time: 1210 us; the launch traced here: 1200 us
  waiting for transfers between devices  596 us (49%)
  matrix products  192 us (16%)
  local copies, waits for them, and re-layouts  127 us (10%)
  other arithmetic  90.9 us (8%)
  starting transfers between devices  71.7 us (6%)
  Pallas kernels  57.8 us (5%)
  blocking collectives  45.9 us (4%)
  between operations  16 us (1%)
    ppermute x74, waiting for transfers between devices, swapped(): return lax.ppermute(block, axis, [(i, i ^ bit) for i in range(size)])  503 us
    all_gather x1, waiting for transfers between devices, of_sequence(): lax.all_gather(block, 'fsdp', axis=0, tiled=True, axis_index_groups=teams)  75.1 us
    dot_general x11, matrix products, against(): lax.dot_general(a, b, (((1,), (1,)), ((), ())), preferred_element_type=f32)  70.1 us
    dot_general x9, matrix products, across(): lax.dot_general(a, b, (((0,), (0,)), ((), ())), preferred_element_type=f32)  66.2 us
    dot_general x5, matrix products, matmul(): return jnp.dot(a, b, preferred_element_type=f32)  55.9 us
    ppermute x74, starting transfers between devices, swapped(): return lax.ppermute(block, axis, [(i, i ^ bit) for i in range(size)])  55.2 us
    unnamed x193, local copies, waits for them, and re-layouts  52 us
    all_to_all x1, blocking collectives, body(): columns_weight = lax.all_to_all(rows_weight, 'fsdp', 0, 0)  45.9 us
  transfers between devices with their start and end apart: 81, of which 37 were waited for; matrix products, arithmetic and copies ran while one was open for 25% of the time, Pallas kernels for 5%

profile of v4, /device:TPU:0, one launch (start us, length us, event | category | flops | bytes accessed | tf_op | source)
XLA Modules:
  0.0 1197.7 jit_solution(12996934326040102227)
XLA Ops:
  11.0 45.9 %all_to_all.25 = bf16[8,64,768]{2,1,0:T(8,128)(2,1)S(1)} all-to-all(bf16[8,64,768]{2,1,0:T(8,128)(2,1)S(1)} %reshape.133), channel_id=1, replica_groups=mesh['rep'=4,'fsdp'=8] {'fsdp'}, dimensions={0} | all-to-all | bytes 1572864 | tf_op jit(solution)/shard_map/all_to_all | solution.py:458
  58.4 10.5 collective-permute-done
  75.1 75.1 %all-gather.3.cloned.1.call-done = bf16[2048,2048]{1,0:T(8,128)(2,1)} async-done(((bf16[256,2048]{1,0:T(8,128)(2,1)}), bf16[2048,2048]{1,0:T(8,128)(2,1)}) %all-gather.3.cloned.1.call-update) | async-done | bytes 8388624 | tf_op jit(solution)/shard_map/all_gather | solution.py:351
  150.2 10.0 convolution_bitcast_fusion.pre_ref
  190.0 19.8 %attend.1 = (bf16[2048,256]{1,0:T(8,128)(2,1)}, f32[2048,256]{1,0:T(8,128)}, f32[2048,256]{1,0:T(8,128)}) custom-call(s32[2]{0:T(128)} %fusion.58.starts_ref, bf16[2048,256]{1,0:T(8,128)(2,1)} %get-tuple-element.56.q_ref, bf16[2048,256]{1,0:T(8,128)(2,1)} %get-tuple-element.57.k_ref, bf16[2048,256]{1,0:T(8,128)(2,1)} %get-tuple-element.58.v_ref), custom_call_target="tpu_custom_call" | custom-call | flops 2147483648 | bytes 8388608 | tf_op jit(solution)/shard_map/attend/pallas_call | solution.py:199
  209.8 14.1 %all-gather.5.cloned.1.call-done = bf16[2048,512]{1,0:T(8,128)(2,1)} async-done(((bf16[256,512]{1,0:T(8,128)(2,1)}), bf16[2048,512]{1,0:T(8,128)(2,1)}) %all-gather.5.cloned.1.call-update) | async-done | bytes 2097168 | tf_op jit(solution)/shard_map/all_gather | solution.py:486
  231.3 38.4 %collective-permute-done.6 = bf16[2048,512]{1,0:T(8,128)(2,1)} collective-permute-done((bf16[2048,512]{1,0:T(8,128)(2,1)}, bf16[2048,512]{1,0:T(8,128)(2,1)}, u32[]{:S(2)}, u32[]{:S(2)}) %collective-permute-start.6) | collective-permute-done | bytes 2097184 | tf_op jit(solution)/shard_map/ppermute | solution.py:46
  297.0 58.0 %collective-permute-done.16 = bf16[2048,256]{1,0:T(8,128)(2,1)} collective-permute-done((bf16[2048,256]{1,0:T(8,128)(2,1)}, bf16[2048,256]{1,0:T(8,128)(2,1)}, u32[]{:S(2)}, u32[]{:S(2)}) %collective-permute-start.16) | collective-permute-done | bytes 1048608 | tf_op jit(solution)/shard_map/ppermute | solution.py:46
  358.9 17.8 %collective-permute-done.20 = bf16[2048,256]{1,0:T(8,128)(2,1)S(1)} collective-permute-done((bf16[2048,256]{1,0:T(8,128)(2,1)}, bf16[2048,256]{1,0:T(8,128)(2,1)S(1)}, u32[]{:S(2)}, u32[]{:S(2)}) %collective-permute-start.20) | collective-permute-done | bytes 1048608 | tf_op jit(solution)/shard_map/ppermute | solution.py:46
  385.9 13.2 %collective-permute-done.13 = bf16[256,2048]{1,0:T(8,128)(2,1)S(1)} collective-permute-done((bf16[256,2048]{1,0:T(8,128)(2,1)S(1)}, bf16[256,2048]{1,0:T(8,128)(2,1)S(1)}, u32[]{:S(2)}, u32[]{:S(2)}) %collective-permute-start.13) | collective-permute-done | bytes 1048608 | tf_op jit(solution)/shard_map/ppermute | solution.py:46
  408.9 26.4 %collective-permute-done.14 = bf16[128,2048]{1,0:T(8,128)(2,1)S(1)} collective-permute-done((bf16[128,2048]{1,0:T(8,128)(2,1)S(1)}, bf16[128,2048]{1,0:T(8,128)(2,1)S(1)}, u32[]{:S(2)}, u32[]{:S(2)}) %collective-permute-start.14) | collective-permute-done | bytes 524320 | tf_op jit(solution)/shard_map/ppermute | solution.py:46
  436.6 13.4 %convolution_convert_fusion.3 = bf16[1024,2048]{1,0:T(8,128)(2,1)} fusion(bf16[1024,2048]{1,0:T(8,128)(2,1)S(1)} %constant_dynamic-update-slice_fusion.4, bf16[2048,2048]{1,0:T(8,128)(2,1)} %constant_dynamic-update-slice_fusion.9), kind=kOutput, calls=%fused_computation.35 | convolution fusion | flops 8592031744 | bytes 16777216 | tf_op jit(solution)/shard_map/dot_general | solution.py:23
  452.5 14.8 %fusion = (bf16[1024,2048]{1,0:T(8,128)(2,1)S(1)}, bf16[1024,2048]{1,0:T(8,128)(2,1)}) fusion(bf16[1024,2048]{1,0:T(8,128)(2,1)} %convolution_convert_fusion.3, bf16[1024,2048]{1,0:T(8,128)(2,1)S(1)} %constant_dynamic-update-slice_fusion.4, bf16[2048,2048]{1,0:T(8,128)(2,1)} %constant_dynamic-update-slice_fusion.14), kind=kOutput, calls=%fused_computation.6 | convolution fusion | flops 8608808960 | bytes 25165824 | tf_op jit(solution)/shard_map/dot_general | solution.py:23
  497.2 22.0 %collective-permute-done.30 = bf16[256,2048]{1,0:T(8,128)(2,1)S(1)} collective-permute-done((bf16[256,2048]{1,0:T(8,128)(2,1)S(1)}, bf16[256,2048]{1,0:T(8,128)(2,1)S(1)}, u32[]{:S(2)}, u32[]{:S(2)}) %collective-permute-start.30) | collective-permute-done | bytes 1048608 | tf_op jit(solution)/shard_map/ppermute | solution.py:46
  530.6 20.4 %collective-permute-done.32 = bf16[256,2048]{1,0:T(8,128)(2,1)S(1)} collective-permute-done((bf16[256,2048]{1,0:T(8,128)(2,1)S(1)}, bf16[256,2048]{1,0:T(8,128)(2,1)S(1)}, u32[]{:S(2)}, u32[]{:S(2)}) %collective-permute-start.32) | collective-permute-done | bytes 1048608 | tf_op jit(solution)/shard_map/ppermute | solution.py:46
  553.9 9.5 collective-permute-done.34
  569.7 15.3 %fusion.3 = (bf16[1024,2048]{1,0:T(8,128)(2,1)S(1)}, bf16[1024,2048]{1,0:T(8,128)(2,1)S(1)}) fusion(bf16[1024,2048]{1,0:T(8,128)(2,1)} %get-tuple-element.195, bf16[1024,2048]{1,0:T(8,128)(2,1)} %convolution_convert_fusion.3, bf16[1024,2048]{1,0:T(8,128)(2,1)S(1)} %constant_dynamic-update-slice_fusion.24, bf16[2048,2048]{1,0:T(8,128)(2,1)} %copy-done.49), kind=kOutput, calls=%fused_computation.9 | convolution fusion | flops 8621391872 | bytes 29360128 | tf_op jit(solution)/shard_map/dot_general | solution.py:23
  585.1 10.4 convert_add_fusion.3
  617.1 9.4 fusion.84
  626.5 9.0 fusion.82
  658.2 9.9 convolution_convert_fusion.4
  668.2 9.0 convert_add_fusion.2
  700.2 8.8 convert_add_fusion.1
  724.6 31.5 %attend_back.1 = (f32[2048,256]{1,0:T(8,128)}, f32[2048,256]{1,0:T(8,128)}, bf16[2048,256]{1,0:T(8,128)(2,1)}) custom-call(s32[2]{0:T(128)} %fusion.58.starts_ref, bf16[2048,256]{1,0:T(8,128)(2,1)} %get-tuple-element.56.q_ref, bf16[2048,256]{1,0:T(8,128)(2,1)} %bitcast.18.grad_ref, f32[2048,256]{1,0:T(8,128)} %get-tuple-element.83.mixed_ref, ...), custom_call_target="tpu_custom_call" | custom-call | flops 5368709120 | bytes 14680064 | tf_op jit(solution)/shard_map/attend_back/pallas_call | solution.py:295
  780.9 9.0 convolution_convert_fusion
  802.7 86.7 %collective-permute-done.70 = bf16[2048,256]{1,0:T(8,128)(2,1)} collective-permute-done((bf16[2048,256]{1,0:T(8,128)(2,1)}, bf16[2048,256]{1,0:T(8,128)(2,1)}, u32[]{:S(2)}, u32[]{:S(2)}) %collective-permute-start.70) | collective-permute-done | bytes 1048608 | tf_op jit(solution)/shard_map/ppermute | solution.py:46
  896.8 8.8 convolution_bitcast_fusion.1
  923.7 9.6 collective-permute-done.58
  947.6 11.8 collective-permute-done.72
  976.4 68.7 %collective-permute-done.53 = bf16[2048,256]{1,0:T(8,128)(2,1)} collective-permute-done((bf16[2048,256]{1,0:T(8,128)(2,1)}, bf16[2048,256]{1,0:T(8,128)(2,1)}, u32[]{:S(2)}, u32[]{:S(2)}) %collective-permute-start.53) | collective-permute-done | bytes 1048608 | tf_op jit(solution)/shard_map/ppermute | solution.py:46
  1058.4 19.7 %collective-permute-done.64 = bf16[2048,256]{1,0:T(8,128)(2,1)} collective-permute-done((bf16[2048,256]{1,0:T(8,128)(2,1)S(1)}, bf16[2048,256]{1,0:T(8,128)(2,1)}, u32[]{:S(2)}, u32[]{:S(2)}) %collective-permute-start.64) | collective-permute-done | bytes 1048608 | tf_op jit(solution)/shard_map/ppermute | solution.py:46
  1099.5 34.5 %collective-permute-done.54 = bf16[8,64,768]{2,1,0:T(8,128)(2,1)S(1)} collective-permute-done((bf16[8,64,768]{2,1,0:T(8,128)(2,1)S(1)}, bf16[8,64,768]{2,1,0:T(8,128)(2,1)S(1)}, u32[]{:S(2)}, u32[]{:S(2)}) %collective-permute-start.54) | collective-permute-done | bytes 786464 | tf_op jit(solution)/shard_map/ppermute | solution.py:46
  (496 shorter events, 420.2 us)
Async XLA Ops:
  7.2 143.0 %all-gather.3.cloned.1.call-start = ((), (), s32[]{:S(2)}) async-start(), calls=%async_computation.6 | async-start | bytes 9437184 | tf_op jit(solution)/shard_map/all_gather | solution.py:351
  7.9 216.0 %all-gather.5.cloned.1.call-start = ((), (), s32[]{:S(2)}) async-start(), calls=%async_computation.7 | async-start | bytes 2359296 | tf_op jit(solution)/shard_map/all_gather | solution.py:486
  223.9 45.8 %collective-permute-start.6 = (bf16[2048,512]{1,0:T(8,128)(2,1)}, bf16[2048,512]{1,0:T(8,128)(2,1)}, u32[]{:S(2)}, u32[]{:S(2)}) collective-permute-start(bf16[2048,512]{1,0:T(8,128)(2,1)} %all-gather.5.cloned.1.call-done), channel_id=1, source_target_pairs={{0,16},{8,24},{16,0},{24,8},{1,17},{9,25},{17,1},{25,9},{2,18},{10... | collective-permute-start | bytes 6291464 | tf_op jit(solution)/shard_map/ppermute | solution.py:46
  227.7 58.7 %all-to-all-start.1 = ((bf16[8,256,256]{1,2,0:T(8,128)(2,1)}), bf16[8,256,256]{1,2,0:T(8,128)(2,1)S(1)}, u32[]{:S(2)}, u32[]{:S(2)}) async-start(bf16[8,256,256]{1,2,0:T(8,128)(2,1)} %copy.55), calls=%async_computation.1 | async-start | bytes 2097152 | tf_op jit(solution)/shard_map/all_to_all | solution.py:368
  231.2 58.7 %collective-permute-start.7 = (bf16[2048,512]{1,0:T(8,128)(2,1)S(1)}, bf16[2048,512]{1,0:T(8,128)(2,1)}, u32[]{:S(2)}, u32[]{:S(2)}) collective-permute-start(bf16[2048,512]{1,0:T(8,128)(2,1)S(1)} %copy-done.38), channel_id=1, source_target_pairs={{0,8},{8,0},{16,24},{24,16},{1,9},{9,1},{17,25},{25,17},{2,10},{10... | collective-permute-start | bytes 6291464 | tf_op jit(solution)/shard_map/ppermute | solution.py:46
  284.8 70.2 %collective-permute-start.16 = (bf16[2048,256]{1,0:T(8,128)(2,1)}, bf16[2048,256]{1,0:T(8,128)(2,1)}, u32[]{:S(2)}, u32[]{:S(2)}) collective-permute-start(bf16[2048,256]{1,0:T(8,128)(2,1)} %get-tuple-element.62), channel_id=1, source_target_pairs={{0,4},{1,5},{2,6},{3,7},{4,0},{5,1},{6,2},{7,3},{8,12},{9,13},{10,... | collective-permute-start | bytes 3145736 | tf_op jit(solution)/shard_map/ppermute | solution.py:46
  286.4 90.2 %collective-permute-start.20 = (bf16[2048,256]{1,0:T(8,128)(2,1)}, bf16[2048,256]{1,0:T(8,128)(2,1)S(1)}, u32[]{:S(2)}, u32[]{:S(2)}) collective-permute-start(bf16[2048,256]{1,0:T(8,128)(2,1)} %get-tuple-element.64), channel_id=1, source_target_pairs={{0,4},{1,5},{2,6},{3,7},{4,0},{5,1},{6,2},{7,3},{8,12},{9,13},{10,... | collective-permute-start | bytes 3145736 | tf_op jit(solution)/shard_map/ppermute | solution.py:46
  356.5 47.4 %collective-permute-start.18 = (bf16[2048,256]{1,0:T(8,128)(2,1)}, bf16[2048,256]{1,0:T(8,128)(2,1)S(1)}, u32[]{:S(2)}, u32[]{:S(2)}) collective-permute-start(bf16[2048,256]{1,0:T(8,128)(2,1)} %collective-permute-done.16), channel_id=1, source_target_pairs={{0,8},{8,0},{16,24},{24,16},{1,9},{9,1},{17,25},{25,17},{2,10},{10... | collective-permute-start | bytes 3145736 | tf_op jit(solution)/shard_map/ppermute | solution.py:46
  358.9 40.2 %collective-permute-start.13 = (bf16[256,2048]{1,0:T(8,128)(2,1)S(1)}, bf16[256,2048]{1,0:T(8,128)(2,1)S(1)}, u32[]{:S(2)}, u32[]{:S(2)}) collective-permute-start(bf16[256,2048]{1,0:T(8,128)(2,1)S(1)} %get-tuple-element.129), channel_id=1, source_target_pairs={{0,2},{1,3},{2,0},{3,1},{4,6},{5,7},{6,4},{7,5},{8,10},{9,11},{10,... | collective-permute-start | bytes 3145736 | tf_op jit(solution)/shard_map/ppermute | solution.py:46
  385.8 64.2 %collective-permute-start.24 = (bf16[2048,256]{1,0:T(8,128)(2,1)S(1)}, bf16[2048,256]{1,0:T(8,128)(2,1)S(1)}, u32[]{:S(2)}, u32[]{:S(2)}) collective-permute-start(bf16[2048,256]{1,0:T(8,128)(2,1)S(1)} %copy-done.42), channel_id=1, source_target_pairs={{0,4},{1,5},{2,6},{3,7},{4,0},{5,1},{6,2},{7,3},{8,12},{9,13},{10,... | collective-permute-start | bytes 3145736 | tf_op jit(solution)/shard_map/ppermute | solution.py:46
  399.1 36.2 %collective-permute-start.14 = (bf16[128,2048]{1,0:T(8,128)(2,1)S(1)}, bf16[128,2048]{1,0:T(8,128)(2,1)S(1)}, u32[]{:S(2)}, u32[]{:S(2)}) collective-permute-start(bf16[128,2048]{1,0:T(8,128)(2,1)S(1)} %slice.306), channel_id=1, source_target_pairs={{0,2},{1,3},{2,0},{3,1},{4,6},{5,7},{6,4},{7,5},{8,10},{9,11},{10,... | collective-permute-start | bytes 1572872 | tf_op jit(solution)/shard_map/ppermute | solution.py:46
  401.2 34.2 %collective-permute-start.15 = (bf16[128,2048]{1,0:T(8,128)(2,1)S(1)}, bf16[128,2048]{1,0:T(8,128)(2,1)S(1)}, u32[]{:S(2)}, u32[]{:S(2)}) collective-permute-start(bf16[128,2048]{1,0:T(8,128)(2,1)S(1)} %slice.307), channel_id=1, source_target_pairs={{0,1},{1,0},{2,3},{3,2},{4,5},{5,4},{6,7},{7,6},{8,9},{9,8},{10,11... | collective-permute-start | bytes 1572872 | tf_op jit(solution)/shard_map/ppermute | solution.py:46
  408.2 43.3 %collective-permute-start.23 = (bf16[2048,256]{1,0:T(8,128)(2,1)S(1)}, bf16[2048,256]{1,0:T(8,128)(2,1)S(1)}, u32[]{:S(2)}, u32[]{:S(2)}) collective-permute-start(bf16[2048,256]{1,0:T(8,128)(2,1)S(1)} %collective-permute-done.21), channel_id=1, source_target_pairs={{0,8},{8,0},{16,24},{24,16},{1,9},{9,1},{17,25},{25,17},{2,10},{10... | collective-permute-start | bytes 3145736 | tf_op jit(solution)/shard_map/ppermute | solution.py:46
  668.0 32.1 %collective-permute-start.42 = (bf16[2048,1024]{1,0:T(8,128)(2,1)}, bf16[2048,1024]{1,0:T(8,128)(2,1)}, u32[]{:S(2)}, u32[]{:S(2)}) collective-permute-start(bf16[2048,1024]{1,0:T(8,128)(2,1)} %convolution_convert_fusion.4), channel_id=1, source_target_pairs={{0,8},{8,0},{16,24},{24,16},{1,9},{9,1},{17,25},{25,17},{2,10},{10... | collective-permute-start | bytes 12582920 | tf_op jit(solution)/shard_map/ppermute | solution.py:46
  698.4 489.8 %reduce-scatter.2.cloned.1.call-start = ((), (), s32[]{:S(2)}) async-start(), calls=%async_computation.8 | async-start | bytes 9437184 | tf_op jit(solution)/shard_map/reduce_scatter | solution.py:354
  698.5 71.0 %collective-permute-start.69 = (bf16[2048,512]{1,0:T(8,128)(2,1)}, bf16[2048,512]{1,0:T(8,128)(2,1)}, u32[]{:S(2)}, u32[]{:S(2)}) collective-permute-start(bf16[2048,512]{1,0:T(8,128)(2,1)} %slice.456), channel_id=1, source_target_pairs={{0,16},{8,24},{16,0},{24,8},{1,17},{9,25},{17,1},{25,9},{2,18},{10... | collective-permute-start | bytes 6291464 | tf_op jit(solution)/shard_map/ppermute | solution.py:46
  796.7 92.8 %collective-permute-start.70 = (bf16[2048,256]{1,0:T(8,128)(2,1)}, bf16[2048,256]{1,0:T(8,128)(2,1)}, u32[]{:S(2)}, u32[]{:S(2)}) collective-permute-start(bf16[2048,256]{1,0:T(8,128)(2,1)} %slice.457), channel_id=1, source_target_pairs={{0,4},{1,5},{2,6},{3,7},{4,0},{5,1},{6,2},{7,3},{8,12},{9,13},{10,... | collective-permute-start | bytes 3145736 | tf_op jit(solution)/shard_map/ppermute | solution.py:46
  796.8 118.1 %collective-permute-start.52 = (bf16[2048,512]{1,0:T(8,128)(2,1)}, bf16[2048,512]{1,0:T(8,128)(2,1)}, u32[]{:S(2)}, u32[]{:S(2)}) collective-permute-start(bf16[2048,512]{1,0:T(8,128)(2,1)} %slice.455), channel_id=1, source_target_pairs={{0,16},{8,24},{16,0},{24,8},{1,17},{9,25},{17,1},{25,9},{2,18},{10... | collective-permute-start | bytes 6291464 | tf_op jit(solution)/shard_map/ppermute | solution.py:46
  798.9 139.8 %collective-permute-start.51 = (bf16[2048,512]{1,0:T(8,128)(2,1)}, bf16[2048,512]{1,0:T(8,128)(2,1)}, u32[]{:S(2)}, u32[]{:S(2)}) collective-permute-start(bf16[2048,512]{1,0:T(8,128)(2,1)} %slice.454), channel_id=1, source_target_pairs={{0,16},{8,24},{16,0},{24,8},{1,17},{9,25},{17,1},{25,9},{2,18},{10... | collective-permute-start | bytes 6291464 | tf_op jit(solution)/shard_map/ppermute | solution.py:46
  798.9 163.3 %collective-permute-start.50 = (bf16[2048,512]{1,0:T(8,128)(2,1)}, bf16[2048,512]{1,0:T(8,128)(2,1)}, u32[]{:S(2)}, u32[]{:S(2)}) collective-permute-start(bf16[2048,512]{1,0:T(8,128)(2,1)} %slice.453), channel_id=1, source_target_pairs={{0,16},{8,24},{16,0},{24,8},{1,17},{9,25},{17,1},{25,9},{2,18},{10... | collective-permute-start | bytes 6291464 | tf_op jit(solution)/shard_map/ppermute | solution.py:46
  896.8 46.8 %collective-permute-start.71 = (bf16[2048,256]{1,0:T(8,128)(2,1)S(1)}, bf16[2048,256]{1,0:T(8,128)(2,1)}, u32[]{:S(2)}, u32[]{:S(2)}) collective-permute-start(bf16[2048,256]{1,0:T(8,128)(2,1)S(1)} %get-tuple-element.112), channel_id=1, source_target_pairs={{0,8},{8,0},{16,24},{24,16},{1,9},{9,1},{17,25},{25,17},{2,10},{10... | collective-permute-start | bytes 3145736 | tf_op jit(solution)/shard_map/ppermute | solution.py:46
  935.9 109.2 %collective-permute-start.53 = (bf16[2048,256]{1,0:T(8,128)(2,1)}, bf16[2048,256]{1,0:T(8,128)(2,1)}, u32[]{:S(2)}, u32[]{:S(2)}) collective-permute-start(bf16[2048,256]{1,0:T(8,128)(2,1)} %slice.458), channel_id=1, source_target_pairs={{0,4},{1,5},{2,6},{3,7},{4,0},{5,1},{6,2},{7,3},{8,12},{9,13},{10,... | collective-permute-start | bytes 3145736 | tf_op jit(solution)/shard_map/ppermute | solution.py:46
  938.7 32.7 %collective-permute-start.47 = (bf16[8,64,768]{2,1,0:T(8,128)(2,1)S(1)}, bf16[8,64,768]{2,1,0:T(8,128)(2,1)S(1)}, u32[]{:S(2)}, u32[]{:S(2)}) collective-permute-start(bf16[8,64,768]{2,1,0:T(8,128)(2,1)S(1)} %get-tuple-element.135), channel_id=1, source_target_pairs={{0,8},{8,0},{16,24},{24,16},{1,9},{9,1},{17,25},{25,17},{2,10},{10... | collective-permute-start | bytes 2359304 | tf_op jit(solution)/shard_map/ppermute | solution.py:46
  959.5 124.8 %collective-permute-start.59 = (bf16[2048,256]{1,0:T(8,128)(2,1)}, bf16[2048,256]{1,0:T(8,128)(2,1)}, u32[]{:S(2)}, u32[]{:S(2)}) collective-permute-start(bf16[2048,256]{1,0:T(8,128)(2,1)} %slice.459), channel_id=1, source_target_pairs={{0,4},{1,5},{2,6},{3,7},{4,0},{5,1},{6,2},{7,3},{8,12},{9,13},{10,... | collective-permute-start | bytes 3145736 | tf_op jit(solution)/shard_map/ppermute | solution.py:46
  962.2 93.5 %collective-permute-start.73 = (bf16[2048,256]{1,0:T(8,128)(2,1)}, bf16[2048,256]{1,0:T(8,128)(2,1)}, u32[]{:S(2)}, u32[]{:S(2)}) collective-permute-start(bf16[2048,256]{1,0:T(8,128)(2,1)} %collective-permute-done.72), channel_id=1, source_target_pairs={{0,8},{8,0},{16,24},{24,16},{1,9},{9,1},{17,25},{25,17},{2,10},{10... | collective-permute-start | bytes 3145736 | tf_op jit(solution)/shard_map/ppermute | solution.py:46
  972.6 107.0 %all-to-all-start.3 = ((bf16[8,64,768]{2,1,0:T(8,128)(2,1)}), bf16[8,64,768]{2,1,0:T(8,128)(2,1)S(1)}, u32[]{:S(2)}, u32[]{:S(2)}) async-start(bf16[8,64,768]{2,1,0:T(8,128)(2,1)} %fusion.31), calls=%async_computation.4 | async-start | bytes 1572864 | tf_op jit(solution)/shard_map/all_to_all | solution.py:676
  1079.6 95.3 %all-to-all-start.4 = ((bf16[8,256,512]{2,1,0:T(8,128)(2,1)}), bf16[8,256,512]{2,1,0:T(8,128)(2,1)}, u32[]{:S(2)}, u32[]{:S(2)}) async-start(bf16[8,256,512]{2,1,0:T(8,128)(2,1)} %bitcast.149), calls=%async_computation.5 | async-start | bytes 4194304 | tf_op jit(solution)/shard_map/all_to_all | solution.py:670
  1091.6 42.9 %collective-permute-start.66 = (bf16[2048,256]{1,0:T(8,128)(2,1)S(1)}, bf16[2048,256]{1,0:T(8,128)(2,1)S(1)}, u32[]{:S(2)}, u32[]{:S(2)}) collective-permute-start(bf16[2048,256]{1,0:T(8,128)(2,1)S(1)} %get-tuple-element.114), channel_id=1, source_target_pairs={{0,8},{8,0},{16,24},{24,16},{1,9},{9,1},{17,25},{25,17},{2,10},{10... | collective-permute-start | bytes 3145736 | tf_op jit(solution)/shard_map/ppermute | solution.py:46
  1092.1 41.9 %collective-permute-start.67 = (bf16[2048,256]{1,0:T(8,128)(2,1)S(1)}, bf16[2048,256]{1,0:T(8,128)(2,1)}, u32[]{:S(2)}, u32[]{:S(2)}) collective-permute-start(bf16[2048,256]{1,0:T(8,128)(2,1)S(1)} %get-tuple-element.114), channel_id=1, source_target_pairs={{0,16},{8,24},{16,0},{24,8},{1,17},{9,25},{17,1},{25,9},{2,18},{10... | collective-permute-start | bytes 3145736 | tf_op jit(solution)/shard_map/ppermute | solution.py:46
  1092.7 41.4 %collective-permute-start.54 = (bf16[8,64,768]{2,1,0:T(8,128)(2,1)S(1)}, bf16[8,64,768]{2,1,0:T(8,128)(2,1)S(1)}, u32[]{:S(2)}, u32[]{:S(2)}) collective-permute-start(bf16[8,64,768]{2,1,0:T(8,128)(2,1)S(1)} %all-to-all-done.3), channel_id=1, source_target_pairs={{0,16},{8,24},{16,0},{24,8},{1,17},{9,25},{17,1},{25,9},{2,18},{10... | collective-permute-start | bytes 2359304 | tf_op jit(solution)/shard_map/ppermute | solution.py:46
  1096.8 41.9 %collective-permute-start.56 = (bf16[8,64,768]{2,1,0:T(8,128)(2,1)S(1)}, bf16[8,64,768]{2,1,0:T(8,128)(2,1)S(1)}, u32[]{:S(2)}, u32[]{:S(2)}) collective-permute-start(bf16[8,64,768]{2,1,0:T(8,128)(2,1)S(1)} %all-to-all-done.3), channel_id=1, source_target_pairs={{0,8},{8,0},{16,24},{24,16},{1,9},{9,1},{17,25},{25,17},{2,10},{10... | collective-permute-start | bytes 2359304 | tf_op jit(solution)/shard_map/ppermute | solution.py:46
  1134.0 43.5 %collective-permute-start.68 = (bf16[2048,256]{1,0:T(8,128)(2,1)}, bf16[2048,256]{1,0:T(8,128)(2,1)}, u32[]{:S(2)}, u32[]{:S(2)}) collective-permute-start(bf16[2048,256]{1,0:T(8,128)(2,1)} %collective-permute-done.67), channel_id=1, source_target_pairs={{0,8},{8,0},{16,24},{24,16},{1,9},{9,1},{17,25},{25,17},{2,10},{10... | collective-permute-start | bytes 3145736 | tf_op jit(solution)/shard_map/ppermute | solution.py:46
  (127 other events, 2265.3 us)
Sparse Core Ops, SparseCore 0:
  10.1 140.0 all-gather.2
  176.6 47.2 all-gather.4
  790.0 250.6 reduce-scatter.1

commit v5 on v4

--- a/solution.py
+++ b/solution.py
@@ -465,20 +465,26 @@
     gains = lax.dynamic_update_slice_in_dim(
         jnp.zeros((4, model_width), f32), own_gains, me * shard, 1
     )
-    gains = xor_sum(gains, "fsdp", group)
     if group == chain:
         pair_gains = own_gains[:2]
     else:
+        gains = xor_sum(gains, "fsdp", group)
         pair_gains = lax.dynamic_slice_in_dim(gains[:2], spot * width, width, 1)
-    mixer_gain = gains[2:3]
-    feeder_gain = gains[3:4]
 
     pre = matmul(all_tokens, triple_weight)
     query_pre, key_pre = pre[:, :width], pre[:, width : 2 * width]
     squares = jnp.stack(
         [jnp.sum(query_pre * query_pre, axis=1), jnp.sum(key_pre * key_pre, axis=1)]
     )
-    squares = xor_sum(squares, "fsdp", chain)
+    if group == chain:
+        packed = xor_sum(
+            jnp.concatenate([squares.reshape(-1, model_width), gains]), "fsdp", group
+        )
+        squares, gains = packed[:-4].reshape(2, -1), packed[-4:]
+    else:
+        squares = xor_sum(squares, "fsdp", chain)
+    mixer_gain = gains[2:3]
+    feeder_gain = gains[3:4]
     query_low, key_low, value_low = prep(
         pre, squares, pair_gains.reshape(1, 2 * width), cosine, sine
     )
@@ -552,7 +558,9 @@
             all_hidden, after(gate_grad, up_send), gate_near
         )
         stage["gate"] = gate_kept, swapped(gate_pass, "rep", 2)
-        return (gate_pass,)
+        kept, passed = to_partner(down_kept, after(down_far, gate_pass))
+        stage["down"] = kept, swapped(passed, "fsdp", 4)
+        return (gate_pass, passed)
 
     def back_terms(low, high, *deps):
         return against(after(back_gate[low:high], *deps), wide_gate) + against(
@@ -588,8 +596,10 @@
     output_kept = output_kept[:, :quarter]
     output_far = swapped(output_pass, "rep", 2)
     if group == 8:
-        down_kept, down_pass = to_partner(down_kept, after(down_far, mixed_grad))
-        down_theirs = swapped(down_pass, "fsdp", 4)
+        down_first, down_theirs = stage["down"]
+        gate_kept, gate_far = stage["gate"]
+        gate_kept, gate_pass = to_partner(gate_kept, after(gate_far, mixed_grad))
+        gate_theirs = swapped(gate_pass, "fsdp", 4)
         mixed_grad = after(mixed_grad, output_pass)
     query_turn, key_turn, value_grad = attend_back(
         starts,
@@ -642,12 +652,9 @@
     triple_grad = jnp.concatenate([query_grad, key_grad, value_grad], axis=1)
     if group == 8:
         down_total = (
-            down_kept + after(down_theirs, triple_grad).astype(f32)
+            down_first + after(down_theirs, triple_grad).astype(f32)
         ).astype(bf16)
         down_pieces = shared(down_total)
-        gate_kept, gate_far = stage["gate"]
-        gate_kept, gate_pass = to_partner(gate_kept, after(gate_far, triple_grad))
-        gate_theirs = swapped(gate_pass, "fsdp", 4)
     token_terms = against(triple_grad, triple_weight).astype(bf16)
     token_rows = to_sequence_rows(token_terms)
     gradient_tokens = (hidden_grad + token_rows).astype(bf16)

time: 1210 us -> 1190 us (0.983)
    ppermute x74 -> x71, waiting for transfers between devices: 503 us -> 463 us  [swapped(): return lax.ppermute(block, axis, [(i, i ^ bit) for i in range(size)])]
    all_to_all x1, waiting for transfers between devices: 0.01 us -> 27.6 us  [body(): heads_rows = lax.all_to_all(kept, 'fsdp', 0, 0)]
    ppermute x74 -> x71, starting transfers between devices: 55.2 us -> 53.6 us  [swapped(): return lax.ppermute(block, axis, [(i, i ^ bit) for i in range(size)])]
  transfers between devices with their start and end apart: 81 -> 78, of which waited for: 37 -> 36; matrix products, arithmetic and copies ran while one was open for 25% -> 26% of each run, Pallas kernels for 5% -> 2%
where the time goes in v5:
time: 1190 us; the launch traced here: 1180 us
  waiting for transfers between devices  586 us (49%)
  matrix products  196 us (16%)
  local copies, waits for them, and re-layouts  126 us (11%)
  other arithmetic  87.4 us (7%)
  starting transfers between devices  70.3 us (6%)
  Pallas kernels  57.8 us (5%)
  blocking collectives  45.9 us (4%)
  between operations  16.1 us (1%)
    ppermute x71, waiting for transfers between devices, swapped(): return lax.ppermute(block, axis, [(i, i ^ bit) for i in range(size)])  463 us
    all_gather x1, waiting for transfers between devices, of_sequence(): lax.all_gather(block, 'fsdp', axis=0, tiled=True, axis_index_groups=teams)  75 us
    dot_general x11, matrix products, against(): lax.dot_general(a, b, (((1,), (1,)), ((), ())), preferred_element_type=f32)  71.4 us
    dot_general x9, matrix products, across(): lax.dot_general(a, b, (((0,), (0,)), ((), ())), preferred_element_type=f32)  68.3 us
    dot_general x5, matrix products, matmul(): return jnp.dot(a, b, preferred_element_type=f32)  55.9 us
    ppermute x71, starting transfers between devices, swapped(): return lax.ppermute(block, axis, [(i, i ^ bit) for i in range(size)])  53.6 us
    unnamed x193, local copies, waits for them, and re-layouts  52.9 us
    all_to_all x1, blocking collectives, body(): columns_weight = lax.all_to_all(rows_weight, 'fsdp', 0, 0)  45.9 us
  transfers between devices with their start and end apart: 78, of which 36 were waited for; matrix products, arithmetic and copies ran while one was open for 26% of the time, Pallas kernels for 2%

profile of v5, /device:TPU:0, one launch (start us, length us, event | category | flops | bytes accessed | tf_op | source)
XLA Modules:
  0.0 1184.1 jit_solution(9085990901235404608)
XLA Ops:
  11.1 45.9 %all_to_all.25 = bf16[8,64,768]{2,1,0:T(8,128)(2,1)S(1)} all-to-all(bf16[8,64,768]{2,1,0:T(8,128)(2,1)S(1)} %reshape.133), channel_id=1, replica_groups=mesh['rep'=4,'fsdp'=8] {'fsdp'}, dimensions={0} | all-to-all | bytes 1572864 | tf_op jit(solution)/shard_map/all_to_all | solution.py:458
  58.5 10.5 collective-permute-done
  75.3 75.0 %all-gather.3.cloned.1.call-done = bf16[2048,2048]{1,0:T(8,128)(2,1)} async-done(((bf16[256,2048]{1,0:T(8,128)(2,1)}), bf16[2048,2048]{1,0:T(8,128)(2,1)}) %all-gather.3.cloned.1.call-update) | async-done | bytes 8388624 | tf_op jit(solution)/shard_map/all_gather | solution.py:351
  150.2 10.0 convolution_bitcast_fusion.pre_ref
  191.8 19.8 %attend.1 = (bf16[2048,256]{1,0:T(8,128)(2,1)}, f32[2048,256]{1,0:T(8,128)}, f32[2048,256]{1,0:T(8,128)}) custom-call(s32[2]{0:T(128)} %fusion.57.starts_ref, bf16[2048,256]{1,0:T(8,128)(2,1)} %get-tuple-element.56.q_ref, bf16[2048,256]{1,0:T(8,128)(2,1)} %get-tuple-element.57.k_ref, bf16[2048,256]{1,0:T(8,128)(2,1)} %get-tuple-element.58.v_ref), custom_call_target="tpu_custom_call" | custom-call | flops 2147483648 | bytes 8388608 | tf_op jit(solution)/shard_map/attend/pallas_call | solution.py:199
  211.6 14.6 %all-gather.5.cloned.1.call-done = bf16[2048,512]{1,0:T(8,128)(2,1)} async-done(((bf16[256,512]{1,0:T(8,128)(2,1)}), bf16[2048,512]{1,0:T(8,128)(2,1)}) %all-gather.5.cloned.1.call-update) | async-done | bytes 2097168 | tf_op jit(solution)/shard_map/all_gather | solution.py:492
  233.6 38.4 %collective-permute-done.6 = bf16[2048,512]{1,0:T(8,128)(2,1)} collective-permute-done((bf16[2048,512]{1,0:T(8,128)(2,1)}, bf16[2048,512]{1,0:T(8,128)(2,1)}, u32[]{:S(2)}, u32[]{:S(2)}) %collective-permute-start.6) | collective-permute-done | bytes 2097184 | tf_op jit(solution)/shard_map/ppermute | solution.py:46
  290.7 59.9 %collective-permute-done.13 = bf16[2048,256]{1,0:T(8,128)(2,1)} collective-permute-done((bf16[2048,256]{1,0:T(8,128)(2,1)}, bf16[2048,256]{1,0:T(8,128)(2,1)}, u32[]{:S(2)}, u32[]{:S(2)}) %collective-permute-start.13) | collective-permute-done | bytes 1048608 | tf_op jit(solution)/shard_map/ppermute | solution.py:46
  354.8 18.2 %collective-permute-done.17 = bf16[2048,256]{1,0:T(8,128)(2,1)S(1)} collective-permute-done((bf16[2048,256]{1,0:T(8,128)(2,1)}, bf16[2048,256]{1,0:T(8,128)(2,1)S(1)}, u32[]{:S(2)}, u32[]{:S(2)}) %collective-permute-start.17) | collective-permute-done | bytes 1048608 | tf_op jit(solution)/shard_map/ppermute | solution.py:46
  382.1 13.4 %collective-permute-done.10 = bf16[256,2048]{1,0:T(8,128)(2,1)S(1)} collective-permute-done((bf16[256,2048]{1,0:T(8,128)(2,1)S(1)}, bf16[256,2048]{1,0:T(8,128)(2,1)S(1)}, u32[]{:S(2)}, u32[]{:S(2)}) %collective-permute-start.10) | collective-permute-done | bytes 1048608 | tf_op jit(solution)/shard_map/ppermute | solution.py:46
  405.9 25.8 %collective-permute-done.11 = bf16[128,2048]{1,0:T(8,128)(2,1)S(1)} collective-permute-done((bf16[128,2048]{1,0:T(8,128)(2,1)S(1)}, bf16[128,2048]{1,0:T(8,128)(2,1)S(1)}, u32[]{:S(2)}, u32[]{:S(2)}) %collective-permute-start.11) | collective-permute-done | bytes 524320 | tf_op jit(solution)/shard_map/ppermute | solution.py:46
  432.9 13.4 %convolution_convert_fusion.3 = bf16[1024,2048]{1,0:T(8,128)(2,1)} fusion(bf16[1024,2048]{1,0:T(8,128)(2,1)S(1)} %constant_dynamic-update-slice_fusion.4, bf16[2048,2048]{1,0:T(8,128)(2,1)} %constant_dynamic-update-slice_fusion.9), kind=kOutput, calls=%fused_computation.35 | convolution fusion | flops 8592031744 | bytes 16777216 | tf_op jit(solution)/shard_map/dot_general | solution.py:23
  448.8 14.8 %fusion = (bf16[1024,2048]{1,0:T(8,128)(2,1)S(1)}, bf16[1024,2048]{1,0:T(8,128)(2,1)}) fusion(bf16[1024,2048]{1,0:T(8,128)(2,1)} %convolution_convert_fusion.3, bf16[1024,2048]{1,0:T(8,128)(2,1)S(1)} %constant_dynamic-update-slice_fusion.4, bf16[2048,2048]{1,0:T(8,128)(2,1)} %constant_dynamic-update-slice_fusion.14), kind=kOutput, calls=%fused_computation.6 | convolution fusion | flops 8608808960 | bytes 25165824 | tf_op jit(solution)/shard_map/dot_general | solution.py:23
  493.5 22.0 %collective-permute-done.27 = bf16[256,2048]{1,0:T(8,128)(2,1)S(1)} collective-permute-done((bf16[256,2048]{1,0:T(8,128)(2,1)S(1)}, bf16[256,2048]{1,0:T(8,128)(2,1)S(1)}, u32[]{:S(2)}, u32[]{:S(2)}) %collective-permute-start.27) | collective-permute-done | bytes 1048608 | tf_op jit(solution)/shard_map/ppermute | solution.py:46
  526.8 20.4 %collective-permute-done.29 = bf16[256,2048]{1,0:T(8,128)(2,1)S(1)} collective-permute-done((bf16[256,2048]{1,0:T(8,128)(2,1)S(1)}, bf16[256,2048]{1,0:T(8,128)(2,1)S(1)}, u32[]{:S(2)}, u32[]{:S(2)}) %collective-permute-start.29) | collective-permute-done | bytes 1048608 | tf_op jit(solution)/shard_map/ppermute | solution.py:46
  550.1 9.5 collective-permute-done.31
  566.0 15.3 %fusion.3 = (bf16[1024,2048]{1,0:T(8,128)(2,1)S(1)}, bf16[1024,2048]{1,0:T(8,128)(2,1)S(1)}) fusion(bf16[1024,2048]{1,0:T(8,128)(2,1)} %get-tuple-element.195, bf16[1024,2048]{1,0:T(8,128)(2,1)} %convolution_convert_fusion.3, bf16[1024,2048]{1,0:T(8,128)(2,1)S(1)} %constant_dynamic-update-slice_fusion.24, bf16[2048,2048]{1,0:T(8,128)(2,1)} %copy-done.49), kind=kOutput, calls=%fused_computation.9 | convolution fusion | flops 8621391872 | bytes 29360128 | tf_op jit(solution)/shard_map/dot_general | solution.py:23
  581.4 10.4 convert_add_fusion.3
  610.2 9.5 fusion.83
  619.7 10.3 fusion.81
  657.0 9.6 convolution_convert_fusion.4
  680.9 20.4 %collective-permute-done.38 = bf16[2048,512]{1,0:T(8,128)(2,1)S(1)} collective-permute-done((bf16[2048,512]{1,0:T(8,128)(2,1)S(1)}, bf16[2048,512]{1,0:T(8,128)(2,1)S(1)}, u32[]{:S(2)}, u32[]{:S(2)}) %collective-permute-start.38) | collective-permute-done | bytes 2097184 | tf_op jit(solution)/shard_map/ppermute | solution.py:46
  746.8 31.6 %attend_back.1 = (f32[2048,256]{1,0:T(8,128)}, f32[2048,256]{1,0:T(8,128)}, bf16[2048,256]{1,0:T(8,128)(2,1)}) custom-call(s32[2]{0:T(128)} %fusion.57.starts_ref, bf16[2048,256]{1,0:T(8,128)(2,1)} %get-tuple-element.56.q_ref, bf16[2048,256]{1,0:T(8,128)(2,1)} %bitcast.18.grad_ref, f32[2048,256]{1,0:T(8,128)} %get-tuple-element.84.mixed_ref, ...), custom_call_target="tpu_custom_call" | custom-call | flops 5368709120 | bytes 14680064 | tf_op jit(solution)/shard_map/attend_back/pallas_call | solution.py:295
  814.4 26.6 %collective-permute-done.50 = bf16[2048,512]{1,0:T(8,128)(2,1)} collective-permute-done((bf16[2048,512]{1,0:T(8,128)(2,1)}, bf16[2048,512]{1,0:T(8,128)(2,1)}, u32[]{:S(2)}, u32[]{:S(2)}) %collective-permute-start.50) | collective-permute-done | bytes 2097184 | tf_op jit(solution)/shard_map/ppermute | solution.py:46
  849.8 11.1 convolution_bitcast_fusion.1
  869.8 58.4 %collective-permute-done.67 = bf16[2048,256]{1,0:T(8,128)(2,1)} collective-permute-done((bf16[2048,256]{1,0:T(8,128)(2,1)}, bf16[2048,256]{1,0:T(8,128)(2,1)}, u32[]{:S(2)}, u32[]{:S(2)}) %collective-permute-start.67) | collective-permute-done | bytes 1048608 | tf_op jit(solution)/shard_map/ppermute | solution.py:46
  946.6 17.5 %collective-permute-done.69 = bf16[2048,256]{1,0:T(8,128)(2,1)} collective-permute-done((bf16[2048,256]{1,0:T(8,128)(2,1)S(1)}, bf16[2048,256]{1,0:T(8,128)(2,1)}, u32[]{:S(2)}, u32[]{:S(2)}) %collective-permute-start.69) | collective-permute-done | bytes 1048608 | tf_op jit(solution)/shard_map/ppermute | solution.py:46
  967.9 12.2 %collective-permute-done.47 = bf16[8,64,768]{2,1,0:T(8,128)(2,1)S(1)} collective-permute-done((bf16[8,64,768]{2,1,0:T(8,128)(2,1)S(1)}, bf16[8,64,768]{2,1,0:T(8,128)(2,1)S(1)}, u32[]{:S(2)}, u32[]{:S(2)}) %collective-permute-start.47) | collective-permute-done | bytes 786464 | tf_op jit(solution)/shard_map/ppermute | solution.py:46
  984.9 13.6 %collective-permute-done.51 = bf16[2048,256]{1,0:T(8,128)(2,1)} collective-permute-done((bf16[2048,256]{1,0:T(8,128)(2,1)}, bf16[2048,256]{1,0:T(8,128)(2,1)}, u32[]{:S(2)}, u32[]{:S(2)}) %collective-permute-start.51) | collective-permute-done | bytes 1048608 | tf_op jit(solution)/shard_map/ppermute | solution.py:46
  1018.4 18.5 %collective-permute-done.62 = bf16[2048,256]{1,0:T(8,128)(2,1)} collective-permute-done((bf16[2048,256]{1,0:T(8,128)(2,1)S(1)}, bf16[2048,256]{1,0:T(8,128)(2,1)}, u32[]{:S(2)}, u32[]{:S(2)}) %collective-permute-start.62) | collective-permute-done | bytes 1048608 | tf_op jit(solution)/shard_map/ppermute | solution.py:46
  1038.4 27.6 %all-to-all-done.3 = bf16[8,64,768]{2,1,0:T(8,128)(2,1)S(1)} async-done(((bf16[8,64,768]{2,1,0:T(8,128)(2,1)}), bf16[8,64,768]{2,1,0:T(8,128)(2,1)S(1)}, u32[]{:S(2)}, u32[]{:S(2)}) %all-to-all-start.3) | async-done | bytes 786464 | tf_op jit(solution)/shard_map/all_to_all | solution.py:683
  1085.4 35.0 %collective-permute-done.52 = bf16[8,64,768]{2,1,0:T(8,128)(2,1)S(1)} collective-permute-done((bf16[8,64,768]{2,1,0:T(8,128)(2,1)S(1)}, bf16[8,64,768]{2,1,0:T(8,128)(2,1)S(1)}, u32[]{:S(2)}, u32[]{:S(2)}) %collective-permute-start.52) | collective-permute-done | bytes 786464 | tf_op jit(solution)/shard_map/ppermute | solution.py:46
  (488 shorter events, 429.0 us)
Async XLA Ops:
  7.2 143.0 %all-gather.3.cloned.1.call-start = ((), (), s32[]{:S(2)}) async-start(), calls=%async_computation.6 | async-start | bytes 9437184 | tf_op jit(solution)/shard_map/all_gather | solution.py:351
  7.9 218.2 %all-gather.5.cloned.1.call-start = ((), (), s32[]{:S(2)}) async-start(), calls=%async_computation.7 | async-start | bytes 2359296 | tf_op jit(solution)/shard_map/all_gather | solution.py:492
  226.2 45.8 %collective-permute-start.6 = (bf16[2048,512]{1,0:T(8,128)(2,1)}, bf16[2048,512]{1,0:T(8,128)(2,1)}, u32[]{:S(2)}, u32[]{:S(2)}) collective-permute-start(bf16[2048,512]{1,0:T(8,128)(2,1)} %all-gather.5.cloned.1.call-done), channel_id=1, source_target_pairs={{0,16},{8,24},{16,0},{24,8},{1,17},{9,25},{17,1},{25,9},{2,18},{10... | collective-permute-start | bytes 6291464 | tf_op jit(solution)/shard_map/ppermute | solution.py:46
  229.9 51.5 %all-to-all-start.1 = ((bf16[8,256,256]{1,2,0:T(8,128)(2,1)}), bf16[8,256,256]{1,2,0:T(8,128)(2,1)S(1)}, u32[]{:S(2)}, u32[]{:S(2)}) async-start(bf16[8,256,256]{1,2,0:T(8,128)(2,1)} %copy.55), calls=%async_computation.1 | async-start | bytes 2097152 | tf_op jit(solution)/shard_map/all_to_all | solution.py:368
  233.5 50.2 %collective-permute-start.7 = (bf16[2048,512]{1,0:T(8,128)(2,1)S(1)}, bf16[2048,512]{1,0:T(8,128)(2,1)}, u32[]{:S(2)}, u32[]{:S(2)}) collective-permute-start(bf16[2048,512]{1,0:T(8,128)(2,1)S(1)} %copy-done.39), channel_id=1, source_target_pairs={{0,8},{8,0},{16,24},{24,16},{1,9},{9,1},{17,25},{25,17},{2,10},{10... | collective-permute-start | bytes 6291464 | tf_op jit(solution)/shard_map/ppermute | solution.py:46
  278.3 72.3 %collective-permute-start.13 = (bf16[2048,256]{1,0:T(8,128)(2,1)}, bf16[2048,256]{1,0:T(8,128)(2,1)}, u32[]{:S(2)}, u32[]{:S(2)}) collective-permute-start(bf16[2048,256]{1,0:T(8,128)(2,1)} %get-tuple-element.62), channel_id=1, source_target_pairs={{0,4},{1,5},{2,6},{3,7},{4,0},{5,1},{6,2},{7,3},{8,12},{9,13},{10,... | collective-permute-start | bytes 3145736 | tf_op jit(solution)/shard_map/ppermute | solution.py:46
  281.4 91.5 %collective-permute-start.17 = (bf16[2048,256]{1,0:T(8,128)(2,1)}, bf16[2048,256]{1,0:T(8,128)(2,1)S(1)}, u32[]{:S(2)}, u32[]{:S(2)}) collective-permute-start(bf16[2048,256]{1,0:T(8,128)(2,1)} %get-tuple-element.64), channel_id=1, source_target_pairs={{0,4},{1,5},{2,6},{3,7},{4,0},{5,1},{6,2},{7,3},{8,12},{9,13},{10,... | collective-permute-start | bytes 3145736 | tf_op jit(solution)/shard_map/ppermute | solution.py:46
  352.1 48.7 %collective-permute-start.15 = (bf16[2048,256]{1,0:T(8,128)(2,1)}, bf16[2048,256]{1,0:T(8,128)(2,1)S(1)}, u32[]{:S(2)}, u32[]{:S(2)}) collective-permute-start(bf16[2048,256]{1,0:T(8,128)(2,1)} %collective-permute-done.13), channel_id=1, source_target_pairs={{0,8},{8,0},{16,24},{24,16},{1,9},{9,1},{17,25},{25,17},{2,10},{10... | collective-permute-start | bytes 3145736 | tf_op jit(solution)/shard_map/ppermute | solution.py:46
  354.5 41.0 %collective-permute-start.10 = (bf16[256,2048]{1,0:T(8,128)(2,1)S(1)}, bf16[256,2048]{1,0:T(8,128)(2,1)S(1)}, u32[]{:S(2)}, u32[]{:S(2)}) collective-permute-start(bf16[256,2048]{1,0:T(8,128)(2,1)S(1)} %get-tuple-element.127), channel_id=1, source_target_pairs={{0,2},{1,3},{2,0},{3,1},{4,6},{5,7},{6,4},{7,5},{8,10},{9,11},{10,... | collective-permute-start | bytes 3145736 | tf_op jit(solution)/shard_map/ppermute | solution.py:46
  382.1 64.2 %collective-permute-start.21 = (bf16[2048,256]{1,0:T(8,128)(2,1)S(1)}, bf16[2048,256]{1,0:T(8,128)(2,1)S(1)}, u32[]{:S(2)}, u32[]{:S(2)}) collective-permute-start(bf16[2048,256]{1,0:T(8,128)(2,1)S(1)} %copy-done.43), channel_id=1, source_target_pairs={{0,4},{1,5},{2,6},{3,7},{4,0},{5,1},{6,2},{7,3},{8,12},{9,13},{10,... | collective-permute-start | bytes 3145736 | tf_op jit(solution)/shard_map/ppermute | solution.py:46
  405.1 42.6 %collective-permute-start.20 = (bf16[2048,256]{1,0:T(8,128)(2,1)S(1)}, bf16[2048,256]{1,0:T(8,128)(2,1)S(1)}, u32[]{:S(2)}, u32[]{:S(2)}) collective-permute-start(bf16[2048,256]{1,0:T(8,128)(2,1)S(1)} %collective-permute-done.18), channel_id=1, source_target_pairs={{0,8},{8,0},{16,24},{24,16},{1,9},{9,1},{17,25},{25,17},{2,10},{10... | collective-permute-start | bytes 3145736 | tf_op jit(solution)/shard_map/ppermute | solution.py:46
  653.3 48.0 %collective-permute-start.38 = (bf16[2048,512]{1,0:T(8,128)(2,1)S(1)}, bf16[2048,512]{1,0:T(8,128)(2,1)S(1)}, u32[]{:S(2)}, u32[]{:S(2)}) collective-permute-start(bf16[2048,512]{1,0:T(8,128)(2,1)S(1)} %slice.465), channel_id=1, source_target_pairs={{0,16},{8,24},{16,0},{24,8},{1,17},{9,25},{17,1},{25,9},{2,18},{10... | collective-permute-start | bytes 6291464 | tf_op jit(solution)/shard_map/ppermute | solution.py:46
  655.1 48.2 %collective-permute-start.36 = (bf16[256,2048]{1,0:T(8,128)(2,1)}, bf16[256,2048]{1,0:T(8,128)(2,1)S(1)}, u32[]{:S(2)}, u32[]{:S(2)}) collective-permute-start(bf16[256,2048]{1,0:T(8,128)(2,1)} %pad_maximum_fusion.7), channel_id=1, source_target_pairs={{0,1},{1,0},{2,3},{3,2},{4,5},{5,4},{6,7},{7,6},{8,9},{9,8},{10,11... | collective-permute-start | bytes 3145736 | tf_op jit(solution)/shard_map/ppermute | solution.py:46
  656.1 48.3 %collective-permute-start.39 = (bf16[256,2048]{1,0:T(8,128)(2,1)}, bf16[256,2048]{1,0:T(8,128)(2,1)S(1)}, u32[]{:S(2)}, u32[]{:S(2)}) collective-permute-start(bf16[256,2048]{1,0:T(8,128)(2,1)} %pad_maximum_fusion.8), channel_id=1, source_target_pairs={{0,2},{1,3},{2,0},{3,1},{4,6},{5,7},{6,4},{7,5},{8,10},{9,11},{10,... | collective-permute-start | bytes 3145736 | tf_op jit(solution)/shard_map/ppermute | solution.py:46
  666.6 53.8 %collective-permute-start.40 = (bf16[2048,1024]{1,0:T(8,128)(2,1)}, bf16[2048,1024]{1,0:T(8,128)(2,1)}, u32[]{:S(2)}, u32[]{:S(2)}) collective-permute-start(bf16[2048,1024]{1,0:T(8,128)(2,1)} %convolution_convert_fusion.4), channel_id=1, source_target_pairs={{0,8},{8,0},{16,24},{24,16},{1,9},{9,1},{17,25},{25,17},{2,10},{10... | collective-permute-start | bytes 12582920 | tf_op jit(solution)/shard_map/ppermute | solution.py:46
  720.3 454.3 %reduce-scatter.2.cloned.1.call-start = ((), (), s32[]{:S(2)}) async-start(), calls=%async_computation.8 | async-start | bytes 9437184 | tf_op jit(solution)/shard_map/reduce_scatter | solution.py:354
  792.2 48.8 %collective-permute-start.50 = (bf16[2048,512]{1,0:T(8,128)(2,1)}, bf16[2048,512]{1,0:T(8,128)(2,1)}, u32[]{:S(2)}, u32[]{:S(2)}) collective-permute-start(bf16[2048,512]{1,0:T(8,128)(2,1)} %slice.464), channel_id=1, source_target_pairs={{0,16},{8,24},{16,0},{24,8},{1,17},{9,25},{17,1},{25,9},{2,18},{10... | collective-permute-start | bytes 6291464 | tf_op jit(solution)/shard_map/ppermute | solution.py:46
  812.3 115.9 %collective-permute-start.67 = (bf16[2048,256]{1,0:T(8,128)(2,1)}, bf16[2048,256]{1,0:T(8,128)(2,1)}, u32[]{:S(2)}, u32[]{:S(2)}) collective-permute-start(bf16[2048,256]{1,0:T(8,128)(2,1)} %slice.468), channel_id=1, source_target_pairs={{0,4},{1,5},{2,6},{3,7},{4,0},{5,1},{6,2},{7,3},{8,12},{9,13},{10,... | collective-permute-start | bytes 3145736 | tf_op jit(solution)/shard_map/ppermute | solution.py:46
  812.9 125.7 %collective-permute-start.49 = (bf16[2048,512]{1,0:T(8,128)(2,1)}, bf16[2048,512]{1,0:T(8,128)(2,1)}, u32[]{:S(2)}, u32[]{:S(2)}) collective-permute-start(bf16[2048,512]{1,0:T(8,128)(2,1)} %slice.463), channel_id=1, source_target_pairs={{0,16},{8,24},{16,0},{24,8},{1,17},{9,25},{17,1},{25,9},{2,18},{10... | collective-permute-start | bytes 6291464 | tf_op jit(solution)/shard_map/ppermute | solution.py:46
  845.8 152.6 %collective-permute-start.51 = (bf16[2048,256]{1,0:T(8,128)(2,1)}, bf16[2048,256]{1,0:T(8,128)(2,1)}, u32[]{:S(2)}, u32[]{:S(2)}) collective-permute-start(bf16[2048,256]{1,0:T(8,128)(2,1)} %slice.466), channel_id=1, source_target_pairs={{0,4},{1,5},{2,6},{3,7},{4,0},{5,1},{6,2},{7,3},{8,12},{9,13},{10,... | collective-permute-start | bytes 3145736 | tf_op jit(solution)/shard_map/ppermute | solution.py:46
  848.0 116.0 %collective-permute-start.48 = (bf16[2048,512]{1,0:T(8,128)(2,1)}, bf16[2048,512]{1,0:T(8,128)(2,1)}, u32[]{:S(2)}, u32[]{:S(2)}) collective-permute-start(bf16[2048,512]{1,0:T(8,128)(2,1)} %slice.462), channel_id=1, source_target_pairs={{0,16},{8,24},{16,0},{24,8},{1,17},{9,25},{17,1},{25,9},{2,18},{10... | collective-permute-start | bytes 6291464 | tf_op jit(solution)/shard_map/ppermute | solution.py:46
  867.5 60.6 %collective-permute-start.55 = (f32[4,2048]{1,0:T(4,128)S(1)}, f32[4,2048]{1,0:T(4,128)S(1)}, u32[]{:S(2)}, u32[]{:S(2)}) collective-permute-start(f32[4,2048]{1,0:T(4,128)S(1)} %slice.357), channel_id=1, source_target_pairs={{0,8},{8,0},{16,24},{24,16},{1,9},{9,1},{17,25},{25,17},{2,10},{10... | collective-permute-start | bytes 98312 | tf_op jit(solution)/shard_map/ppermute | solution.py:46
  938.7 41.5 %collective-permute-start.45 = (bf16[8,64,768]{2,1,0:T(8,128)(2,1)S(1)}, bf16[8,64,768]{2,1,0:T(8,128)(2,1)S(1)}, u32[]{:S(2)}, u32[]{:S(2)}) collective-permute-start(bf16[8,64,768]{2,1,0:T(8,128)(2,1)S(1)} %get-tuple-element.133), channel_id=1, source_target_pairs={{0,8},{8,0},{16,24},{24,16},{1,9},{9,1},{17,25},{25,17},{2,10},{10... | collective-permute-start | bytes 2359304 | tf_op jit(solution)/shard_map/ppermute | solution.py:46
  964.1 106.5 %collective-permute-start.57 = (bf16[2048,256]{1,0:T(8,128)(2,1)}, bf16[2048,256]{1,0:T(8,128)(2,1)}, u32[]{:S(2)}, u32[]{:S(2)}) collective-permute-start(bf16[2048,256]{1,0:T(8,128)(2,1)} %slice.467), channel_id=1, source_target_pairs={{0,4},{1,5},{2,6},{3,7},{4,0},{5,1},{6,2},{7,3},{8,12},{9,13},{10,... | collective-permute-start | bytes 3145736 | tf_op jit(solution)/shard_map/ppermute | solution.py:46
  964.1 51.6 %collective-permute-start.70 = (bf16[2048,256]{1,0:T(8,128)(2,1)}, bf16[2048,256]{1,0:T(8,128)(2,1)}, u32[]{:S(2)}, u32[]{:S(2)}) collective-permute-start(bf16[2048,256]{1,0:T(8,128)(2,1)} %collective-permute-done.69), channel_id=1, source_target_pairs={{0,8},{8,0},{16,24},{24,16},{1,9},{9,1},{17,25},{25,17},{2,10},{10... | collective-permute-start | bytes 3145736 | tf_op jit(solution)/shard_map/ppermute | solution.py:46
  981.3 84.6 %all-to-all-start.3 = ((bf16[8,64,768]{2,1,0:T(8,128)(2,1)}), bf16[8,64,768]{2,1,0:T(8,128)(2,1)S(1)}, u32[]{:S(2)}, u32[]{:S(2)}) async-start(bf16[8,64,768]{2,1,0:T(8,128)(2,1)} %fusion.31), calls=%async_computation.4 | async-start | bytes 1572864 | tf_op jit(solution)/shard_map/all_to_all | solution.py:683
  1036.9 45.8 %collective-permute-start.63 = (bf16[2048,256]{1,0:T(8,128)(2,1)}, bf16[2048,256]{1,0:T(8,128)(2,1)}, u32[]{:S(2)}, u32[]{:S(2)}) collective-permute-start(bf16[2048,256]{1,0:T(8,128)(2,1)} %collective-permute-done.62), channel_id=1, source_target_pairs={{0,8},{8,0},{16,24},{24,16},{1,9},{9,1},{17,25},{25,17},{2,10},{10... | collective-permute-start | bytes 3145736 | tf_op jit(solution)/shard_map/ppermute | solution.py:46
  1065.9 95.3 %all-to-all-start.4 = ((bf16[8,256,512]{2,1,0:T(8,128)(2,1)}), bf16[8,256,512]{2,1,0:T(8,128)(2,1)}, u32[]{:S(2)}, u32[]{:S(2)}) async-start(bf16[8,256,512]{2,1,0:T(8,128)(2,1)} %bitcast.149), calls=%async_computation.5 | async-start | bytes 4194304 | tf_op jit(solution)/shard_map/all_to_all | solution.py:677
  1077.9 42.9 %collective-permute-start.64 = (bf16[2048,256]{1,0:T(8,128)(2,1)S(1)}, bf16[2048,256]{1,0:T(8,128)(2,1)S(1)}, u32[]{:S(2)}, u32[]{:S(2)}) collective-permute-start(bf16[2048,256]{1,0:T(8,128)(2,1)S(1)} %get-tuple-element.114), channel_id=1, source_target_pairs={{0,8},{8,0},{16,24},{24,16},{1,9},{9,1},{17,25},{25,17},{2,10},{10... | collective-permute-start | bytes 3145736 | tf_op jit(solution)/shard_map/ppermute | solution.py:46
  1078.0 42.4 %collective-permute-start.65 = (bf16[2048,256]{1,0:T(8,128)(2,1)S(1)}, bf16[2048,256]{1,0:T(8,128)(2,1)}, u32[]{:S(2)}, u32[]{:S(2)}) collective-permute-start(bf16[2048,256]{1,0:T(8,128)(2,1)S(1)} %get-tuple-element.114), channel_id=1, source_target_pairs={{0,16},{8,24},{16,0},{24,8},{1,17},{9,25},{17,1},{25,9},{2,18},{10... | collective-permute-start | bytes 3145736 | tf_op jit(solution)/shard_map/ppermute | solution.py:46
  1082.7 42.4 %collective-permute-start.54 = (bf16[8,64,768]{2,1,0:T(8,128)(2,1)S(1)}, bf16[8,64,768]{2,1,0:T(8,128)(2,1)S(1)}, u32[]{:S(2)}, u32[]{:S(2)}) collective-permute-start(bf16[8,64,768]{2,1,0:T(8,128)(2,1)S(1)} %all-to-all-done.3), channel_id=1, source_target_pairs={{0,8},{8,0},{16,24},{24,16},{1,9},{9,1},{17,25},{25,17},{2,10},{10... | collective-permute-start | bytes 2359304 | tf_op jit(solution)/shard_map/ppermute | solution.py:46
  1120.4 44.5 %collective-permute-start.66 = (bf16[2048,256]{1,0:T(8,128)(2,1)}, bf16[2048,256]{1,0:T(8,128)(2,1)}, u32[]{:S(2)}, u32[]{:S(2)}) collective-permute-start(bf16[2048,256]{1,0:T(8,128)(2,1)} %collective-permute-done.65), channel_id=1, source_target_pairs={{0,8},{8,0},{16,24},{24,16},{1,9},{9,1},{17,25},{25,17},{2,10},{10... | collective-permute-start | bytes 3145736 | tf_op jit(solution)/shard_map/ppermute | solution.py:46
  (124 other events, 2449.6 us)
Sparse Core Ops, SparseCore 0:
  10.1 140.0 all-gather.2
  178.4 47.6 all-gather.4
  812.4 240.1 reduce-scatter.1
